TPU v7x, 512 devices: a whole 4x4x16 slice. The times are simulated.
512 devices in a mesh: section: 2 (over y_lo), hid: 16 (over z), wid: 16 (over x, y_hi, core).
Axes of the slice: x: 4, y: 4 (y_hi: 2, y_lo: 2; y = y_hi * 2 + y_lo), z: 16, core: 2. Of those that a mesh axis runs over, the one named last changes fastest.
Arguments:
- weights: bfloat16 [2, 6144, 24576], P('section', 'hid', 'wid'), may hold values from -0.078125 to 0.078125
- preact: bfloat16 [1024, 24576], P(('section', 'hid'), 'wid'), may hold values from -6 to 6
- inputs: bfloat16 [1024, 6144], P(('section', 'wid'), 'hid'), may hold values from -6 to 6
- grad_out: bfloat16 [1024, 6144], P(('section', 'wid'), 'hid'), may hold values from -6 to 6
- row_state: float32 [2, 6144], P('section', 'hid'), may hold values from 32 to 256
- col_state: float32 [2, 24576], P('section', 'wid'), may hold values from 32 to 256
Outputs:
- input_grad: float32 [1024, 6144], P(('section', 'wid'), 'hid')
- update: float32 [2, 6144, 24576], P('section', 'hid', 'wid')
All inputs are finite; a program needn't handle non-finite values.
Results may differ from a plain program's by a relative error of at most 0.0029.
Values may be sent and summed in bfloat16 or wider, within the bound.
No kernel may reach another device: no remote copies, remote signals or barrier semaphores. Data moves between devices by JAX's collectives and lax.ppermute only.
A program may use at most 64 MiB of HBM per device.

v0:
```python
import jax
import jax.numpy as jnp
from jax import lax
from jax.sharding import PartitionSpec as P

D = 6144
FF = 24576


decay_rate = 0.9
root_half = 0.7071067811865476
inv_root_tau = 0.3989422804014327


def from_behind(block, axis, distance):
    devices = range(lax.axis_size(axis))
    route = [((i - distance) % len(devices), i) for i in devices]
    return lax.ppermute(block, axis, route)


def normal_cdf(pre):
    return 0.5 * (1.0 + lax.erf(pre * root_half))


def gelu_value(pre):
    return pre * normal_cdf(pre)


def gelu_slope(pre):
    return normal_cdf(pre) + pre * jnp.exp(-0.5 * pre * pre) * inv_root_tau


def contract(left, right):
    return lax.dot_general(
        left, right, (((0,), (0,)), ((), ())), preferred_element_type=jnp.float32
    )


def shards(weights, preact, inputs, grad_out, row_state, col_state):
    own_tile = weights[0]
    first_section = lax.axis_index("section") == 0
    other_tile = from_behind(own_tile, "section", 1)
    up_tile = jnp.where(first_section, own_tile, other_tile)
    down_tile = jnp.where(first_section, other_tile, own_tile)
    grad_half, input_half = (
        lax.all_gather(grad_out, "wid", axis=0, tiled=True),
        lax.all_gather(inputs, "wid", axis=0, tiled=True),
    )
    pre_half = lax.all_gather(preact, "hid", axis=0, tiled=True)
    pre_float = pre_half.astype(jnp.float32)
    activation = gelu_value(pre_float).astype(jnp.bfloat16)
    grad_rows = grad_half
    hidden_share = lax.psum_scatter(
        jnp.dot(grad_rows, down_tile, preferred_element_type=jnp.float32),
        "hid",
        scatter_dimension=0,
        tiled=True,
    )
    pre_share = (hidden_share * gelu_slope(preact.astype(jnp.float32))).astype(jnp.bfloat16)
    pre_grad = lax.all_gather(pre_share, "hid", axis=0, tiled=True)
    grad_rows = pre_grad
    input_sum = lax.psum_scatter(
        lax.dot_general(
            grad_rows, up_tile, (((1,), (1,)), ((), ())), preferred_element_type=jnp.float32
        ),
        "wid",
        scatter_dimension=0,
        tiled=True,
    )
    input_grad = input_sum + grad_out.astype(jnp.float32)
    own_left = jnp.where(first_section, input_half, grad_half)
    own_right = jnp.where(first_section, pre_grad, activation)
    give_left = jnp.where(first_section, grad_half, input_half)
    give_right = jnp.where(first_section, activation, pre_grad)
    gradient = contract(own_left, own_right)
    give_part = contract(give_left, give_right)
    gradient = gradient + from_behind(give_part, "section", 1)
    squares = gradient * gradient
    row_local = jnp.sum(squares, axis=1)
    col_local = jnp.sum(squares, axis=0)
    row_prev = row_state[0]
    col_prev = col_state[0]
    row_total = lax.psum(row_local, "wid")
    row_moment = decay_rate * row_prev + (1.0 - decay_rate) / FF * row_total
    col_total, row_sum = lax.psum((col_local, jnp.sum(row_moment)), "hid")
    col_moment = decay_rate * col_prev + (1.0 - decay_rate) / D * col_total
    row_mean = row_sum / D
    update = gradient * lax.rsqrt(row_moment[:, None] * col_moment[None, :] / row_mean)
    return (input_grad, update[None])


def solution(mesh):
    placed = (
        P("section", "hid", "wid"),
        P(("section", "hid"), "wid"),
        P(("section", "wid"), "hid"),
        P(("section", "wid"), "hid"),
        P("section", "hid"),
        P("section", "wid"),
    )
    return jax.shard_map(
        shards,
        mesh=mesh,
        in_specs=placed,
        out_specs=(P(("section", "wid"), "hid"), P("section", "hid", "wid")),
        check_vma=False,
    )
```

profile of v0, /device:TPU:1, one launch (start us, length us, event | category | flops | bytes accessed | tf_op | source)
XLA Modules:
  0.0 455.3 jit_solution(17599260504651210402)
XLA Ops:
  7.2 4.0 collective-permute-start
  11.2 45.3 %all_gather.12 = bf16[512,384]{1,0:T(8,128)(2,1)S(1)} all-gather(bf16[32,384]{1,0:T(8,128)(2,1)} %param.9), channel_id=1, replica_groups=mesh['section'=2,'hid'=16,'wid'=16] {'wid'}, dimensions={0}, use_global_device_ids=true | all-gather | bytes 417792 | tf_op jit(solution)/shard_map/all_gather | solution.py:46
  56.6 2.7 convolution_bitcast_fusion
  59.3 2.4 copy.13
  61.7 0.0 all-gather.5.cloned.1.call-start
  61.7 0.7 all-gather.5.cloned.1.call-update
  62.5 67.7 %reduce-scatter.7.cloned.1.call-done = f32[32,1536]{1,0:T(8,128)} async-done(((f32[512,1536]{1,0:T(8,128)}), f32[32,1536]{1,0:T(8,128)}) %reduce-scatter.7.cloned.1.call-update) | async-done | bytes 196624 | tf_op jit(solution)/shard_map/reduce_scatter | solution.py:53
  130.2 1.7 fusion.25
  131.9 0.0 reduce-scatter.5.cloned.1.call-start
  131.9 36.1 %all_gather.14 = bf16[512,384]{1,0:T(8,128)(2,1)} all-gather(bf16[32,384]{1,0:T(8,128)(2,1)S(1)} %copy-done.3), channel_id=1, replica_groups=mesh['section'=2,'hid'=16,'wid'=16] {'wid'}, dimensions={0}, use_global_device_ids=true | all-gather | bytes 417792 | tf_op jit(solution)/shard_map/all_gather | solution.py:47
  168.1 33.0 %all-gather.5.cloned.1.call-done = bf16[512,1536]{1,0:T(8,128)(2,1)} async-done(((bf16[32,1536]{1,0:T(8,128)(2,1)}), bf16[512,1536]{1,0:T(8,128)(2,1)}) %all-gather.5.cloned.1.call-update) | async-done | bytes 1572880 | tf_op jit(solution)/shard_map/all_gather | solution.py:49
  201.1 1.9 fusion.3
  203.0 69.8 %all-gather.3.cloned.1.call-done = bf16[512,1536]{1,0:T(8,128)(2,1)} async-done(((bf16[32,1536]{1,0:T(8,128)(2,1)}), bf16[512,1536]{1,0:T(8,128)(2,1)}) %all-gather.3.cloned.1.call-update) | async-done | bytes 1572880 | tf_op jit(solution)/shard_map/all_gather | solution.py:60
  272.7 2.2 fusion.4
  275.0 4.9 %collective-permute-start.1 = (f32[384,1536]{1,0:T(8,128)}, f32[384,1536]{1,0:T(8,128)}, u32[]{:S(2)}, u32[]{:S(2)}) collective-permute-start(f32[384,1536]{1,0:T(8,128)} %fusion.4), channel_id=1, source_target_pairs={{256,0},{0,256},{257,1},{1,257},{258,2},{2,258},{259,3},{3,259},{2... | collective-permute-start | bytes 7077896 | tf_op jit(solution)/shard_map/ppermute | solution.py:18
  279.9 1.9 fusion.9
  281.8 0.6 multiply_reduce_fusion.3
  282.5 93.6 %reduce-scatter.5.cloned.1.call-done = f32[32,384]{1,0:T(8,128)} async-done(((f32[512,384]{1,0:T(8,128)}), f32[32,384]{1,0:T(8,128)}) %reduce-scatter.5.cloned.1.call-update) | async-done | bytes 49168 | tf_op jit(solution)/shard_map/reduce_scatter | solution.py:62
  376.0 1.4 convert_add_fusion
  377.4 4.7 %multiply_reduce_fusion = (f32[1536]{0:T(1024)S(1)}, f32[384]{0:T(512)}, f32[384,1536]{1,0:T(8,128)}) fusion(f32[384,1536]{1,0:T(8,128)} %collective-permute-done.1, bf16[512,1536]{1,0:T(8,128)(2,1)S(1)} %copy-done, bf16[512,1536]{1,0:T(8,128)(2,1)S(1)} %fusion.3, pred[]{:T(512)S(6)} %eq.3, bf16[512,384]{1,0:T(8,128)(2,1)} %all_gather.14, ...), kind=kOutput, calls=%fused_computation.9 | convolution fusion | flops 607320192 | bytes 8658433 | tf_op jit(solution)/shard_map/dot_general | solution.py:34
  382.1 35.2 %psum.21 = f32[384]{0:T(512)S(1)} all-reduce(f32[384]{0:T(512)} %get-tuple-element.3), channel_id=1, replica_groups=mesh['section'=2,'hid'=16,'wid'=16] {'wid'}, use_global_device_ids=true, to_apply=%region_3.4 | all-reduce | flops 384 | bytes 3072 | tf_op jit(solution)/shard_map/psum | solution.py:83
  417.3 1.3 fusion.28
  418.6 26.0 %all-reduce = (f32[]{:T(128)}, f32[1536]{0:T(1024)S(1)}) all-reduce(f32[]{:T(128)} %get-tuple-element.6, f32[1536]{0:T(1024)S(1)} %get-tuple-element.2), channel_id=1, replica_groups=mesh['section'=2,'hid'=16,'wid'=16] {'hid'}, use_global_device_ids=true, to_apply=%region_7.8 | all-reduce | flops 1537 | bytes 12296 | tf_op jit(solution)/shard_map/psum | solution.py:85
  445.3 3.5 multiply_bitcast_fusion
  (21 shorter events, 0.2 us)
Async XLA Ops:
  7.2 123.0 %reduce-scatter.7.cloned.1.call-start = ((), (), s32[]{:S(2)}) async-start(), calls=%async_computation.5 | async-start | bytes 3342336 | tf_op jit(solution)/shard_map/reduce_scatter | solution.py:53
  7.2 49.4 %collective-permute-start = (bf16[384,1536]{1,0:T(8,128)(2,1)}, bf16[384,1536]{1,0:T(8,128)(2,1)}, u32[]{:S(2)}, u32[]{:S(2)}) collective-permute-start(bf16[384,1536]{1,0:T(8,128)(2,1)} %bitcast.16), channel_id=1, source_target_pairs={{256,0},{0,256},{257,1},{1,257},{258,2},{2,258},{259,3},{3,259},{2... | collective-permute-start | bytes 3538952 | tf_op jit(solution)/shard_map/ppermute | solution.py:18
  61.7 68.5 %copy-start.2 = (bf16[32,1536]{1,0:T(8,128)(2,1)S(1)}, bf16[32,1536]{1,0:T(8,128)(2,1)}, u32[]{:S(2)}) copy-start(bf16[32,1536]{1,0:T(8,128)(2,1)} %param.7) | copy-start | bytes 294916
  61.7 70.2 %copy-start.3 = (bf16[32,384]{1,0:T(8,128)(2,1)S(1)}, bf16[32,384]{1,0:T(8,128)(2,1)}, u32[]{:S(2)}) copy-start(bf16[32,384]{1,0:T(8,128)(2,1)} %param.8) | copy-start | bytes 73732
  61.7 139.4 %all-gather.5.cloned.1.call-start = ((), (), s32[]{:S(2)}) async-start(), calls=%async_computation.4 | async-start | bytes 1671168 | tf_op jit(solution)/shard_map/all_gather | solution.py:49
  62.5 210.3 %all-gather.3.cloned.1.call-start = ((), (), s32[]{:S(2)}) async-start(), calls=%async_computation.2 | async-start | bytes 1671168 | tf_op jit(solution)/shard_map/all_gather | solution.py:60
  131.9 244.2 %reduce-scatter.5.cloned.1.call-start = ((), (), s32[]{:S(2)}) async-start(), calls=%async_computation.3 | async-start | bytes 835584 | tf_op jit(solution)/shard_map/reduce_scatter | solution.py:62
  272.7 7.1 %copy-start = (bf16[512,1536]{1,0:T(8,128)(2,1)S(1)}, bf16[512,1536]{1,0:T(8,128)(2,1)}, u32[]{:S(2)}) copy-start(bf16[512,1536]{1,0:T(8,128)(2,1)} %all-gather.3.cloned.1.call-done) | copy-start | bytes 4718596
  272.7 7.2 %copy-start.1 = (bf16[1,384,1536]{2,1,0:T(8,128)(2,1)S(1)}, bf16[1,384,1536]{2,1,0:T(8,128)(2,1)}, u32[]{:S(2)}) copy-start(bf16[1,384,1536]{2,1,0:T(8,128)(2,1)} %param.6) | copy-start | bytes 3538948
  274.9 6.9 %copy-start.5 = (f32[1,384]{1,0:T(1,128)S(1)}, f32[1,384]{1,0:T(1,128)}, u32[]{:S(2)}) copy-start(f32[1,384]{1,0:T(1,128)} %param.10) | copy-start | bytes 4612
  275.0 7.5 %copy-start.4 = (f32[1,1536]{1,0:T(1,128)S(1)}, f32[1,1536]{1,0:T(1,128)}, u32[]{:S(2)}) copy-start(f32[1,1536]{1,0:T(1,128)} %param.11) | copy-start | bytes 18436
  275.0 102.5 %collective-permute-start.1 = (f32[384,1536]{1,0:T(8,128)}, f32[384,1536]{1,0:T(8,128)}, u32[]{:S(2)}, u32[]{:S(2)}) collective-permute-start(f32[384,1536]{1,0:T(8,128)} %fusion.4), channel_id=1, source_target_pairs={{256,0},{0,256},{257,1},{1,257},{258,2},{2,258},{259,3},{3,259},{2... | collective-permute-start | bytes 7077896 | tf_op jit(solution)/shard_map/ppermute | solution.py:18
Sparse Core Ops, SparseCore 0:
  61.8 68.3 reduce-scatter.6
  132.3 68.7 all-gather.4
  203.7 68.9 all-gather.2
  281.9 94.0 reduce-scatter.4
where the time goes:
time: 461 us; the launch traced here: 455 us
  waiting for transfers between devices  265 us (57%)
  blocking collectives  143 us (31%)
  between operations  14.5 us (3%)
  matrix products  11.4 us (2%)
  other arithmetic  10.3 us (2%)
  starting transfers between devices  9.09 us (2%)
    reduce_scatter x1, waiting for transfers between devices, shards(): lax.psum_scatter(lax.dot_general(grad_rows, up_tile, (((1,), (1,)), ((),...  93.6 us
    all_gather x1, waiting for transfers between devices, shards(): pre_grad = lax.all_gather(pre_share, 'hid', axis=0, tiled=True)  69.8 us
    reduce_scatter x1, waiting for transfers between devices, shards(): lax.psum_scatter(jnp.dot(grad_rows, down_tile, preferred_element_type=jnp...  67.7 us
    all_gather x1, blocking collectives, shards(): lax.all_gather(grad_out, 'wid', axis=0, tiled=True)  45.3 us
    all_gather x1, blocking collectives, shards(): lax.all_gather(inputs, 'wid', axis=0, tiled=True)  36.1 us
    psum x1, blocking collectives, shards(): row_total = lax.psum(row_local, 'wid')  35.2 us
    all_gather x1, waiting for transfers between devices, shards(): pre_half = lax.all_gather(preact, 'hid', axis=0, tiled=True)  33 us
    psum x1, blocking collectives, shards(): col_total, row_sum = lax.psum((col_local, jnp.sum(row_moment)), 'hid')  26 us
  transfers between devices with their start and end apart: 6, of which 4 were waited for; matrix products, arithmetic and copies ran while one was open for 2% of the time, Pallas kernels for 0%

commit v1 on v0

v1 whole, which is shorter than its diff:
```python
import jax
import jax.numpy as jnp
from jax import lax
from jax.sharding import PartitionSpec as P

D = 6144
FF = 24576


decay_rate = 0.9
root_half = 0.7071067811865476
inv_root_tau = 0.3989422804014327
LANES = 128


def normal_cdf(pre):
    return 0.5 * (1.0 + lax.erf(pre * root_half))


def gelu_value(pre):
    return pre * normal_cdf(pre)


def gelu_slope(pre):
    return normal_cdf(pre) + pre * jnp.exp(-0.5 * pre * pre) * inv_root_tau


def contract(left, right):
    return lax.dot_general(
        left, right, (((0,), (0,)), ((), ())), preferred_element_type=jnp.float32
    )


def exchange(blocks, axis):
    return lax.all_to_all(blocks, axis, split_axis=0, concat_axis=0, tiled=True)


def spread(block, axis):
    n = lax.axis_size(axis)
    copies = jnp.broadcast_to(block[None], (n,) + block.shape)
    return exchange(copies.reshape((n * block.shape[0],) + block.shape[1:]), axis)


def shards(weights, preact, inputs, grad_out, row_state, col_state):
    hid = lax.axis_size("hid")
    wid = lax.axis_size("wid")
    own_tile = weights[0]
    features, hidden = own_tile.shape
    rows = grad_out.shape[0]
    first = lax.axis_index("section") == 0

    kept = jnp.where(first, inputs, grad_out)
    given = jnp.where(first, grad_out, inputs)
    taken = lax.ppermute(given, "section", [(0, 1), (1, 0)])
    pre_taken = lax.ppermute(preact, "section", [(0, 1), (1, 0)])
    left_own = jnp.concatenate([jnp.where(first, kept, taken), jnp.where(first, taken, kept)])
    left = spread(left_own, "wid")

    hidden_share = lax.psum_scatter(
        jnp.dot(left, own_tile, preferred_element_type=jnp.float32),
        "hid",
        scatter_dimension=0,
        tiled=True,
    )
    pre_pair = jnp.concatenate(
        [jnp.where(first, preact, pre_taken), jnp.where(first, pre_taken, preact)]
    ).astype(jnp.float32)
    pre_share = (hidden_share * gelu_slope(pre_pair)).astype(jnp.bfloat16)
    pre_share = lax.ppermute(pre_share, "section", [(1, 0)])
    act_share = gelu_value(pre_pair).astype(jnp.bfloat16)
    right = lax.all_gather(jnp.where(first, pre_share, act_share), "hid", axis=0, tiled=True)

    gradient = contract(left, right)
    squares = gradient * gradient
    row_local = jnp.sum(squares, axis=1)
    col_local = jnp.sum(squares, axis=0)
    row_prev = row_state[0]
    col_prev = col_state[0]
    scalars = jnp.stack([jnp.sum(row_local), jnp.sum(row_prev)])
    tail = jnp.concatenate([scalars, jnp.zeros((4 * LANES - 2,), jnp.float32)])
    packed = jnp.concatenate([col_local, tail]).reshape(-1, LANES)
    over_hid = jnp.sum(
        spread(packed, "hid").reshape((hid,) + packed.shape), axis=0
    ).reshape(-1)
    col_total = over_hid[:hidden]
    square_sum, prev_sum = over_hid[hidden], over_hid[hidden + 1]

    partial = lax.dot_general(
        right, own_tile, (((1,), (1,)), ((), ())), preferred_element_type=jnp.float32
    )
    extra = jnp.concatenate(
        [row_local[None], jnp.broadcast_to(square_sum, (1, features)), jnp.zeros((6, features), jnp.float32)]
    )
    blocks = jnp.concatenate(
        [partial.reshape(wid, 2 * rows, features), jnp.broadcast_to(extra[None], (wid,) + extra.shape)],
        axis=1,
    )
    over_wid = jnp.sum(
        exchange(blocks.reshape(-1, features), "wid").reshape(blocks.shape), axis=0
    )
    input_sum = jnp.where(
        first, over_wid[:rows], lax.ppermute(over_wid[rows : 2 * rows], "section", [(0, 1)])
    )
    input_grad = input_sum + grad_out.astype(jnp.float32)

    row_total = over_wid[2 * rows]
    square_total = over_wid[2 * rows + 1, 0]
    row_moment = decay_rate * row_prev + (1.0 - decay_rate) / FF * row_total
    col_moment = decay_rate * col_prev + (1.0 - decay_rate) / D * col_total
    row_mean = decay_rate / D * prev_sum + (1.0 - decay_rate) / FF / D * square_total
    update = gradient * lax.rsqrt(row_moment[:, None] * col_moment[None, :] / row_mean)
    return (input_grad, update[None])


def solution(mesh):
    placed = (
        P("section", "hid", "wid"),
        P(("section", "hid"), "wid"),
        P(("section", "wid"), "hid"),
        P(("section", "wid"), "hid"),
        P("section", "hid"),
        P("section", "wid"),
    )
    return jax.shard_map(
        shards,
        mesh=mesh,
        in_specs=placed,
        out_specs=(P(("section", "wid"), "hid"), P("section", "hid", "wid")),
        check_vma=False,
    )
```

time: 461 us -> 293 us (0.64); the launches traced: 455 us -> 292 us
  blocking collectives: 143 us -> 24.3 us
  waiting for transfers between devices: 265 us -> 189 us
  starting transfers between devices: 9.09 us -> 34.9 us
    reduce_scatter x2 -> x1, waiting for transfers between devices: 161 us -> 73.4 us  [shards(): lax.psum_scatter(jnp.dot(left, own_tile, preferred_element_type=jnp.float...]
    all_gather x2 -> x0, blocking collectives: 81.5 us -> none  [the longest x1 45.3 us: shards(): lax.all_gather(grad_out, 'wid', axis=0, tiled=True)]
    psum x2 -> x0, blocking collectives: 61.2 us -> none  [the longest x1 35.2 us: shards(): row_total = lax.psum(row_local, 'wid')]
    all_to_all x0 -> x2, waiting for transfers between devices: none -> 32.3 us  [exchange(): return lax.all_to_all(blocks, axis, split_axis=0, concat_axis=0, tiled=True)]
    all_gather x2 -> x1, waiting for transfers between devices: 103 us -> 73.4 us  [shards(): lax.all_gather(jnp.where(first, pre_share, act_share), 'hid', axis=0, til...]
    all_to_all x0 -> x2, starting transfers between devices: none -> 25.4 us  [exchange(): return lax.all_to_all(blocks, axis, split_axis=0, concat_axis=0, tiled=True)]
    all_to_all x0 -> x1, blocking collectives: none -> 24.3 us  [exchange(): return lax.all_to_all(blocks, axis, split_axis=0, concat_axis=0, tiled=True)]
    ppermute x2 -> x4, waiting for transfers between devices: 0.01 us -> 10.2 us  [the longest x1 5.11 us: shards(): pre_share = lax.ppermute(pre_share, 'section', [(1, 0)])]
  transfers between devices with their start and end apart: 6 -> 8, of which waited for: 4 -> 7; matrix products, arithmetic and copies ran while one was open for 2% -> 3% of each run, Pallas kernels for 0% -> 0%
where the time goes in v1:
time: 293 us; the launch traced here: 292 us
  waiting for transfers between devices  189 us (65%)
  starting transfers between devices  34.9 us (12%)
  blocking collectives  24.3 us (8%)
  between operations  15.5 us (5%)
  matrix products  13.5 us (5%)
  other arithmetic  9.83 us (3%)
  local copies, waits for them, and re-layouts  4.92 us (2%)
    all_gather x1, waiting for transfers between devices, shards(): lax.all_gather(jnp.where(first, pre_share, act_share), 'hid', axis=0, til...  73.4 us
    reduce_scatter x1, waiting for transfers between devices, shards(): lax.psum_scatter(jnp.dot(left, own_tile, preferred_element_type=jnp.float...  73.4 us
    all_to_all x2, waiting for transfers between devices, exchange(): return lax.all_to_all(blocks, axis, split_axis=0, concat_axis=0, tiled=True)  32.3 us
    all_to_all x2, starting transfers between devices, exchange(): return lax.all_to_all(blocks, axis, split_axis=0, concat_axis=0, tiled=True)  25.4 us
    all_to_all x1, blocking collectives, exchange(): return lax.all_to_all(blocks, axis, split_axis=0, concat_axis=0, tiled=True)  24.3 us
  transfers between devices with their start and end apart: 8, of which 7 were waited for; matrix products, arithmetic and copies ran while one was open for 3% of the time, Pallas kernels for 0%

profile of v1, /device:TPU:1, one launch (start us, length us, event | category | flops | bytes accessed | tf_op | source)
XLA Modules:
  0.0 292.3 jit_solution(9100968734572021930)
XLA Ops:
  7.2 0.8 broadcast_select_fusion.4
  8.1 4.0 %collective-permute-start = (bf16[32,384]{1,0:T(8,128)(2,1)S(1)}, bf16[32,384]{1,0:T(8,128)(2,1)S(1)}, u32[]{:S(2)}, u32[]{:S(2)}) collective-permute-start(bf16[32,384]{1,0:T(8,128)(2,1)S(1)} %broadcast_select_fusion.4), channel_id=1, source_target_pairs={{0,256},{256,0},{1,257},{257,1},{2,258},{258,2},{3,259},{259,3},{4... | collective-permute-start | bytes 73736 | tf_op jit(solution)/shard_map/ppermute | solution.py:54
  12.1 1.2 collective-permute-done
  14.2 24.3 %all_to_all.21 = bf16[16,64,384]{2,1,0:T(8,128)(2,1)S(1)} all-to-all(bf16[16,64,384]{2,1,0:T(8,128)(2,1)S(1)} %broadcast_in_dim.36), channel_id=1, replica_groups=mesh['section'=2,'hid'=16,'wid'=16] {'wid'}, dimensions={0} | all-to-all | bytes 1572864 | tf_op jit(solution)/shard_map/all_to_all | solution.py:35
  38.5 4.5 %fusion.2 = f32[1024,1536]{1,0:T(8,128)} fusion(bf16[1024,384]{1,0:T(8,128)(2,1)S(1)} %bitcast.28, bf16[1,384,1536]{2,1,0:T(8,128)(2,1)S(1)} %copy-done), kind=kOutput, calls=%fused_computation.7 | convolution fusion | flops 1207959552 | bytes 8257536 | tf_op jit(solution)/shard_map/dot_general | solution.py:60
  43.0 0.8 copy-done.2
  43.8 1.9 collective-permute-start.1
  45.7 3.9 %collective-permute-done.1 = bf16[32,1536]{1,0:T(8,128)(2,1)S(1)} collective-permute-done((bf16[32,1536]{1,0:T(8,128)(2,1)S(1)}, bf16[32,1536]{1,0:T(8,128)(2,1)S(1)}, u32[]{:S(2)}, u32[]{:S(2)}) %collective-permute-start.1) | collective-permute-done | bytes 98336 | tf_op jit(solution)/shard_map/ppermute | solution.py:55
  49.7 73.4 %reduce-scatter.2.cloned.1.call-done = f32[64,1536]{1,0:T(8,128)} async-done(((f32[1024,1536]{1,0:T(8,128)}), f32[64,1536]{1,0:T(8,128)}) %reduce-scatter.2.cloned.1.call-update) | async-done | bytes 393232 | tf_op jit(solution)/shard_map/reduce_scatter | solution.py:59
  123.0 1.2 fusion.11
  124.2 1.3 collective-permute-start.2
  125.5 5.1 %collective-permute-done.2 = bf16[64,1536]{1,0:T(8,128)(2,1)S(1)} collective-permute-done((bf16[64,1536]{1,0:T(8,128)(2,1)S(1)}, bf16[64,1536]{1,0:T(8,128)(2,1)S(1)}, u32[]{:S(2)}, u32[]{:S(2)}) %collective-permute-start.2) | collective-permute-done | bytes 196640 | tf_op jit(solution)/shard_map/ppermute | solution.py:69
  130.6 0.8 fusion.13
  132.0 73.4 %all-gather.2.cloned.1.call-done = bf16[1024,1536]{1,0:T(8,128)(2,1)} async-done(((bf16[64,1536]{1,0:T(8,128)(2,1)}), bf16[1024,1536]{1,0:T(8,128)(2,1)}) %all-gather.2.cloned.1.call-update) | async-done | bytes 3145744 | tf_op jit(solution)/shard_map/all_gather | solution.py:71
  205.4 5.4 %multiply_reduce_fusion = (f32[]{:T(128)}, f32[1536]{0:T(1024)S(1)}, f32[384]{0:T(512)S(1)}, f32[384,1536]{1,0:T(8,128)}) fusion(bf16[1024,384]{1,0:T(8,128)(2,1)S(1)} %bitcast.29, bf16[1024,1536]{1,0:T(8,128)(2,1)} %all-gather.2.cloned.1.call-done), kind=kOutput, calls=%fused_computation.1 | convolution fusion | flops 1210316928 | bytes 6299140 | tf_op jit(solution)/shard_map/dot_general | solution.py:29
  210.8 1.3 concatenate.17
  212.7 6.6 %all-to-all-start.1 = ((f32[16,16,128]{2,1,0:T(8,128)}), f32[16,16,128]{2,1,0:T(8,128)S(1)}, u32[]{:S(2)}, u32[]{:S(2)}) async-start(f32[16,16,128]{2,1,0:T(8,128)} %broadcast_in_dim.40), calls=%async_computation.2 | async-start | bytes 262144 | tf_op jit(solution)/shard_map/all_to_all | solution.py:35
  219.5 3.7 %fusion = f32[16,64,384]{2,1,0:T(8,128)S(1)} fusion(bf16[16,64,1536]{2,1,0:T(8,128)(2,1)} %bitcast.32, bf16[1,384,1536]{2,1,0:T(8,128)(2,1)S(1)} %copy-done), kind=kOutput, calls=%fused_computation.5 | convolution fusion | flops 1207959552 | bytes 5898240 | tf_op jit(solution)/shard_map/dot_general | solution.py:88
  223.2 8.2 %all-to-all-done.1 = f32[16,16,128]{2,1,0:T(8,128)S(1)} async-done(((f32[16,16,128]{2,1,0:T(8,128)}), f32[16,16,128]{2,1,0:T(8,128)S(1)}, u32[]{:S(2)}, u32[]{:S(2)}) %all-to-all-start.1) | async-done | bytes 131104 | tf_op jit(solution)/shard_map/all_to_all | solution.py:35
  232.8 1.3 pad_maximum_fusion
  234.2 18.7 %all-to-all-start.2 = ((f32[16,72,384]{2,1,0:T(8,128)}), f32[16,72,384]{2,1,0:T(8,128)S(1)}, u32[]{:S(2)}, u32[]{:S(2)}) async-start(f32[16,72,384]{2,1,0:T(8,128)} %pad_maximum_fusion), calls=%async_computation.3 | async-start | bytes 3538944 | tf_op jit(solution)/shard_map/all_to_all | solution.py:35
  253.6 24.1 %all-to-all-done.2 = f32[16,72,384]{2,1,0:T(8,128)S(1)} async-done(((f32[16,72,384]{2,1,0:T(8,128)}), f32[16,72,384]{2,1,0:T(8,128)S(1)}, u32[]{:S(2)}, u32[]{:S(2)}) %all-to-all-start.2) | async-done | bytes 1769504 | tf_op jit(solution)/shard_map/all_to_all | solution.py:35
  278.4 2.2 collective-permute-start.3
  281.3 3.5 %multiply_bitcast_fusion = f32[1,384,1536]{2,1,0:T(8,128)} fusion(f32[384,1536]{1,0:T(8,128)} %get-tuple-element.11, f32[]{:T(128)S(6)} %add.35, f32[1536]{0:T(1024)S(1)} %fusion.16, f32[384]{0:T(512)S(1)} %fusion.18), kind=kLoop, calls=%fused_computation | loop fusion | flops 1769472 | bytes 4726276 | tf_op jit(solution)/shard_map/broadcast_in_dim | solution.py:112
  (36 shorter events, 5.2 us)
Async XLA Ops:
  7.2 31.3 %copy-start = (bf16[1,384,1536]{2,1,0:T(8,128)(2,1)S(1)}, bf16[1,384,1536]{2,1,0:T(8,128)(2,1)}, u32[]{:S(2)}) copy-start(bf16[1,384,1536]{2,1,0:T(8,128)(2,1)} %param.6) | copy-start | bytes 3538948
  7.2 115.9 %reduce-scatter.2.cloned.1.call-start = ((), (), s32[]{:S(2)}) async-start(), calls=%async_computation.4 | async-start | bytes 6684672 | tf_op jit(solution)/shard_map/reduce_scatter | solution.py:59
  8.1 5.2 %collective-permute-start = (bf16[32,384]{1,0:T(8,128)(2,1)S(1)}, bf16[32,384]{1,0:T(8,128)(2,1)S(1)}, u32[]{:S(2)}, u32[]{:S(2)}) collective-permute-start(bf16[32,384]{1,0:T(8,128)(2,1)S(1)} %broadcast_select_fusion.4), channel_id=1, source_target_pairs={{0,256},{256,0},{1,257},{257,1},{2,258},{258,2},{3,259},{259,3},{4... | collective-permute-start | bytes 73736 | tf_op jit(solution)/shard_map/ppermute | solution.py:54
  42.9 0.9 copy-start.2
  42.9 88.5 %copy-start.3 = (f32[1,384]{1,0:T(1,128)S(1)}, f32[1,384]{1,0:T(1,128)}, u32[]{:S(2)}) copy-start(f32[1,384]{1,0:T(1,128)} %param.10) | copy-start | bytes 4612
  43.0 162.5 %all-gather.2.cloned.1.call-start = ((), (), s32[]{:S(2)}) async-start(), calls=%async_computation.5 | async-start | bytes 3342336 | tf_op jit(solution)/shard_map/all_gather | solution.py:71
  43.8 5.8 %collective-permute-start.1 = (bf16[32,1536]{1,0:T(8,128)(2,1)S(1)}, bf16[32,1536]{1,0:T(8,128)(2,1)S(1)}, u32[]{:S(2)}, u32[]{:S(2)}) collective-permute-start(bf16[32,1536]{1,0:T(8,128)(2,1)S(1)} %copy-done.2), channel_id=1, source_target_pairs={{0,256},{256,0},{1,257},{257,1},{2,258},{258,2},{3,259},{259,3},{4... | collective-permute-start | bytes 294920 | tf_op jit(solution)/shard_map/ppermute | solution.py:55
  124.2 6.4 %collective-permute-start.2 = (bf16[64,1536]{1,0:T(8,128)(2,1)S(1)}, bf16[64,1536]{1,0:T(8,128)(2,1)S(1)}, u32[]{:S(2)}, u32[]{:S(2)}) collective-permute-start(bf16[64,1536]{1,0:T(8,128)(2,1)S(1)} %fusion.11), channel_id=1, source_target_pairs={{256,0},{257,1},{258,2},{259,3},{260,4},{261,5},{262,6},{263,7},{2... | collective-permute-start | bytes 589832 | tf_op jit(solution)/shard_map/ppermute | solution.py:69
  212.7 18.6 %all-to-all-start.1 = ((f32[16,16,128]{2,1,0:T(8,128)}), f32[16,16,128]{2,1,0:T(8,128)S(1)}, u32[]{:S(2)}, u32[]{:S(2)}) async-start(f32[16,16,128]{2,1,0:T(8,128)} %broadcast_in_dim.40), calls=%async_computation.2 | async-start | bytes 262144 | tf_op jit(solution)/shard_map/all_to_all | solution.py:35
  234.2 19.4 %copy-start.4 = (f32[1,1536]{1,0:T(1,128)S(1)}, f32[1,1536]{1,0:T(1,128)}, u32[]{:S(2)}) copy-start(f32[1,1536]{1,0:T(1,128)} %param.11) | copy-start | bytes 18436
  234.2 43.5 %all-to-all-start.2 = ((f32[16,72,384]{2,1,0:T(8,128)}), f32[16,72,384]{2,1,0:T(8,128)S(1)}, u32[]{:S(2)}, u32[]{:S(2)}) async-start(f32[16,72,384]{2,1,0:T(8,128)} %pad_maximum_fusion), calls=%async_computation.3 | async-start | bytes 3538944 | tf_op jit(solution)/shard_map/all_to_all | solution.py:35
  278.4 6.4 %collective-permute-start.3 = (f32[32,384]{1,0:T(8,128)S(1)}, f32[32,384]{1,0:T(8,128)S(1)}, u32[]{:S(2)}, u32[]{:S(2)}) collective-permute-start(f32[32,384]{1,0:T(8,128)S(1)} %slice.31), channel_id=1, source_target_pairs={{0,256},{1,257},{2,258},{3,259},{4,260},{5,261},{6,262},{7,263},{8... | collective-permute-start | bytes 147464 | tf_op jit(solution)/shard_map/ppermute | solution.py:102
  281.3 3.5 %copy-start.1 = (bf16[32,384]{1,0:T(8,128)(2,1)S(1)}, bf16[32,384]{1,0:T(8,128)(2,1)}, u32[]{:S(2)}) copy-start(bf16[32,384]{1,0:T(8,128)(2,1)} %param.9) | copy-start | bytes 73732
Sparse Core Ops, SparseCore 0:
  43.1 79.9 reduce-scatter.1
  131.6 73.8 all-gather.1

commit v2 on v1

--- a/solution.py
+++ b/solution.py
@@ -41,6 +41,18 @@
     return exchange(copies.reshape((n * block.shape[0],) + block.shape[1:]), axis)
 
 
+def thirds(values, scalar):
+    shape = (16, values.shape[0])
+    row = lax.broadcasted_iota(jnp.int32, shape, 0)
+    rest = jnp.where(row < 8, jnp.broadcast_to(values[None], shape), scalar)
+    out = jnp.zeros(shape, jnp.float32)
+    for k in range(3):
+        term = lax.reduce_precision(rest, exponent_bits=8, mantissa_bits=7)
+        out = jnp.where(row % 8 == k, term, out)
+        rest = rest - term
+    return out.astype(jnp.bfloat16)
+
+
 def shards(weights, preact, inputs, grad_out, row_state, col_state):
     hid = lax.axis_size("hid")
     wid = lax.axis_size("wid")
@@ -48,27 +60,42 @@
     features, hidden = own_tile.shape
     rows = grad_out.shape[0]
     first = lax.axis_index("section") == 0
+    even = lax.axis_index("hid") % 2 == 0
+    pair = ("section", "hid")
+    evens = range(0, hid, 2)
+    down = [(h, hid + h) for h in evens]
+    across = [(h + 1, hid + h) for h in evens] + [(hid + h, hid + h + 1) for h in evens]
+    swap = [(hid + h, hid + (h ^ 1)) for h in range(hid)]
+    rings = [list(range(p, hid, 2)) for p in range(2)]
 
-    kept = jnp.where(first, inputs, grad_out)
-    given = jnp.where(first, grad_out, inputs)
-    taken = lax.ppermute(given, "section", [(0, 1), (1, 0)])
-    pre_taken = lax.ppermute(preact, "section", [(0, 1), (1, 0)])
-    left_own = jnp.concatenate([jnp.where(first, kept, taken), jnp.where(first, taken, kept)])
-    left = spread(left_own, "wid")
-
+    grad_down = lax.ppermute(grad_out, pair, down)
+    grad_across = lax.ppermute(grad_out, pair, across)
+    next_tile = lax.ppermute(own_tile, pair, swap)
+    grad_pair = jnp.concatenate([jnp.where(even, grad_down, grad_out), grad_across], axis=1)
+    grad_half = spread(grad_pair, "wid")
+    hidden_part = jnp.dot(
+        grad_half[:, :features], own_tile, preferred_element_type=jnp.float32
+    ) + jnp.dot(grad_half[:, features:], next_tile, preferred_element_type=jnp.float32)
     hidden_share = lax.psum_scatter(
-        jnp.dot(left, own_tile, preferred_element_type=jnp.float32),
-        "hid",
-        scatter_dimension=0,
-        tiled=True,
+        hidden_part, "hid", scatter_dimension=0, axis_index_groups=rings, tiled=True
     )
+    pre_down = lax.ppermute(preact, pair, down)
+    pre_across = lax.ppermute(preact, pair, across)
     pre_pair = jnp.concatenate(
-        [jnp.where(first, preact, pre_taken), jnp.where(first, pre_taken, preact)]
+        [jnp.where(even, pre_down, pre_across), jnp.where(even, pre_across, preact)]
     ).astype(jnp.float32)
     pre_share = (hidden_share * gelu_slope(pre_pair)).astype(jnp.bfloat16)
     pre_share = lax.ppermute(pre_share, "section", [(1, 0)])
     act_share = gelu_value(pre_pair).astype(jnp.bfloat16)
     right = lax.all_gather(jnp.where(first, pre_share, act_share), "hid", axis=0, tiled=True)
+
+    kept = jnp.where(first, inputs, grad_out)
+    given = jnp.where(first, grad_out, inputs)
+    taken = lax.ppermute(given, "section", [(0, 1), (1, 0)])
+    left_own = jnp.concatenate([jnp.where(first, kept, taken), jnp.where(first, taken, kept)])
+    left = jnp.swapaxes(
+        spread(left_own, "wid").reshape(wid // 2, 2, 2, rows, features), 1, 2
+    ).reshape(2 * wid * rows, features)
 
     gradient = contract(left, right)
     squares = gradient * gradient
@@ -87,24 +114,21 @@
 
     partial = lax.dot_general(
         right, own_tile, (((1,), (1,)), ((), ())), preferred_element_type=jnp.float32
-    )
-    extra = jnp.concatenate(
-        [row_local[None], jnp.broadcast_to(square_sum, (1, features)), jnp.zeros((6, features), jnp.float32)]
-    )
+    ).astype(jnp.bfloat16)
+    blocks = jnp.swapaxes(partial.reshape(wid // 2, 2, 2, rows, features), 1, 2)
+    extra = thirds(row_local, square_sum)
     blocks = jnp.concatenate(
-        [partial.reshape(wid, 2 * rows, features), jnp.broadcast_to(extra[None], (wid,) + extra.shape)],
+        [blocks.reshape(wid, 2 * rows, features), jnp.broadcast_to(extra[None], (wid,) + extra.shape)],
         axis=1,
     )
-    over_wid = jnp.sum(
-        exchange(blocks.reshape(-1, features), "wid").reshape(blocks.shape), axis=0
-    )
+    over_wid = jnp.sum(exchange(blocks, "wid").astype(jnp.float32), axis=0)
     input_sum = jnp.where(
         first, over_wid[:rows], lax.ppermute(over_wid[rows : 2 * rows], "section", [(0, 1)])
     )
     input_grad = input_sum + grad_out.astype(jnp.float32)
+    row_total = jnp.sum(over_wid[2 * rows : 2 * rows + 8], axis=0)
+    square_total = jnp.sum(over_wid[2 * rows + 8 :, 0])
 
-    row_total = over_wid[2 * rows]
-    square_total = over_wid[2 * rows + 1, 0]
     row_moment = decay_rate * row_prev + (1.0 - decay_rate) / FF * row_total
     col_moment = decay_rate * col_prev + (1.0 - decay_rate) / D * col_total
     row_mean = decay_rate / D * prev_sum + (1.0 - decay_rate) / FF / D * square_total

time: 293 us -> 287 us (0.980)
  waiting for transfers between devices: 189 us -> 166 us
  starting transfers between devices: 34.9 us -> 50.8 us
    all_gather x1, waiting for transfers between devices: 73.4 us -> 41.9 us  [shards(): lax.all_gather(jnp.where(first, pre_share, act_share), 'hid', axis=0, til...]
    all_to_all x2 -> x3, starting transfers between devices: 25.4 us -> 33.8 us  [exchange(): return lax.all_to_all(blocks, axis, split_axis=0, concat_axis=0, tiled=True)]
    reduce_scatter x1, waiting for transfers between devices: 73.4 us -> 81.1 us  [shards(): lax.psum_scatter(hidden_part, 'hid', scatter_dimension=0, axis_index_grou...]
    ppermute x1 -> x5, starting transfers between devices: 1.91 us -> 9.33 us  [the longest x1 5.34 us: shards(): pre_down = lax.ppermute(preact, pair, down)]
    all_to_all x2 -> x3, waiting for transfers between devices: 32.3 us -> 35.4 us  [exchange(): return lax.all_to_all(blocks, axis, split_axis=0, concat_axis=0, tiled=True)]
    ppermute x1 -> x5, waiting for transfers between devices: 3.9 us -> 0.95 us  [the longest x1 0.94 us: shards(): pre_down = lax.ppermute(preact, pair, down)]
  transfers between devices with their start and end apart: 8 -> 13, of which waited for: 7 -> 7; matrix products, arithmetic and copies ran while one was open for 3% -> 4% of each run, Pallas kernels for 0% -> 0%
where the time goes in v2:
time: 287 us; the launch traced here: 286 us
  waiting for transfers between devices  166 us (58%)
  starting transfers between devices  50.8 us (18%)
  blocking collectives  24 us (8%)
  between operations  15.6 us (5%)
  other arithmetic  12 us (4%)
  matrix products  11.9 us (4%)
  local copies, waits for them, and re-layouts  6.38 us (2%)
    reduce_scatter x1, waiting for transfers between devices, shards(): lax.psum_scatter(hidden_part, 'hid', scatter_dimension=0, axis_index_grou...  81.1 us
    all_gather x1, waiting for transfers between devices, shards(): lax.all_gather(jnp.where(first, pre_share, act_share), 'hid', axis=0, til...  41.9 us
    all_to_all x3, waiting for transfers between devices, exchange(): return lax.all_to_all(blocks, axis, split_axis=0, concat_axis=0, tiled=True)  35.4 us
    all_to_all x3, starting transfers between devices, exchange(): return lax.all_to_all(blocks, axis, split_axis=0, concat_axis=0, tiled=True)  33.8 us
    all_to_all x1, blocking collectives, exchange(): return lax.all_to_all(blocks, axis, split_axis=0, concat_axis=0, tiled=True)  24 us
    ppermute x1, waiting for transfers between devices, shards(): pre_share = lax.ppermute(pre_share, 'section', [(1, 0)])  6.18 us
  transfers between devices with their start and end apart: 13, of which 7 were waited for; matrix products, arithmetic and copies ran while one was open for 4% of the time, Pallas kernels for 0%

profile of v2, /device:TPU:1, one launch (start us, length us, event | category | flops | bytes accessed | tf_op | source)
XLA Modules:
  0.0 286.2 jit_solution(6512408949016189230)
XLA Ops:
  8.1 4.0 %collective-permute-start.6 = (bf16[32,384]{1,0:T(8,128)(2,1)S(1)}, bf16[32,384]{1,0:T(8,128)(2,1)S(1)}, u32[]{:S(2)}, u32[]{:S(2)}) collective-permute-start(bf16[32,384]{1,0:T(8,128)(2,1)S(1)} %broadcast_select_fusion.5), channel_id=1, source_target_pairs={{0,256},{256,0},{1,257},{257,1},{2,258},{258,2},{3,259},{259,3},{4... | collective-permute-start | bytes 73736 | tf_op jit(solution)/shard_map/ppermute | solution.py:94
  12.1 1.9 collective-permute-start
  16.4 24.0 %all_to_all.26 = bf16[16,32,768]{2,1,0:T(8,128)(2,1)S(1)} all-to-all(bf16[16,32,768]{2,1,0:T(8,128)(2,1)S(1)} %broadcast_in_dim.22), channel_id=1, replica_groups=mesh['section'=2,'hid'=16,'wid'=16] {'wid'}, dimensions={0} | all-to-all | bytes 1572864 | tf_op jit(solution)/shard_map/all_to_all | solution.py:35
  41.3 2.6 convolution_add_fusion
  44.8 5.3 %collective-permute-start.3 = (bf16[32,1536]{1,0:T(8,128)(2,1)S(1)}, bf16[32,1536]{1,0:T(8,128)(2,1)S(1)}, u32[]{:S(2)}, u32[]{:S(2)}) collective-permute-start(bf16[32,1536]{1,0:T(8,128)(2,1)S(1)} %copy-done.2), channel_id=1, source_target_pairs={{0,256},{32,288},{64,320},{96,352},{128,384},{160,416},{192,448},{... | collective-permute-start | bytes 294920 | tf_op jit(solution)/shard_map/ppermute | solution.py:82
  51.8 81.1 %reduce-scatter.2.cloned.1.call-done = f32[64,1536]{1,0:T(8,128)} async-done(((f32[512,1536]{1,0:T(8,128)}), f32[64,1536]{1,0:T(8,128)}) %reduce-scatter.2.cloned.1.call-update) | async-done | bytes 393232 | tf_op jit(solution)/shard_map/reduce_scatter | solution.py:79
  132.9 1.2 fusion.7
  134.1 1.3 collective-permute-start.5
  135.4 6.2 %collective-permute-done.5 = bf16[64,1536]{1,0:T(8,128)(2,1)S(1)} collective-permute-done((bf16[64,1536]{1,0:T(8,128)(2,1)S(1)}, bf16[64,1536]{1,0:T(8,128)(2,1)S(1)}, u32[]{:S(2)}, u32[]{:S(2)}) %collective-permute-start.5) | collective-permute-done | bytes 196640 | tf_op jit(solution)/shard_map/ppermute | solution.py:88
  143.4 8.5 %all-to-all-start.1 = ((bf16[16,64,384]{2,1,0:T(8,128)(2,1)}), bf16[16,64,384]{2,1,0:T(8,128)(2,1)S(1)}, u32[]{:S(2)}, u32[]{:S(2)}) async-start(bf16[16,64,384]{2,1,0:T(8,128)(2,1)} %broadcast_in_dim.23), calls=%async_computation.2 | async-start | bytes 1572864 | tf_op jit(solution)/shard_map/all_to_all | solution.py:35
  153.2 12.3 %all-to-all-done.1 = bf16[16,64,384]{2,1,0:T(8,128)(2,1)S(1)} async-done(((bf16[16,64,384]{2,1,0:T(8,128)(2,1)}), bf16[16,64,384]{2,1,0:T(8,128)(2,1)S(1)}, u32[]{:S(2)}, u32[]{:S(2)}) %all-to-all-start.1) | async-done | bytes 786464 | tf_op jit(solution)/shard_map/all_to_all | solution.py:35
  165.5 1.0 copy.12
  166.5 41.9 %all-gather.2.cloned.1.call-done = bf16[1024,1536]{1,0:T(8,128)(2,1)} async-done(((bf16[64,1536]{1,0:T(8,128)(2,1)}), bf16[1024,1536]{1,0:T(8,128)(2,1)}) %all-gather.2.cloned.1.call-update) | async-done | bytes 3145744 | tf_op jit(solution)/shard_map/all_gather | solution.py:90
  208.4 4.6 %multiply_reduce_fusion.2 = (f32[384]{0:T(512)}, f32[1536]{0:T(1024)}, f32[]{:T(128)}, f32[384,1536]{1,0:T(8,128)S(1)}) fusion(bf16[1024,384]{1,0:T(8,128)(2,1)} %bitcast.38, bf16[1024,1536]{1,0:T(8,128)(2,1)} %all-gather.2.cloned.1.call-done), kind=kOutput, calls=%fused_computation.4 | convolution fusion | flops 1210316928 | bytes 6299140 | tf_op jit(solution)/shard_map/dot_general | solution.py:29
  213.0 2.1 concatenate.18
  215.8 6.8 %all-to-all-start.2 = ((f32[16,16,128]{2,1,0:T(8,128)}), f32[16,16,128]{2,1,0:T(8,128)}, u32[]{:S(2)}, u32[]{:S(2)}) async-start(f32[16,16,128]{2,1,0:T(8,128)} %broadcast_in_dim.51), calls=%async_computation.3 | async-start | bytes 262144 | tf_op jit(solution)/shard_map/all_to_all | solution.py:35
  223.2 3.7 %convolution_convert_fusion = bf16[1024,384]{1,0:T(8,128)(2,1)S(1)} fusion(bf16[1024,1536]{1,0:T(8,128)(2,1)} %all-gather.2.cloned.1.call-done, bf16[1,384,1536]{2,1,0:T(8,128)(2,1)S(1)} %copy-done), kind=kOutput, calls=%fused_computation.6 | convolution fusion | flops 1208352768 | bytes 5111808 | tf_op jit(solution)/shard_map/dot_general | solution.py:115
  227.0 7.6 %all-to-all-done.2 = f32[16,16,128]{2,1,0:T(8,128)} async-done(((f32[16,16,128]{2,1,0:T(8,128)}), f32[16,16,128]{2,1,0:T(8,128)}, u32[]{:S(2)}, u32[]{:S(2)}) %all-to-all-start.2) | async-done | bytes 131104 | tf_op jit(solution)/shard_map/all_to_all | solution.py:35
  236.1 1.4 fusion.16
  237.5 1.0 pad_maximum_fusion
  238.6 18.5 %all-to-all-start.3 = ((bf16[16,80,384]{2,1,0:T(8,128)(2,1)}), bf16[16,80,384]{2,1,0:T(8,128)(2,1)S(1)}, u32[]{:S(2)}, u32[]{:S(2)}) async-start(bf16[16,80,384]{2,1,0:T(8,128)(2,1)} %pad_maximum_fusion), calls=%async_computation.4 | async-start | bytes 1966080 | tf_op jit(solution)/shard_map/all_to_all | solution.py:35
  257.8 15.4 %all-to-all-done.3 = bf16[16,80,384]{2,1,0:T(8,128)(2,1)S(1)} async-done(((bf16[16,80,384]{2,1,0:T(8,128)(2,1)}), bf16[16,80,384]{2,1,0:T(8,128)(2,1)S(1)}, u32[]{:S(2)}, u32[]{:S(2)}) %all-to-all-start.3) | async-done | bytes 983072 | tf_op jit(solution)/shard_map/all_to_all | solution.py:35
  274.0 2.2 collective-permute-start.7
  276.9 1.8 multiply_bitcast_fusion
  (56 shorter events, 14.0 us)
Async XLA Ops:
  7.2 33.2 %copy-start = (bf16[1,384,1536]{2,1,0:T(8,128)(2,1)S(1)}, bf16[1,384,1536]{2,1,0:T(8,128)(2,1)}, u32[]{:S(2)}) copy-start(bf16[1,384,1536]{2,1,0:T(8,128)(2,1)} %param.6) | copy-start | bytes 3538948
  7.2 125.7 %reduce-scatter.2.cloned.1.call-start = ((), (), s32[]{:S(2)}) async-start(), calls=%async_computation.5 | async-start | bytes 3538944 | tf_op jit(solution)/shard_map/reduce_scatter | solution.py:79
  8.1 7.4 %collective-permute-start.6 = (bf16[32,384]{1,0:T(8,128)(2,1)S(1)}, bf16[32,384]{1,0:T(8,128)(2,1)S(1)}, u32[]{:S(2)}, u32[]{:S(2)}) collective-permute-start(bf16[32,384]{1,0:T(8,128)(2,1)S(1)} %broadcast_select_fusion.5), channel_id=1, source_target_pairs={{0,256},{256,0},{1,257},{257,1},{2,258},{258,2},{3,259},{259,3},{4... | collective-permute-start | bytes 73736 | tf_op jit(solution)/shard_map/ppermute | solution.py:94
  12.1 3.4 %collective-permute-start = (bf16[32,384]{1,0:T(8,128)(2,1)}, bf16[32,384]{1,0:T(8,128)(2,1)S(1)}, u32[]{:S(2)}, u32[]{:S(2)}) collective-permute-start(bf16[32,384]{1,0:T(8,128)(2,1)} %param.9), channel_id=1, source_target_pairs={{0,256},{32,288},{64,320},{96,352},{128,384},{160,416},{192,448},{... | collective-permute-start | bytes 73736 | tf_op jit(solution)/shard_map/ppermute | solution.py:71
  14.0 2.2 collective-permute-start.1
  14.7 26.6 %collective-permute-start.2 = (bf16[384,1536]{1,0:T(8,128)(2,1)}, bf16[384,1536]{1,0:T(8,128)(2,1)S(1)}, u32[]{:S(2)}, u32[]{:S(2)}) collective-permute-start(bf16[384,1536]{1,0:T(8,128)(2,1)} %bitcast.37), channel_id=1, source_target_pairs={{256,272},{272,256},{288,304},{304,288},{320,336},{336,320},{352,3... | collective-permute-start | bytes 3538952 | tf_op jit(solution)/shard_map/ppermute | solution.py:73
  43.9 0.9 copy-start.2
  44.0 108.5 %copy-start.5 = (f32[1,384]{1,0:T(1,128)S(1)}, f32[1,384]{1,0:T(1,128)}, u32[]{:S(2)}) copy-start(f32[1,384]{1,0:T(1,128)} %param.10) | copy-start | bytes 4612
  44.0 164.4 %all-gather.2.cloned.1.call-start = ((), (), s32[]{:S(2)}) async-start(), calls=%async_computation.6 | async-start | bytes 3342336 | tf_op jit(solution)/shard_map/all_gather | solution.py:90
  44.8 7.0 %collective-permute-start.3 = (bf16[32,1536]{1,0:T(8,128)(2,1)S(1)}, bf16[32,1536]{1,0:T(8,128)(2,1)S(1)}, u32[]{:S(2)}, u32[]{:S(2)}) collective-permute-start(bf16[32,1536]{1,0:T(8,128)(2,1)S(1)} %copy-done.2), channel_id=1, source_target_pairs={{0,256},{32,288},{64,320},{96,352},{128,384},{160,416},{192,448},{... | collective-permute-start | bytes 294920 | tf_op jit(solution)/shard_map/ppermute | solution.py:82
  50.2 1.6 collective-permute-start.4
  134.1 7.5 %collective-permute-start.5 = (bf16[64,1536]{1,0:T(8,128)(2,1)S(1)}, bf16[64,1536]{1,0:T(8,128)(2,1)S(1)}, u32[]{:S(2)}, u32[]{:S(2)}) collective-permute-start(bf16[64,1536]{1,0:T(8,128)(2,1)S(1)} %fusion.7), channel_id=1, source_target_pairs={{256,0},{257,1},{258,2},{259,3},{260,4},{261,5},{262,6},{263,7},{2... | collective-permute-start | bytes 589832 | tf_op jit(solution)/shard_map/ppermute | solution.py:88
  143.4 22.1 %all-to-all-start.1 = ((bf16[16,64,384]{2,1,0:T(8,128)(2,1)}), bf16[16,64,384]{2,1,0:T(8,128)(2,1)S(1)}, u32[]{:S(2)}, u32[]{:S(2)}) async-start(bf16[16,64,384]{2,1,0:T(8,128)(2,1)} %broadcast_in_dim.23), calls=%async_computation.2 | async-start | bytes 1572864 | tf_op jit(solution)/shard_map/all_to_all | solution.py:35
  215.8 18.8 %all-to-all-start.2 = ((f32[16,16,128]{2,1,0:T(8,128)}), f32[16,16,128]{2,1,0:T(8,128)}, u32[]{:S(2)}, u32[]{:S(2)}) async-start(f32[16,16,128]{2,1,0:T(8,128)} %broadcast_in_dim.51), calls=%async_computation.3 | async-start | bytes 262144 | tf_op jit(solution)/shard_map/all_to_all | solution.py:35
  223.1 12.9 %copy-start.4 = (f32[384]{0:T(512)S(1)}, f32[384]{0:T(512)}, u32[]{:S(2)}) copy-start(f32[384]{0:T(512)} %get-tuple-element.2) | copy-start | bytes 4612
  223.1 12.9 %copy-start.6 = (pred[16]{0:T(512)(128)(4,1)S(1)}, pred[16]{0:T(512)(128)(4,1)}, u32[]{:S(2)}) copy-start(pred[16]{0:T(512)(128)(4,1)} %get-tuple-element.15) | copy-start | bytes 52
  223.2 12.9 %copy-start.7 = (pred[16]{0:T(512)(128)(4,1)S(1)}, pred[16]{0:T(512)(128)(4,1)}, u32[]{:S(2)}) copy-start(pred[16]{0:T(512)(128)(4,1)} %get-tuple-element.16) | copy-start | bytes 52
  227.0 30.8 %copy-start.3 = (f32[1,1536]{1,0:T(1,128)S(1)}, f32[1,1536]{1,0:T(1,128)}, u32[]{:S(2)}) copy-start(f32[1,1536]{1,0:T(1,128)} %param.11) | copy-start | bytes 18436
  238.6 34.7 %all-to-all-start.3 = ((bf16[16,80,384]{2,1,0:T(8,128)(2,1)}), bf16[16,80,384]{2,1,0:T(8,128)(2,1)S(1)}, u32[]{:S(2)}, u32[]{:S(2)}) async-start(bf16[16,80,384]{2,1,0:T(8,128)(2,1)} %pad_maximum_fusion), calls=%async_computation.4 | async-start | bytes 1966080 | tf_op jit(solution)/shard_map/all_to_all | solution.py:35
  274.0 4.7 %collective-permute-start.7 = (f32[32,384]{1,0:T(8,128)S(1)}, f32[32,384]{1,0:T(8,128)S(1)}, u32[]{:S(2)}, u32[]{:S(2)}) collective-permute-start(f32[32,384]{1,0:T(8,128)S(1)} %slice.41), channel_id=1, source_target_pairs={{0,256},{1,257},{2,258},{3,259},{4,260},{5,261},{6,262},{7,263},{8... | collective-permute-start | bytes 147464 | tf_op jit(solution)/shard_map/ppermute | solution.py:126
  276.9 1.8 copy-start.1
Sparse Core Ops, SparseCore 0:
  44.1 88.7 reduce-scatter.1
  142.5 65.8 all-gather.1

commit v3 on v2

--- a/solution.py
+++ b/solution.py
@@ -53,6 +53,20 @@
     return out.astype(jnp.bfloat16)
 
 
+def sum_blocks(partial, axis, groups):
+    members = len(groups[0])
+    top = jnp.max(jnp.abs(partial), axis=1, keepdims=True)
+    power = jnp.clip(jnp.ceil(jnp.log2(jnp.maximum(top, 1e-30))), -96.0, 96.0)
+    coded = (partial * jnp.exp2(14.0 - power)).astype(jnp.float16)
+    power = jnp.broadcast_to(power, (partial.shape[0], LANES)).astype(jnp.float16)
+    coded = jnp.concatenate([coded, power], axis=1).reshape(members, -1, partial.shape[1] + LANES)
+    taken = lax.all_to_all(
+        coded, axis, split_axis=0, concat_axis=0, axis_index_groups=groups, tiled=True
+    )
+    power = jnp.max(taken[:, :, -LANES:].astype(jnp.float32), axis=2, keepdims=True)
+    return jnp.sum(taken[:, :, :-LANES].astype(jnp.float32) * jnp.exp2(power - 14.0), axis=0)
+
+
 def shards(weights, preact, inputs, grad_out, row_state, col_state):
     hid = lax.axis_size("hid")
     wid = lax.axis_size("wid")
@@ -76,9 +90,7 @@
     hidden_part = jnp.dot(
         grad_half[:, :features], own_tile, preferred_element_type=jnp.float32
     ) + jnp.dot(grad_half[:, features:], next_tile, preferred_element_type=jnp.float32)
-    hidden_share = lax.psum_scatter(
-        hidden_part, "hid", scatter_dimension=0, axis_index_groups=rings, tiled=True
-    )
+    hidden_share = sum_blocks(hidden_part, "hid", rings)
     pre_down = lax.ppermute(preact, pair, down)
     pre_across = lax.ppermute(preact, pair, across)
     pre_pair = jnp.concatenate(

time: 287 us -> 292 us (1.017)
  starting transfers between devices: 50.8 us -> 64.9 us
  waiting for transfers between devices: 166 us -> 158 us
    reduce_scatter x1 -> x0, waiting for transfers between devices: 81.1 us -> none  [shards(): lax.psum_scatter(hidden_part, 'hid', scatter_dimension=0, axis_index_grou...]
    all_to_all x0 -> x1, waiting for transfers between devices: none -> 43.6 us  [sum_blocks(): lax.all_to_all(coded, axis, split_axis=0, concat_axis=0, axis_index_group...]
    ppermute x1, waiting for transfers between devices: 6.18 us -> 38 us  [shards(): pre_share = lax.ppermute(pre_share, 'section', [(1, 0)])]
    all_to_all x0 -> x1, starting transfers between devices: none -> 13.8 us  [sum_blocks(): lax.all_to_all(coded, axis, split_axis=0, concat_axis=0, axis_index_group...]
where the time goes in v3:
time: 292 us; the launch traced here: 291 us
  waiting for transfers between devices  158 us (54%)
  starting transfers between devices  64.9 us (22%)
  blocking collectives  24 us (8%)
  between operations  15.6 us (5%)
  other arithmetic  13.4 us (5%)
  matrix products  10.3 us (4%)
  local copies, waits for them, and re-layouts  5.64 us (2%)
    all_to_all x1, waiting for transfers between devices, sum_blocks(): lax.all_to_all(coded, axis, split_axis=0, concat_axis=0, axis_index_group...  43.6 us
    all_gather x1, waiting for transfers between devices, shards(): lax.all_gather(jnp.where(first, pre_share, act_share), 'hid', axis=0, til...  39.6 us
    ppermute x1, waiting for transfers between devices, shards(): pre_share = lax.ppermute(pre_share, 'section', [(1, 0)])  38 us
    all_to_all x3, waiting for transfers between devices, exchange(): return lax.all_to_all(blocks, axis, split_axis=0, concat_axis=0, tiled=True)  35.4 us
    all_to_all x3, starting transfers between devices, exchange(): return lax.all_to_all(blocks, axis, split_axis=0, concat_axis=0, tiled=True)  33.8 us
    all_to_all x1, blocking collectives, exchange(): return lax.all_to_all(blocks, axis, split_axis=0, concat_axis=0, tiled=True)  24 us
    all_to_all x1, starting transfers between devices, sum_blocks(): lax.all_to_all(coded, axis, split_axis=0, concat_axis=0, axis_index_group...  13.8 us
  transfers between devices with their start and end apart: 13, of which 7 were waited for; matrix products, arithmetic and copies ran while one was open for 4% of the time, Pallas kernels for 0%

profile of v3, /device:TPU:1, one launch (start us, length us, event | category | flops | bytes accessed | tf_op | source)
XLA Modules:
  0.0 291.4 jit_solution(6604632691149043642)
XLA Ops:
  8.0 4.0 %collective-permute-start.6 = (bf16[32,384]{1,0:T(8,128)(2,1)S(1)}, bf16[32,384]{1,0:T(8,128)(2,1)S(1)}, u32[]{:S(2)}, u32[]{:S(2)}) collective-permute-start(bf16[32,384]{1,0:T(8,128)(2,1)S(1)} %broadcast_select_fusion.5), channel_id=1, source_target_pairs={{0,256},{256,0},{1,257},{257,1},{2,258},{258,2},{3,259},{259,3},{4... | collective-permute-start | bytes 73736 | tf_op jit(solution)/shard_map/ppermute | solution.py:106
  12.1 1.9 collective-permute-start
  16.3 24.0 %all_to_all.31 = bf16[16,32,768]{2,1,0:T(8,128)(2,1)S(1)} all-to-all(bf16[16,32,768]{2,1,0:T(8,128)(2,1)S(1)} %broadcast_in_dim.24), channel_id=1, replica_groups=mesh['section'=2,'hid'=16,'wid'=16] {'wid'}, dimensions={0} | all-to-all | bytes 1572864 | tf_op jit(solution)/shard_map/all_to_all | solution.py:35
  41.3 1.1 abs_reduce_fusion
  42.9 1.6 pad_maximum_fusion
  44.5 13.8 %all-to-all-start.1 = ((f16[8,64,1664]{2,1,0:T(8,128)(2,1)}), f16[8,64,1664]{2,1,0:T(8,128)(2,1)S(1)}, u32[]{:S(2)}, u32[]{:S(2)}) async-start(f16[8,64,1664]{2,1,0:T(8,128)(2,1)} %bitcast.2), calls=%async_computation.1 | async-start | bytes 3407872 | tf_op jit(solution)/shard_map/all_to_all | solution.py:63
  58.4 5.7 %collective-permute-start.3 = (bf16[32,1536]{1,0:T(8,128)(2,1)S(1)}, bf16[32,1536]{1,0:T(8,128)(2,1)S(1)}, u32[]{:S(2)}, u32[]{:S(2)}) collective-permute-start(bf16[32,1536]{1,0:T(8,128)(2,1)S(1)} %copy-done.2), channel_id=1, source_target_pairs={{0,256},{32,288},{64,320},{96,352},{128,384},{160,416},{192,448},{... | collective-permute-start | bytes 294920 | tf_op jit(solution)/shard_map/ppermute | solution.py:94
  65.7 43.6 %all-to-all-done.1 = f16[8,64,1664]{2,1,0:T(8,128)(2,1)S(1)} async-done(((f16[8,64,1664]{2,1,0:T(8,128)(2,1)}), f16[8,64,1664]{2,1,0:T(8,128)(2,1)S(1)}, u32[]{:S(2)}, u32[]{:S(2)}) %all-to-all-start.1) | async-done | bytes 1703968 | tf_op jit(solution)/shard_map/all_to_all | solution.py:63
  110.0 1.3 collective-permute-start.5
  111.3 38.0 %collective-permute-done.5 = bf16[64,1536]{1,0:T(8,128)(2,1)S(1)} collective-permute-done((bf16[64,1536]{1,0:T(8,128)(2,1)S(1)}, bf16[64,1536]{1,0:T(8,128)(2,1)S(1)}, u32[]{:S(2)}, u32[]{:S(2)}) %collective-permute-start.5) | collective-permute-done | bytes 196640 | tf_op jit(solution)/shard_map/ppermute | solution.py:100
  151.1 8.3 %all-to-all-start.2 = ((bf16[16,64,384]{2,1,0:T(8,128)(2,1)}), bf16[16,64,384]{2,1,0:T(8,128)(2,1)S(1)}, u32[]{:S(2)}, u32[]{:S(2)}) async-start(bf16[16,64,384]{2,1,0:T(8,128)(2,1)} %broadcast_in_dim.26), calls=%async_computation.2 | async-start | bytes 1572864 | tf_op jit(solution)/shard_map/all_to_all | solution.py:35
  160.6 12.4 %all-to-all-done.2 = bf16[16,64,384]{2,1,0:T(8,128)(2,1)S(1)} async-done(((bf16[16,64,384]{2,1,0:T(8,128)(2,1)}), bf16[16,64,384]{2,1,0:T(8,128)(2,1)S(1)}, u32[]{:S(2)}, u32[]{:S(2)}) %all-to-all-start.2) | async-done | bytes 786464 | tf_op jit(solution)/shard_map/all_to_all | solution.py:35
  173.9 39.6 %all-gather.2.cloned.1.call-done = bf16[1024,1536]{1,0:T(8,128)(2,1)} async-done(((bf16[64,1536]{1,0:T(8,128)(2,1)}), bf16[1024,1536]{1,0:T(8,128)(2,1)}) %all-gather.2.cloned.1.call-update) | async-done | bytes 3145744 | tf_op jit(solution)/shard_map/all_gather | solution.py:102
  213.6 4.5 %multiply_reduce_fusion.3 = (f32[384]{0:T(512)}, f32[1536]{0:T(1024)}, f32[]{:T(128)}, f32[384,1536]{1,0:T(8,128)S(1)}) fusion(bf16[1024,384]{1,0:T(8,128)(2,1)} %bitcast.39, bf16[1024,1536]{1,0:T(8,128)(2,1)} %all-gather.2.cloned.1.call-done), kind=kOutput, calls=%fused_computation.7 | convolution fusion | flops 1210316928 | bytes 6299140 | tf_op jit(solution)/shard_map/dot_general | solution.py:29
  218.1 2.0 concatenate.22
  220.8 6.9 %all-to-all-start.3 = ((f32[16,16,128]{2,1,0:T(8,128)}), f32[16,16,128]{2,1,0:T(8,128)}, u32[]{:S(2)}, u32[]{:S(2)}) async-start(f32[16,16,128]{2,1,0:T(8,128)} %broadcast_in_dim.30), calls=%async_computation.3 | async-start | bytes 262144 | tf_op jit(solution)/shard_map/all_to_all | solution.py:35
  228.3 3.7 %convolution_convert_fusion = bf16[1024,384]{1,0:T(8,128)(2,1)S(1)} fusion(bf16[1024,1536]{1,0:T(8,128)(2,1)} %all-gather.2.cloned.1.call-done, bf16[1,384,1536]{2,1,0:T(8,128)(2,1)S(1)} %copy-done), kind=kOutput, calls=%fused_computation.10 | convolution fusion | flops 1208352768 | bytes 5111808 | tf_op jit(solution)/shard_map/dot_general | solution.py:127
  232.2 7.6 %all-to-all-done.3 = f32[16,16,128]{2,1,0:T(8,128)} async-done(((f32[16,16,128]{2,1,0:T(8,128)}), f32[16,16,128]{2,1,0:T(8,128)}, u32[]{:S(2)}, u32[]{:S(2)}) %all-to-all-start.3) | async-done | bytes 131104 | tf_op jit(solution)/shard_map/all_to_all | solution.py:35
  241.3 1.4 fusion.16
  242.7 1.0 pad_maximum_fusion.1
  243.8 18.6 %all-to-all-start.4 = ((bf16[16,80,384]{2,1,0:T(8,128)(2,1)}), bf16[16,80,384]{2,1,0:T(8,128)(2,1)S(1)}, u32[]{:S(2)}, u32[]{:S(2)}) async-start(bf16[16,80,384]{2,1,0:T(8,128)(2,1)} %pad_maximum_fusion.1), calls=%async_computation.4 | async-start | bytes 1966080 | tf_op jit(solution)/shard_map/all_to_all | solution.py:35
  263.1 15.4 %all-to-all-done.4 = bf16[16,80,384]{2,1,0:T(8,128)(2,1)S(1)} async-done(((bf16[16,80,384]{2,1,0:T(8,128)(2,1)}), bf16[16,80,384]{2,1,0:T(8,128)(2,1)S(1)}, u32[]{:S(2)}, u32[]{:S(2)}) %all-to-all-start.4) | async-done | bytes 983072 | tf_op jit(solution)/shard_map/all_to_all | solution.py:35
  279.3 2.2 collective-permute-start.7
  282.2 1.8 multiply_bitcast_fusion
  (62 shorter events, 15.3 us)
Async XLA Ops:
  7.2 33.1 %copy-start = (bf16[1,384,1536]{2,1,0:T(8,128)(2,1)S(1)}, bf16[1,384,1536]{2,1,0:T(8,128)(2,1)}, u32[]{:S(2)}) copy-start(bf16[1,384,1536]{2,1,0:T(8,128)(2,1)} %param.6) | copy-start | bytes 3538948
  8.0 7.4 %collective-permute-start.6 = (bf16[32,384]{1,0:T(8,128)(2,1)S(1)}, bf16[32,384]{1,0:T(8,128)(2,1)S(1)}, u32[]{:S(2)}, u32[]{:S(2)}) collective-permute-start(bf16[32,384]{1,0:T(8,128)(2,1)S(1)} %broadcast_select_fusion.5), channel_id=1, source_target_pairs={{0,256},{256,0},{1,257},{257,1},{2,258},{258,2},{3,259},{259,3},{4... | collective-permute-start | bytes 73736 | tf_op jit(solution)/shard_map/ppermute | solution.py:106
  12.1 3.4 %collective-permute-start = (bf16[32,384]{1,0:T(8,128)(2,1)}, bf16[32,384]{1,0:T(8,128)(2,1)S(1)}, u32[]{:S(2)}, u32[]{:S(2)}) collective-permute-start(bf16[32,384]{1,0:T(8,128)(2,1)} %param.9), channel_id=1, source_target_pairs={{0,256},{32,288},{64,320},{96,352},{128,384},{160,416},{192,448},{... | collective-permute-start | bytes 73736 | tf_op jit(solution)/shard_map/ppermute | solution.py:85
  14.0 2.2 collective-permute-start.1
  14.6 26.6 %collective-permute-start.2 = (bf16[384,1536]{1,0:T(8,128)(2,1)}, bf16[384,1536]{1,0:T(8,128)(2,1)S(1)}, u32[]{:S(2)}, u32[]{:S(2)}) collective-permute-start(bf16[384,1536]{1,0:T(8,128)(2,1)} %bitcast.38), channel_id=1, source_target_pairs={{256,272},{272,256},{288,304},{304,288},{320,336},{336,320},{352,3... | collective-permute-start | bytes 3538952 | tf_op jit(solution)/shard_map/ppermute | solution.py:87
  44.5 13.9 %copy-start.2 = (bf16[32,1536]{1,0:T(8,128)(2,1)S(1)}, bf16[32,1536]{1,0:T(8,128)(2,1)}, u32[]{:S(2)}) copy-start(bf16[32,1536]{1,0:T(8,128)(2,1)} %param.7) | copy-start | bytes 294916
  44.5 64.8 %all-to-all-start.1 = ((f16[8,64,1664]{2,1,0:T(8,128)(2,1)}), f16[8,64,1664]{2,1,0:T(8,128)(2,1)S(1)}, u32[]{:S(2)}, u32[]{:S(2)}) async-start(f16[8,64,1664]{2,1,0:T(8,128)(2,1)} %bitcast.2), calls=%async_computation.1 | async-start | bytes 3407872 | tf_op jit(solution)/shard_map/all_to_all | solution.py:63
  58.3 155.3 %all-gather.2.cloned.1.call-start = ((), (), s32[]{:S(2)}) async-start(), calls=%async_computation.5 | async-start | bytes 3342336 | tf_op jit(solution)/shard_map/all_gather | solution.py:102
  58.4 7.3 %collective-permute-start.3 = (bf16[32,1536]{1,0:T(8,128)(2,1)S(1)}, bf16[32,1536]{1,0:T(8,128)(2,1)S(1)}, u32[]{:S(2)}, u32[]{:S(2)}) collective-permute-start(bf16[32,1536]{1,0:T(8,128)(2,1)S(1)} %copy-done.2), channel_id=1, source_target_pairs={{0,256},{32,288},{64,320},{96,352},{128,384},{160,416},{192,448},{... | collective-permute-start | bytes 294920 | tf_op jit(solution)/shard_map/ppermute | solution.py:94
  64.0 1.6 collective-permute-start.4
  109.8 50.1 %copy-start.5 = (f32[1,384]{1,0:T(1,128)S(1)}, f32[1,384]{1,0:T(1,128)}, u32[]{:S(2)}) copy-start(f32[1,384]{1,0:T(1,128)} %param.10) | copy-start | bytes 4612
  110.0 39.3 %collective-permute-start.5 = (bf16[64,1536]{1,0:T(8,128)(2,1)S(1)}, bf16[64,1536]{1,0:T(8,128)(2,1)S(1)}, u32[]{:S(2)}, u32[]{:S(2)}) collective-permute-start(bf16[64,1536]{1,0:T(8,128)(2,1)S(1)} %fusion.7), channel_id=1, source_target_pairs={{256,0},{257,1},{258,2},{259,3},{260,4},{261,5},{262,6},{263,7},{2... | collective-permute-start | bytes 589832 | tf_op jit(solution)/shard_map/ppermute | solution.py:100
  151.1 21.9 %all-to-all-start.2 = ((bf16[16,64,384]{2,1,0:T(8,128)(2,1)}), bf16[16,64,384]{2,1,0:T(8,128)(2,1)S(1)}, u32[]{:S(2)}, u32[]{:S(2)}) async-start(bf16[16,64,384]{2,1,0:T(8,128)(2,1)} %broadcast_in_dim.26), calls=%async_computation.2 | async-start | bytes 1572864 | tf_op jit(solution)/shard_map/all_to_all | solution.py:35
  220.8 19.0 %all-to-all-start.3 = ((f32[16,16,128]{2,1,0:T(8,128)}), f32[16,16,128]{2,1,0:T(8,128)}, u32[]{:S(2)}, u32[]{:S(2)}) async-start(f32[16,16,128]{2,1,0:T(8,128)} %broadcast_in_dim.30), calls=%async_computation.3 | async-start | bytes 262144 | tf_op jit(solution)/shard_map/all_to_all | solution.py:35
  228.3 13.0 %copy-start.4 = (f32[384]{0:T(512)S(1)}, f32[384]{0:T(512)}, u32[]{:S(2)}) copy-start(f32[384]{0:T(512)} %get-tuple-element.2) | copy-start | bytes 4612
  228.3 13.0 %copy-start.6 = (pred[16]{0:T(512)(128)(4,1)S(1)}, pred[16]{0:T(512)(128)(4,1)}, u32[]{:S(2)}) copy-start(pred[16]{0:T(512)(128)(4,1)} %get-tuple-element.19) | copy-start | bytes 52
  228.3 13.0 %copy-start.7 = (pred[16]{0:T(512)(128)(4,1)S(1)}, pred[16]{0:T(512)(128)(4,1)}, u32[]{:S(2)}) copy-start(pred[16]{0:T(512)(128)(4,1)} %get-tuple-element.20) | copy-start | bytes 52
  232.2 30.9 %copy-start.3 = (f32[1,1536]{1,0:T(1,128)S(1)}, f32[1,1536]{1,0:T(1,128)}, u32[]{:S(2)}) copy-start(f32[1,1536]{1,0:T(1,128)} %param.11) | copy-start | bytes 18436
  243.8 34.8 %all-to-all-start.4 = ((bf16[16,80,384]{2,1,0:T(8,128)(2,1)}), bf16[16,80,384]{2,1,0:T(8,128)(2,1)S(1)}, u32[]{:S(2)}, u32[]{:S(2)}) async-start(bf16[16,80,384]{2,1,0:T(8,128)(2,1)} %pad_maximum_fusion.1), calls=%async_computation.4 | async-start | bytes 1966080 | tf_op jit(solution)/shard_map/all_to_all | solution.py:35
  279.3 4.7 %collective-permute-start.7 = (f32[32,384]{1,0:T(8,128)S(1)}, f32[32,384]{1,0:T(8,128)S(1)}, u32[]{:S(2)}, u32[]{:S(2)}) collective-permute-start(f32[32,384]{1,0:T(8,128)S(1)} %slice.51), channel_id=1, source_target_pairs={{0,256},{1,257},{2,258},{3,259},{4,260},{5,261},{6,262},{7,263},{8... | collective-permute-start | bytes 147464 | tf_op jit(solution)/shard_map/ppermute | solution.py:138
  282.2 1.8 copy-start.1
Sparse Core Ops, SparseCore 0:
  150.2 63.3 all-gather.1

commit v4 on v2

--- a/solution.py
+++ b/solution.py
@@ -53,40 +53,82 @@
     return out.astype(jnp.bfloat16)
 
 
+def sum_blocks(partial, axis, groups):
+    members = len(groups[0])
+    columns = partial.shape[1]
+    rows = partial.shape[0] // members
+    power = jnp.clip(jnp.ceil(jnp.log2(jnp.maximum(jnp.max(jnp.abs(partial)), 1e-30))), -96.0, 96.0)
+    coded = (partial * jnp.exp2(14.0 - power)).astype(jnp.float16).reshape(members, rows, columns)
+    power = jnp.broadcast_to(power, (members, 8, columns)).astype(jnp.float16)
+    taken = lax.all_to_all(
+        jnp.concatenate([coded, power], axis=1),
+        axis,
+        split_axis=0,
+        concat_axis=0,
+        axis_index_groups=groups,
+        tiled=True,
+    )
+    power = jnp.max(taken[:, rows:, :LANES].astype(jnp.float32), axis=(1, 2), keepdims=True)
+    return jnp.sum(taken[:, :rows].astype(jnp.float32) * jnp.exp2(power - 14.0), axis=0)
+
+
 def shards(weights, preact, inputs, grad_out, row_state, col_state):
     hid = lax.axis_size("hid")
     wid = lax.axis_size("wid")
     own_tile = weights[0]
     features, hidden = own_tile.shape
+    half = hidden // 2
     rows = grad_out.shape[0]
     first = lax.axis_index("section") == 0
     even = lax.axis_index("hid") % 2 == 0
+    home = lax.axis_index("section") == lax.axis_index("hid") % 2
     pair = ("section", "hid")
-    evens = range(0, hid, 2)
-    down = [(h, hid + h) for h in evens]
-    across = [(h + 1, hid + h) for h in evens] + [(hid + h, hid + h + 1) for h in evens]
-    swap = [(hid + h, hid + (h ^ 1)) for h in range(hid)]
+
+    def at(section, h):
+        return section * hid + h
+
+    over = [(at(h % 2, h), at(1 - h % 2, h)) for h in range(hid)]
+    beside = [(at(h % 2, h ^ 1), at(h % 2, h)) for h in range(hid)]
+    across = [(at(h % 2, h ^ 1), at(1 - h % 2, h)) for h in range(hid)]
     rings = [list(range(p, hid, 2)) for p in range(2)]
 
-    grad_down = lax.ppermute(grad_out, pair, down)
-    grad_across = lax.ppermute(grad_out, pair, across)
-    next_tile = lax.ppermute(own_tile, pair, swap)
-    grad_pair = jnp.concatenate([jnp.where(even, grad_down, grad_out), grad_across], axis=1)
+    def token_blocks(same, other):
+        own = jnp.where(home, same, lax.ppermute(other, pair, over))
+        near = lax.ppermute(same, pair, beside)
+        far = lax.ppermute(other, pair, across)
+        return own, jnp.where(home, near, far)
+
+    grad_pair = jnp.concatenate(token_blocks(grad_out, grad_out), axis=1)
+    tile_near = lax.ppermute(own_tile[:, :half], pair, [(at(1, h), at(1, h ^ 1)) for h in range(hid)])
+    tile_over = lax.ppermute(own_tile[:, half:], pair, [(at(1, h), at(0, h)) for h in range(hid)])
+    tile_far = lax.ppermute(own_tile[:, half:], pair, [(at(1, h), at(0, h ^ 1)) for h in range(hid)])
     grad_half = spread(grad_pair, "wid")
+    pre_own, pre_next = token_blocks(
+        jnp.where(first, preact[:, half:], preact[:, :half]),
+        jnp.where(first, preact[:, :half], preact[:, half:]),
+    )
+    grad_half, pre_own, pre_next = lax.optimization_barrier((grad_half, pre_own, pre_next))
     hidden_part = jnp.dot(
-        grad_half[:, :features], own_tile, preferred_element_type=jnp.float32
-    ) + jnp.dot(grad_half[:, features:], next_tile, preferred_element_type=jnp.float32)
-    hidden_share = lax.psum_scatter(
-        hidden_part, "hid", scatter_dimension=0, axis_index_groups=rings, tiled=True
+        grad_half[:, :features],
+        jnp.where(first, tile_over, own_tile[:, :half]),
+        preferred_element_type=jnp.float32,
+    ) + jnp.dot(
+        grad_half[:, features:],
+        jnp.where(first, tile_far, tile_near),
+        preferred_element_type=jnp.float32,
     )
-    pre_down = lax.ppermute(preact, pair, down)
-    pre_across = lax.ppermute(preact, pair, across)
-    pre_pair = jnp.concatenate(
-        [jnp.where(even, pre_down, pre_across), jnp.where(even, pre_across, preact)]
-    ).astype(jnp.float32)
-    pre_share = (hidden_share * gelu_slope(pre_pair)).astype(jnp.bfloat16)
-    pre_share = lax.ppermute(pre_share, "section", [(1, 0)])
-    act_share = gelu_value(pre_pair).astype(jnp.bfloat16)
+    hidden_share = sum_blocks(hidden_part, "hid", rings)
+    pre_half = jnp.concatenate(
+        [jnp.where(even, pre_own, pre_next), jnp.where(even, pre_next, pre_own)]
+    )
+    pre_taken = lax.ppermute(pre_half, "section", [(0, 1)])
+    act_share = gelu_value(
+        jnp.concatenate([pre_half, pre_taken], axis=1).astype(jnp.float32)
+    ).astype(jnp.bfloat16)
+    pre_share = (hidden_share * gelu_slope(pre_half.astype(jnp.float32))).astype(jnp.bfloat16)
+    pre_share = jnp.concatenate(
+        [lax.ppermute(pre_share, "section", [(1, 0)]), pre_share], axis=1
+    )
     right = lax.all_gather(jnp.where(first, pre_share, act_share), "hid", axis=0, tiled=True)
 
     kept = jnp.where(first, inputs, grad_out)

time: 287 us -> 274 us (0.955)
  starting transfers between devices: 50.8 us -> 87.3 us
  waiting for transfers between devices: 166 us -> 139 us
  blocking collectives: 24 us -> 0 us
    reduce_scatter x1 -> x0, waiting for transfers between devices: 81.1 us -> none  [shards(): lax.psum_scatter(hidden_part, 'hid', scatter_dimension=0, axis_index_grou...]
    all_to_all x0 -> x1, waiting for transfers between devices: none -> 29.3 us  [sum_blocks(): lax.all_to_all(jnp.concatenate([coded, power], axis=1), axis, split_axis=...]
    all_to_all x1 -> x0, blocking collectives: 24 us -> none  [exchange(): return lax.all_to_all(blocks, axis, split_axis=0, concat_axis=0, tiled=True)]
    all_to_all x0 -> x1, starting transfers between devices: none -> 13.7 us  [sum_blocks(): lax.all_to_all(jnp.concatenate([coded, power], axis=1), axis, split_axis=...]
    ppermute x6 -> x11, waiting for transfers between devices: 7.14 us -> 20.4 us  [the longest x2 6.68 us: token_blocks(): near = lax.ppermute(same, pair, beside)]
    ppermute x6 -> x11, starting transfers between devices: 10.6 us -> 21.8 us  [the longest x2 11.1 us: token_blocks(): own = jnp.where(home, same, lax.ppermute(other, pair, over))]
    all_gather x1, waiting for transfers between devices: 41.9 us -> 53 us  [shards(): lax.all_gather(jnp.where(first, pre_share, act_share), 'hid', axis=0, til...]
    all_to_all x3 -> x4, starting transfers between devices: 33.8 us -> 43.1 us  [exchange(): return lax.all_to_all(blocks, axis, split_axis=0, concat_axis=0, tiled=True)]
  transfers between devices with their start and end apart: 13 -> 19, of which waited for: 7 -> 9; matrix products, arithmetic and copies ran while one was open for 4% -> 5% of each run, Pallas kernels for 0% -> 0%
where the time goes in v4:
time: 274 us; the launch traced here: 273 us
  waiting for transfers between devices  139 us (51%)
  starting transfers between devices  87.3 us (32%)
  between operations  16.5 us (6%)
  matrix products  13 us (5%)
  other arithmetic  9.81 us (4%)
  local copies, waits for them, and re-layouts  7.24 us (3%)
    all_gather x1, waiting for transfers between devices, shards(): lax.all_gather(jnp.where(first, pre_share, act_share), 'hid', axis=0, til...  53 us
    all_to_all x4, starting transfers between devices, exchange(): return lax.all_to_all(blocks, axis, split_axis=0, concat_axis=0, tiled=True)  43.1 us
    all_to_all x4, waiting for transfers between devices, exchange(): return lax.all_to_all(blocks, axis, split_axis=0, concat_axis=0, tiled=True)  36.5 us
    all_to_all x1, waiting for transfers between devices, sum_blocks(): lax.all_to_all(jnp.concatenate([coded, power], axis=1), axis, split_axis=...  29.3 us
    all_to_all x1, starting transfers between devices, sum_blocks(): lax.all_to_all(jnp.concatenate([coded, power], axis=1), axis, split_axis=...  13.7 us
    ppermute x2, starting transfers between devices, token_blocks(): own = jnp.where(home, same, lax.ppermute(other, pair, over))  11.1 us
    ppermute x2, waiting for transfers between devices, token_blocks(): near = lax.ppermute(same, pair, beside)  6.68 us
    ppermute x1, starting transfers between devices, shards(): taken = lax.ppermute(given, 'section', [(0, 1), (1, 0)])  6.41 us
  transfers between devices with their start and end apart: 19, of which 9 were waited for; matrix products, arithmetic and copies ran while one was open for 5% of the time, Pallas kernels for 0%

profile of v4, /device:TPU:1, one launch (start us, length us, event | category | flops | bytes accessed | tf_op | source)
XLA Modules:
  0.0 273.0 jit_solution(15380726887972053118)
XLA Ops:
  7.2 4.2 %collective-permute-start = (bf16[32,384]{1,0:T(8,128)(2,1)}, bf16[32,384]{1,0:T(8,128)(2,1)S(1)}, u32[]{:S(2)}, u32[]{:S(2)}) collective-permute-start(bf16[32,384]{1,0:T(8,128)(2,1)} %param.9), channel_id=1, source_target_pairs={{0,256},{272,16},{32,288},{304,48},{64,320},{336,80},{96,352},{368... | collective-permute-start | bytes 73736 | tf_op jit(solution)/shard_map/ppermute | solution.py:96
  14.1 6.4 %collective-permute-start.11 = (bf16[32,384]{1,0:T(8,128)(2,1)S(1)}, bf16[32,384]{1,0:T(8,128)(2,1)S(1)}, u32[]{:S(2)}, u32[]{:S(2)}) collective-permute-start(bf16[32,384]{1,0:T(8,128)(2,1)S(1)} %broadcast_select_fusion.10), channel_id=1, source_target_pairs={{0,256},{256,0},{1,257},{257,1},{2,258},{258,2},{3,259},{259,3},{4... | collective-permute-start | bytes 73736 | tf_op jit(solution)/shard_map/ppermute | solution.py:136
  23.3 1.5 collective-permute-start.8
  26.4 8.4 %all-to-all-start = ((bf16[16,32,768]{2,1,0:T(8,128)(2,1)}), bf16[16,32,768]{2,1,0:T(8,128)(2,1)S(1)}, u32[]{:S(2)}, u32[]{:S(2)}) async-start(bf16[16,32,768]{2,1,0:T(8,128)(2,1)} %broadcast_in_dim.22), calls=%async_computation | async-start | bytes 1572864 | tf_op jit(solution)/shard_map/all_to_all | solution.py:35
  34.9 7.0 %collective-permute-start.3 = (bf16[32,768]{1,0:T(8,128)(2,1)S(1)}, bf16[32,768]{1,0:T(8,128)(2,1)S(1)}, u32[]{:S(2)}, u32[]{:S(2)}) collective-permute-start(bf16[32,768]{1,0:T(8,128)(2,1)S(1)} %broadcast_select_fusion.2), channel_id=1, source_target_pairs={{0,256},{272,16},{32,288},{304,48},{64,320},{336,80},{96,352},{368... | collective-permute-start | bytes 147464 | tf_op jit(solution)/shard_map/ppermute | solution.py:96
  43.9 3.7 %collective-permute-done.3 = bf16[32,768]{1,0:T(8,128)(2,1)S(1)} collective-permute-done((bf16[32,768]{1,0:T(8,128)(2,1)S(1)}, bf16[32,768]{1,0:T(8,128)(2,1)S(1)}, u32[]{:S(2)}, u32[]{:S(2)}) %collective-permute-start.3) | collective-permute-done | bytes 49184 | tf_op jit(solution)/shard_map/ppermute | solution.py:96
  49.5 6.7 %collective-permute-done.4 = bf16[32,768]{1,0:T(8,128)(2,1)S(1)} collective-permute-done((bf16[32,768]{1,0:T(8,128)(2,1)S(1)}, bf16[32,768]{1,0:T(8,128)(2,1)S(1)}, u32[]{:S(2)}, u32[]{:S(2)}) %collective-permute-start.4) | collective-permute-done | bytes 49184 | tf_op jit(solution)/shard_map/ppermute | solution.py:97
  56.8 1.6 fusion
  58.4 6.0 %collective-permute-done.6 = bf16[384,768]{1,0:T(8,128)(2,1)} collective-permute-done((bf16[384,768]{1,0:T(8,128)(2,1)S(1)}, bf16[384,768]{1,0:T(8,128)(2,1)}, u32[]{:S(2)}, u32[]{:S(2)}) %collective-permute-start.6) | collective-permute-done | bytes 589856 | tf_op jit(solution)/shard_map/ppermute | solution.py:103
  64.4 2.3 abs_reduce_fusion
  68.6 13.7 %all-to-all-start.1 = ((f16[8,72,768]{2,1,0:T(8,128)(2,1)}), f16[8,72,768]{2,1,0:T(8,128)(2,1)S(1)}, u32[]{:S(2)}, u32[]{:S(2)}) async-start(f16[8,72,768]{2,1,0:T(8,128)(2,1)} %concatenate.25), calls=%async_computation.1 | async-start | bytes 1769472 | tf_op jit(solution)/shard_map/all_to_all | solution.py:63
  83.7 29.3 %all-to-all-done.1 = f16[8,72,768]{2,1,0:T(8,128)(2,1)S(1)} async-done(((f16[8,72,768]{2,1,0:T(8,128)(2,1)}), f16[8,72,768]{2,1,0:T(8,128)(2,1)S(1)}, u32[]{:S(2)}, u32[]{:S(2)}) %all-to-all-start.1) | async-done | bytes 884768 | tf_op jit(solution)/shard_map/all_to_all | solution.py:63
  114.8 4.1 %collective-permute-done.9 = bf16[64,768]{1,0:T(8,128)(2,1)S(1)} collective-permute-done((bf16[64,768]{1,0:T(8,128)(2,1)S(1)}, bf16[64,768]{1,0:T(8,128)(2,1)S(1)}, u32[]{:S(2)}, u32[]{:S(2)}) %collective-permute-start.9) | collective-permute-done | bytes 98336 | tf_op jit(solution)/shard_map/ppermute | solution.py:130
  120.7 9.0 %all-to-all-start.2 = ((bf16[16,64,384]{2,1,0:T(8,128)(2,1)}), bf16[16,64,384]{2,1,0:T(8,128)(2,1)S(1)}, u32[]{:S(2)}, u32[]{:S(2)}) async-start(bf16[16,64,384]{2,1,0:T(8,128)(2,1)} %broadcast_in_dim.23), calls=%async_computation.2 | async-start | bytes 1572864 | tf_op jit(solution)/shard_map/all_to_all | solution.py:35
  130.4 12.9 %all-to-all-done.2 = bf16[16,64,384]{2,1,0:T(8,128)(2,1)S(1)} async-done(((bf16[16,64,384]{2,1,0:T(8,128)(2,1)}), bf16[16,64,384]{2,1,0:T(8,128)(2,1)S(1)}, u32[]{:S(2)}, u32[]{:S(2)}) %all-to-all-start.2) | async-done | bytes 786464 | tf_op jit(solution)/shard_map/all_to_all | solution.py:35
  143.4 53.0 %all-gather.2.cloned.1.call-done = bf16[1024,1536]{1,0:T(8,128)(2,1)} async-done(((bf16[64,1536]{1,0:T(8,128)(2,1)}), bf16[1024,1536]{1,0:T(8,128)(2,1)}) %all-gather.2.cloned.1.call-update) | async-done | bytes 3145744 | tf_op jit(solution)/shard_map/all_gather | solution.py:132
  196.4 5.4 %multiply_reduce_fusion.2 = (f32[384]{0:T(512)S(1)}, f32[1536]{0:T(1024)S(1)}, f32[]{:T(128)}, f32[384,1536]{1,0:T(8,128)}) fusion(bf16[1024,384]{1,0:T(8,128)(2,1)S(1)} %bitcast.38, bf16[1024,1536]{1,0:T(8,128)(2,1)} %all-gather.2.cloned.1.call-done), kind=kOutput, calls=%fused_computation.3 | convolution fusion | flops 1210316928 | bytes 6299140 | tf_op jit(solution)/shard_map/dot_general | solution.py:29
  203.8 7.0 %all-to-all-start.3 = ((f32[16,16,128]{2,1,0:T(8,128)}), f32[16,16,128]{2,1,0:T(8,128)S(1)}, u32[]{:S(2)}, u32[]{:S(2)}) async-start(f32[16,16,128]{2,1,0:T(8,128)} %broadcast_in_dim.27), calls=%async_computation.3 | async-start | bytes 262144 | tf_op jit(solution)/shard_map/all_to_all | solution.py:35
  210.9 3.7 %convolution_convert_fusion = bf16[1024,384]{1,0:T(8,128)(2,1)S(1)} fusion(bf16[1024,1536]{1,0:T(8,128)(2,1)} %all-gather.2.cloned.1.call-done, bf16[1,384,1536]{2,1,0:T(8,128)(2,1)S(1)} %copy-done), kind=kOutput, calls=%fused_computation.9 | convolution fusion | flops 1208352768 | bytes 5111808 | tf_op jit(solution)/shard_map/dot_general | solution.py:157
  214.7 8.1 %all-to-all-done.3 = f32[16,16,128]{2,1,0:T(8,128)S(1)} async-done(((f32[16,16,128]{2,1,0:T(8,128)}), f32[16,16,128]{2,1,0:T(8,128)S(1)}, u32[]{:S(2)}, u32[]{:S(2)}) %all-to-all-start.3) | async-done | bytes 131104 | tf_op jit(solution)/shard_map/all_to_all | solution.py:35
  225.2 18.7 %all-to-all-start.4 = ((bf16[16,80,384]{2,1,0:T(8,128)(2,1)}), bf16[16,80,384]{2,1,0:T(8,128)(2,1)S(1)}, u32[]{:S(2)}, u32[]{:S(2)}) async-start(bf16[16,80,384]{2,1,0:T(8,128)(2,1)} %pad_maximum_fusion), calls=%async_computation.4 | async-start | bytes 1966080 | tf_op jit(solution)/shard_map/all_to_all | solution.py:35
  244.6 15.4 %all-to-all-done.4 = bf16[16,80,384]{2,1,0:T(8,128)(2,1)S(1)} async-done(((bf16[16,80,384]{2,1,0:T(8,128)(2,1)}), bf16[16,80,384]{2,1,0:T(8,128)(2,1)S(1)}, u32[]{:S(2)}, u32[]{:S(2)}) %all-to-all-start.4) | async-done | bytes 983072 | tf_op jit(solution)/shard_map/all_to_all | solution.py:35
  260.8 2.2 collective-permute-start.12
  263.7 1.8 multiply_bitcast_fusion
  (85 shorter events, 24.5 us)
Async XLA Ops:
  7.2 17.6 %collective-permute-start = (bf16[32,384]{1,0:T(8,128)(2,1)}, bf16[32,384]{1,0:T(8,128)(2,1)S(1)}, u32[]{:S(2)}, u32[]{:S(2)}) collective-permute-start(bf16[32,384]{1,0:T(8,128)(2,1)} %param.9), channel_id=1, source_target_pairs={{0,256},{272,16},{32,288},{304,48},{64,320},{336,80},{96,352},{368... | collective-permute-start | bytes 73736 | tf_op jit(solution)/shard_map/ppermute | solution.py:96
  11.3 14.1 %collective-permute-start.1 = (bf16[32,384]{1,0:T(8,128)(2,1)}, bf16[32,384]{1,0:T(8,128)(2,1)S(1)}, u32[]{:S(2)}, u32[]{:S(2)}) collective-permute-start(bf16[32,384]{1,0:T(8,128)(2,1)} %param.9), channel_id=1, source_target_pairs={{16,0},{256,272},{48,32},{288,304},{80,64},{320,336},{112,96},{352... | collective-permute-start | bytes 73736 | tf_op jit(solution)/shard_map/ppermute | solution.py:97
  12.6 12.8 %collective-permute-start.2 = (bf16[32,384]{1,0:T(8,128)(2,1)}, bf16[32,384]{1,0:T(8,128)(2,1)S(1)}, u32[]{:S(2)}, u32[]{:S(2)}) collective-permute-start(bf16[32,384]{1,0:T(8,128)(2,1)} %param.9), channel_id=1, source_target_pairs={{16,256},{256,16},{48,288},{288,48},{80,320},{320,80},{112,352},{3... | collective-permute-start | bytes 73736 | tf_op jit(solution)/shard_map/ppermute | solution.py:98
  14.1 9.2 %collective-permute-start.11 = (bf16[32,384]{1,0:T(8,128)(2,1)S(1)}, bf16[32,384]{1,0:T(8,128)(2,1)S(1)}, u32[]{:S(2)}, u32[]{:S(2)}) collective-permute-start(bf16[32,384]{1,0:T(8,128)(2,1)S(1)} %broadcast_select_fusion.10), channel_id=1, source_target_pairs={{0,256},{256,0},{1,257},{257,1},{2,258},{258,2},{3,259},{259,3},{4... | collective-permute-start | bytes 73736 | tf_op jit(solution)/shard_map/ppermute | solution.py:136
  21.8 35.0 %collective-permute-start.7 = (bf16[384,768]{1,0:T(8,128)(2,1)S(1)}, bf16[384,768]{1,0:T(8,128)(2,1)}, u32[]{:S(2)}, u32[]{:S(2)}) collective-permute-start(bf16[384,768]{1,0:T(8,128)(2,1)S(1)} %get-tuple-element.16), channel_id=1, source_target_pairs={{256,16},{272,0},{288,48},{304,32},{320,80},{336,64},{352,112},{36... | collective-permute-start | bytes 1769480 | tf_op jit(solution)/shard_map/ppermute | solution.py:104
  23.3 33.5 %collective-permute-start.8 = (bf16[384,768]{1,0:T(8,128)(2,1)S(1)}, bf16[384,768]{1,0:T(8,128)(2,1)}, u32[]{:S(2)}, u32[]{:S(2)}) collective-permute-start(bf16[384,768]{1,0:T(8,128)(2,1)S(1)} %get-tuple-element.15), channel_id=1, source_target_pairs={{256,272},{272,256},{288,304},{304,288},{320,336},{336,320},{352,3... | collective-permute-start | bytes 1769480 | tf_op jit(solution)/shard_map/ppermute | solution.py:102
  26.4 30.4 %all-to-all-start = ((bf16[16,32,768]{2,1,0:T(8,128)(2,1)}), bf16[16,32,768]{2,1,0:T(8,128)(2,1)S(1)}, u32[]{:S(2)}, u32[]{:S(2)}) async-start(bf16[16,32,768]{2,1,0:T(8,128)(2,1)} %broadcast_in_dim.22), calls=%async_computation | async-start | bytes 1572864 | tf_op jit(solution)/shard_map/all_to_all | solution.py:35
  34.9 29.5 %copy-start = (bf16[1,384,1536]{2,1,0:T(8,128)(2,1)S(1)}, bf16[1,384,1536]{2,1,0:T(8,128)(2,1)}, u32[]{:S(2)}) copy-start(bf16[1,384,1536]{2,1,0:T(8,128)(2,1)} %param.6) | copy-start | bytes 3538948
  34.9 12.6 %collective-permute-start.3 = (bf16[32,768]{1,0:T(8,128)(2,1)S(1)}, bf16[32,768]{1,0:T(8,128)(2,1)S(1)}, u32[]{:S(2)}, u32[]{:S(2)}) collective-permute-start(bf16[32,768]{1,0:T(8,128)(2,1)S(1)} %broadcast_select_fusion.2), channel_id=1, source_target_pairs={{0,256},{272,16},{32,288},{304,48},{64,320},{336,80},{96,352},{368... | collective-permute-start | bytes 147464 | tf_op jit(solution)/shard_map/ppermute | solution.py:96
  41.9 7.6 %collective-permute-start.5 = (bf16[32,768]{1,0:T(8,128)(2,1)S(1)}, bf16[32,768]{1,0:T(8,128)(2,1)S(1)}, u32[]{:S(2)}, u32[]{:S(2)}) collective-permute-start(bf16[32,768]{1,0:T(8,128)(2,1)S(1)} %broadcast_select_fusion.2), channel_id=1, source_target_pairs={{16,256},{256,16},{48,288},{288,48},{80,320},{320,80},{112,352},{3... | collective-permute-start | bytes 147464 | tf_op jit(solution)/shard_map/ppermute | solution.py:98
  42.6 21.8 %collective-permute-start.6 = (bf16[384,768]{1,0:T(8,128)(2,1)S(1)}, bf16[384,768]{1,0:T(8,128)(2,1)}, u32[]{:S(2)}, u32[]{:S(2)}) collective-permute-start(bf16[384,768]{1,0:T(8,128)(2,1)S(1)} %get-tuple-element.16), channel_id=1, source_target_pairs={{256,0},{272,16},{288,32},{304,48},{320,64},{336,80},{352,96},{368... | collective-permute-start | bytes 1769480 | tf_op jit(solution)/shard_map/ppermute | solution.py:103
  48.2 8.0 %collective-permute-start.4 = (bf16[32,768]{1,0:T(8,128)(2,1)S(1)}, bf16[32,768]{1,0:T(8,128)(2,1)S(1)}, u32[]{:S(2)}, u32[]{:S(2)}) collective-permute-start(bf16[32,768]{1,0:T(8,128)(2,1)S(1)} %get-tuple-element.14), channel_id=1, source_target_pairs={{16,0},{256,272},{48,32},{288,304},{80,64},{320,336},{112,96},{352... | collective-permute-start | bytes 147464 | tf_op jit(solution)/shard_map/ppermute | solution.py:97
  68.6 51.1 %copy-start.8 = (bf16[32,384]{1,0:T(8,128)(2,1)S(1)}, bf16[32,384]{1,0:T(8,128)(2,1)}, u32[]{:S(2)}) copy-start(bf16[32,384]{1,0:T(8,128)(2,1)} %get-tuple-element.19) | copy-start | bytes 73732
  68.6 51.1 %copy-start.9 = (bf16[32,384]{1,0:T(8,128)(2,1)S(1)}, bf16[32,384]{1,0:T(8,128)(2,1)}, u32[]{:S(2)}) copy-start(bf16[32,384]{1,0:T(8,128)(2,1)} %get-tuple-element.20) | copy-start | bytes 73732
  68.6 44.4 %all-to-all-start.1 = ((f16[8,72,768]{2,1,0:T(8,128)(2,1)}), f16[8,72,768]{2,1,0:T(8,128)(2,1)S(1)}, u32[]{:S(2)}, u32[]{:S(2)}) async-start(f16[8,72,768]{2,1,0:T(8,128)(2,1)} %concatenate.25), calls=%async_computation.1 | async-start | bytes 1769472 | tf_op jit(solution)/shard_map/all_to_all | solution.py:63
  82.3 114.1 %all-gather.2.cloned.1.call-start = ((), (), s32[]{:S(2)}) async-start(), calls=%async_computation.5 | async-start | bytes 3342336 | tf_op jit(solution)/shard_map/all_gather | solution.py:132
  82.4 32.4 %collective-permute-start.10 = (bf16[64,768]{1,0:T(8,128)(2,1)S(1)}, bf16[64,768]{1,0:T(8,128)(2,1)S(1)}, u32[]{:S(2)}, u32[]{:S(2)}) collective-permute-start(bf16[64,768]{1,0:T(8,128)(2,1)S(1)} %pad_maximum_fusion.1), channel_id=1, source_target_pairs={{0,256},{1,257},{2,258},{3,259},{4,260},{5,261},{6,262},{7,263},{8... | collective-permute-start | bytes 294920 | tf_op jit(solution)/shard_map/ppermute | solution.py:124
  113.5 5.4 %collective-permute-start.9 = (bf16[64,768]{1,0:T(8,128)(2,1)S(1)}, bf16[64,768]{1,0:T(8,128)(2,1)S(1)}, u32[]{:S(2)}, u32[]{:S(2)}) collective-permute-start(bf16[64,768]{1,0:T(8,128)(2,1)S(1)} %fusion.19), channel_id=1, source_target_pairs={{256,0},{257,1},{258,2},{259,3},{260,4},{261,5},{262,6},{263,7},{2... | collective-permute-start | bytes 294920 | tf_op jit(solution)/shard_map/ppermute | solution.py:130
  120.7 22.6 %all-to-all-start.2 = ((bf16[16,64,384]{2,1,0:T(8,128)(2,1)}), bf16[16,64,384]{2,1,0:T(8,128)(2,1)S(1)}, u32[]{:S(2)}, u32[]{:S(2)}) async-start(bf16[16,64,384]{2,1,0:T(8,128)(2,1)} %broadcast_in_dim.23), calls=%async_computation.2 | async-start | bytes 1572864 | tf_op jit(solution)/shard_map/all_to_all | solution.py:35
  203.8 19.0 %all-to-all-start.3 = ((f32[16,16,128]{2,1,0:T(8,128)}), f32[16,16,128]{2,1,0:T(8,128)S(1)}, u32[]{:S(2)}, u32[]{:S(2)}) async-start(f32[16,16,128]{2,1,0:T(8,128)} %broadcast_in_dim.27), calls=%async_computation.3 | async-start | bytes 262144 | tf_op jit(solution)/shard_map/all_to_all | solution.py:35
  224.1 20.4 %copy-start.10 = (f32[1,1536]{1,0:T(1,128)S(1)}, f32[1,1536]{1,0:T(1,128)}, u32[]{:S(2)}) copy-start(f32[1,1536]{1,0:T(1,128)} %param.11) | copy-start | bytes 18436
  225.2 38.5 %copy-start.1 = (f32[384,1536]{1,0:T(8,128)S(1)}, f32[384,1536]{1,0:T(8,128)}, u32[]{:S(2)}) copy-start(f32[384,1536]{1,0:T(8,128)} %get-tuple-element.26) | copy-start | bytes 7077892
  225.2 34.8 %all-to-all-start.4 = ((bf16[16,80,384]{2,1,0:T(8,128)(2,1)}), bf16[16,80,384]{2,1,0:T(8,128)(2,1)S(1)}, u32[]{:S(2)}, u32[]{:S(2)}) async-start(bf16[16,80,384]{2,1,0:T(8,128)(2,1)} %pad_maximum_fusion), calls=%async_computation.4 | async-start | bytes 1966080 | tf_op jit(solution)/shard_map/all_to_all | solution.py:35
  260.8 4.7 %collective-permute-start.12 = (f32[32,384]{1,0:T(8,128)S(1)}, f32[32,384]{1,0:T(8,128)S(1)}, u32[]{:S(2)}, u32[]{:S(2)}) collective-permute-start(f32[32,384]{1,0:T(8,128)S(1)} %slice.71), channel_id=1, source_target_pairs={{0,256},{1,257},{2,258},{3,259},{4,260},{5,261},{6,262},{7,263},{8... | collective-permute-start | bytes 147464 | tf_op jit(solution)/shard_map/ppermute | solution.py:168
  (7 other events, 96.1 us)
Sparse Core Ops, SparseCore 0:
  119.8 76.5 all-gather.1

commit v5 on v4

v5 whole, which is shorter than its diff:
```python
import jax
import jax.numpy as jnp
from jax import lax
from jax.experimental.layout import Layout, with_layout_constraint
from jax.sharding import PartitionSpec as P


D = 6144
FF = 24576


decay_rate = 0.9
root_half = 0.7071067811865476
inv_root_tau = 0.3989422804014327
LANES = 128


def normal_cdf(pre):
    return 0.5 * (1.0 + lax.erf(pre * root_half))


def gelu_value(pre):
    return pre * normal_cdf(pre)


def gelu_slope(pre):
    return normal_cdf(pre) + pre * jnp.exp(-0.5 * pre * pre) * inv_root_tau


def by_rows(block):
    return with_layout_constraint(block, Layout(major_to_minor=(0, 1)))


def contract(left, right):
    return lax.dot_general(
        left, right, (((0,), (0,)), ((), ())), preferred_element_type=jnp.float32
    )


def exchange(blocks, axis):
    return lax.all_to_all(blocks, axis, split_axis=0, concat_axis=0, tiled=True)


def spread(block, axis):
    n = lax.axis_size(axis)
    copies = jnp.broadcast_to(block[None], (n,) + block.shape)
    return exchange(copies.reshape((n * block.shape[0],) + block.shape[1:]), axis)


def thirds(values, scalar):
    shape = (8, 2 * values.shape[0])
    row = lax.broadcasted_iota(jnp.int32, shape, 0)
    rest = jnp.concatenate([values, jnp.broadcast_to(scalar, values.shape)])
    rest = jnp.broadcast_to(rest[None], shape)
    out = jnp.zeros(shape, jnp.float32)
    for k in range(3):
        term = lax.reduce_precision(rest, exponent_bits=8, mantissa_bits=7)
        out = jnp.where(row == k, term, out)
        rest = rest - term
    return out.astype(jnp.bfloat16)


def sum_blocks(partial, axis, groups):
    members = len(groups[0])
    columns = partial.shape[1]
    rows = partial.shape[0] // members
    power = jnp.clip(jnp.ceil(jnp.log2(jnp.maximum(jnp.max(jnp.abs(partial)), 1e-30))), -96.0, 96.0)
    coded = (partial * jnp.exp2(14.0 - power)).astype(jnp.float16).reshape(members, rows, columns)
    power = jnp.broadcast_to(power, (members, 8, columns)).astype(jnp.float16)
    taken = lax.all_to_all(
        jnp.concatenate([coded, power], axis=1),
        axis,
        split_axis=0,
        concat_axis=0,
        axis_index_groups=groups,
        tiled=True,
    )
    power = jnp.max(taken[:, rows:, :LANES].astype(jnp.float32), axis=(1, 2), keepdims=True)
    return jnp.sum(taken[:, :rows].astype(jnp.float32) * jnp.exp2(power - 14.0), axis=0)


def shards(weights, preact, inputs, grad_out, row_state, col_state):
    hid = lax.axis_size("hid")
    wid = lax.axis_size("wid")
    own_tile = weights[0]
    features, hidden = own_tile.shape
    half = hidden // 2
    rows = grad_out.shape[0]
    first = lax.axis_index("section") == 0
    even = lax.axis_index("hid") % 2 == 0
    home = lax.axis_index("section") == lax.axis_index("hid") % 2
    pair = ("section", "hid")

    def at(section, h):
        return section * hid + h

    over = [(at(h % 2, h), at(1 - h % 2, h)) for h in range(hid)]
    beside = [(at(h % 2, h ^ 1), at(h % 2, h)) for h in range(hid)]
    across = [(at(h % 2, h ^ 1), at(1 - h % 2, h)) for h in range(hid)]
    rings = [list(range(p, hid, 2)) for p in range(2)]

    def token_blocks(same, other):
        same, other = lax.optimization_barrier((same, other))
        far = lax.ppermute(other, pair, across)
        return same, lax.ppermute(other, pair, over), lax.ppermute(same, pair, beside), far

    def pick(blocks, columns):
        same, there, near, far = (block[:, columns] for block in blocks)
        return jnp.where(home, same, there), jnp.where(home, near, far)

    tile_near = lax.ppermute(
        by_rows(jnp.where(first & even, own_tile[:, half:], own_tile[:, :half])),
        "hid",
        [(h, h ^ 1) for h in range(hid)],
    )
    tile_over = lax.ppermute(own_tile[:, half:], pair, [(at(1, h), at(0, h)) for h in range(hid)])
    tile_far = lax.ppermute(
        own_tile[:, half:], pair, [(at(1, h), at(0, h ^ 1)) for h in range(hid)]
    )
    blocks = token_blocks(
        jnp.concatenate([grad_out, jnp.where(first, preact[:, half:], preact[:, :half])], axis=1),
        jnp.concatenate([grad_out, jnp.where(first, preact[:, :half], preact[:, half:])], axis=1),
    )
    grad_half = spread(jnp.concatenate(pick(blocks, slice(features)), axis=1), "wid")
    hidden_part = jnp.dot(
        grad_half[:, :features],
        jnp.where(first, tile_over, own_tile[:, :half]),
        preferred_element_type=jnp.float32,
    ) + jnp.dot(
        grad_half[:, features:],
        jnp.where(first, tile_far, tile_near),
        preferred_element_type=jnp.float32,
    )
    hidden_share = sum_blocks(hidden_part, "hid", rings)
    pre_own, pre_next = pick(blocks, slice(features, None))
    pre_half = jnp.concatenate(
        [jnp.where(even, pre_own, pre_next), jnp.where(even, pre_next, pre_own)]
    )

    def column_blocks(own, near):
        return jnp.concatenate([jnp.where(even, own, near), jnp.where(even, near, own)])

    evens = range(0, hid, 2)
    pre_over = lax.ppermute(pre_half, pair, [(at(0, h + 1), at(1, h + 1)) for h in evens])
    pre_near = lax.ppermute(
        pre_half,
        pair,
        [(at(1, h + 1), at(1, h)) for h in evens] + [(at(0, h), at(1, h + 1)) for h in evens],
    )
    act_share = gelu_value(
        column_blocks(jnp.where(even, pre_half, pre_over), pre_near).astype(jnp.float32)
    ).astype(jnp.bfloat16)
    pre_share = (hidden_share * gelu_slope(pre_half.astype(jnp.float32))).astype(jnp.bfloat16)
    share_over = lax.ppermute(pre_share, pair, [(at(1, h), at(0, h)) for h in evens])
    share_near = lax.ppermute(
        pre_share,
        pair,
        [(at(1, h + 1), at(0, h)) for h in evens] + [(at(0, h), at(0, h + 1)) for h in evens],
    )
    pre_share = column_blocks(jnp.where(even, share_over, pre_share), share_near)
    right = lax.all_gather(
        jnp.where(first, pre_share, act_share), "hid", axis=0, axis_index_groups=rings, tiled=True
    )

    def neighbour(block):
        return lax.ppermute(block, "hid", [(h, h ^ 1) for h in range(hid)])

    kept = jnp.where(first, inputs, grad_out)
    given = jnp.where(first, grad_out, inputs)
    taken = lax.ppermute(given, "section", [(0, 1), (1, 0)])
    left_own = jnp.concatenate([jnp.where(first, kept, taken), jnp.where(first, taken, kept)])
    left = spread(jnp.concatenate([left_own, neighbour(left_own)], axis=1), "wid")
    left = jnp.swapaxes(left.reshape(wid // 2, 2, 2, rows, 2 * features), 1, 2)
    left = left.reshape(2 * wid * rows, 2 * features)

    both = by_rows(contract(left, right))
    squares = both * both
    row_both = jnp.sum(squares, axis=1)
    col_local = jnp.sum(squares, axis=0)
    swapped = neighbour(both[features:])
    row_prev = row_state[0]
    col_prev = col_state[0]
    scalars = jnp.stack([jnp.sum(row_both), jnp.sum(row_prev)])
    packed = jnp.concatenate(
        [col_local, row_both[features:], scalars, jnp.zeros((-(half + features + 2) % (8 * LANES),), jnp.float32)]
    ).reshape(-1, LANES)
    taken = spread(packed, "hid").reshape((hid,) + packed.shape)
    over_hid = jnp.sum(taken.reshape((hid // 2, 2) + packed.shape), axis=0).reshape(2, -1)
    col_total = over_hid[:, :half].reshape(-1)
    square_sum = over_hid[0, half + features] + over_hid[1, half + features]
    prev_sum = over_hid[0, half + features + 1] + over_hid[1, half + features + 1]
    is_near = lax.broadcasted_iota(jnp.int32, (hid, 1, 1), 0) == lax.axis_index("hid") ^ 1
    row_near = jnp.sum(
        jnp.where(is_near, taken[:, half // LANES : (half + features) // LANES], 0.0), axis=0
    ).reshape(-1)
    row_local = row_both[:features] + row_near

    my_columns = jnp.where(even, own_tile[:, :half], own_tile[:, half:])
    my_columns, tile_next = lax.optimization_barrier((by_rows(my_columns), by_rows(tile_near)))

    def input_blocks(tile):
        partial = lax.dot_general(
            right, tile, (((1,), (1,)), ((), ())), preferred_element_type=jnp.float32
        ).astype(jnp.bfloat16)
        blocks = jnp.swapaxes(partial.reshape(wid // 2, 2, 2, rows, features), 1, 2)
        return blocks.reshape(wid, 2 * rows, features)

    blocks = jnp.concatenate([input_blocks(my_columns), input_blocks(tile_next)], axis=2)
    extra = thirds(row_local, square_sum)
    blocks = jnp.concatenate([blocks, jnp.broadcast_to(extra[None], (wid,) + extra.shape)], axis=1)
    over_wid = jnp.sum(exchange(blocks, "wid").astype(jnp.float32), axis=0)
    mine, others = over_wid[: 2 * rows, :features], over_wid[: 2 * rows, features:]
    near_sum = lax.ppermute(others[:rows], pair, [(at(0, h), at(0, h ^ 1)) for h in range(hid)])
    over_sum = lax.ppermute(mine[rows:], pair, [(at(0, h), at(1, h)) for h in range(hid)])
    far_sum = lax.ppermute(others[rows:], pair, [(at(0, h), at(1, h ^ 1)) for h in range(hid)])
    input_sum = jnp.where(first, mine[:rows], over_sum) + jnp.where(first, near_sum, far_sum)
    input_grad = input_sum + grad_out.astype(jnp.float32)
    totals = jnp.sum(over_wid[2 * rows :], axis=0)
    row_total, square_total = totals[:features], totals[features]

    own_half = both[:features]
    gradient = jnp.concatenate(
        [jnp.where(even, own_half, swapped), jnp.where(even, swapped, own_half)], axis=1
    )
    row_moment = decay_rate * row_prev + (1.0 - decay_rate) / FF * row_total
    col_moment = decay_rate * col_prev + (1.0 - decay_rate) / D * col_total
    row_mean = decay_rate / D * prev_sum + (1.0 - decay_rate) / FF / D * square_total
    update = gradient * lax.rsqrt(row_moment[:, None] * col_moment[None, :] / row_mean)
    return (input_grad, update[None])


def solution(mesh):
    placed = (
        P("section", "hid", "wid"),
        P(("section", "hid"), "wid"),
        P(("section", "wid"), "hid"),
        P(("section", "wid"), "hid"),
        P("section", "hid"),
        P("section", "wid"),
    )

    return jax.shard_map(
        shards,
        mesh=mesh,
        in_specs=placed,
        out_specs=(P(("section", "wid"), "hid"), P("section", "hid", "wid")),
        check_vma=False,
    )
```

time: 274 us -> 283 us (1.033)
  starting transfers between devices: 87.3 us -> 104 us
  waiting for transfers between devices: 139 us -> 124 us
  local copies, waits for them, and re-layouts: 7.24 us -> 10.2 us
    all_gather x1, waiting for transfers between devices: 53 us -> 2.65 us  [shards(): lax.all_gather(jnp.where(first, pre_share, act_share), 'hid', axis=0, axi...]
    ppermute x8 -> x12, waiting for transfers between devices: 14.4 us -> 32.1 us  [the longest x2 26.4 us: neighbour(): return lax.ppermute(block, 'hid', [(h, h ^ 1) for h in range(hid)])]
    ppermute x1, waiting for transfers between devices: 0.01 us -> 17.1 us  [shards(): lax.ppermute(own_tile[:, half:], pair, [(at(1, h), at(0, h ^ 1)) for h in...]
    ppermute x8 -> x12, starting transfers between devices: 20 us -> 37 us  [the longest x1 11.9 us: shards(): lax.ppermute(pre_share, pair, [(at(1, h + 1), at(0, h)) for h in evens] +...]
    all_to_all x4, waiting for transfers between devices: 36.5 us -> 29.2 us  [exchange(): return lax.all_to_all(blocks, axis, split_axis=0, concat_axis=0, tiled=True)]
    ppermute x1, waiting for transfers between devices: 5.95 us -> 10.5 us  [shards(): lax.ppermute(own_tile[:, half:], pair, [(at(1, h), at(0, h)) for h in ran...]
    ppermute x1, starting transfers between devices: 6.41 us -> 1.92 us  [shards(): taken = lax.ppermute(given, 'section', [(0, 1), (1, 0)])]
    all_to_all x4, starting transfers between devices: 43.1 us -> 47.2 us  [exchange(): return lax.all_to_all(blocks, axis, split_axis=0, concat_axis=0, tiled=True)]
  transfers between devices with their start and end apart: 19 -> 22, of which waited for: 9 -> 11; matrix products, arithmetic and copies ran while one was open for 5% -> 5% of each run, Pallas kernels for 0% -> 0%
where the time goes in v5:
time: 283 us; the launch traced here: 281 us
  waiting for transfers between devices  124 us (44%)
  starting transfers between devices  104 us (37%)
  between operations  18.6 us (7%)
  matrix products  12.7 us (4%)
  other arithmetic  11.6 us (4%)
  local copies, waits for them, and re-layouts  10.2 us (4%)
    all_to_all x4, starting transfers between devices, exchange(): return lax.all_to_all(blocks, axis, split_axis=0, concat_axis=0, tiled=True)  47.2 us
    all_to_all x1, waiting for transfers between devices, sum_blocks(): lax.all_to_all(jnp.concatenate([coded, power], axis=1), axis, split_axis=...  29.6 us
    all_to_all x4, waiting for transfers between devices, exchange(): return lax.all_to_all(blocks, axis, split_axis=0, concat_axis=0, tiled=True)  29.2 us
    ppermute x2, waiting for transfers between devices, neighbour(): return lax.ppermute(block, 'hid', [(h, h ^ 1) for h in range(hid)])  26.4 us
    ppermute x1, waiting for transfers between devices, shards(): lax.ppermute(own_tile[:, half:], pair, [(at(1, h), at(0, h ^ 1)) for h in...  17.1 us
    all_to_all x1, starting transfers between devices, sum_blocks(): lax.all_to_all(jnp.concatenate([coded, power], axis=1), axis, split_axis=...  14.5 us
    ppermute x1, starting transfers between devices, shards(): lax.ppermute(pre_share, pair, [(at(1, h + 1), at(0, h)) for h in evens] +...  11.9 us
    ppermute x1, waiting for transfers between devices, shards(): lax.ppermute(own_tile[:, half:], pair, [(at(1, h), at(0, h)) for h in ran...  10.5 us
  transfers between devices with their start and end apart: 22, of which 11 were waited for; matrix products, arithmetic and copies ran while one was open for 5% of the time, Pallas kernels for 0%

profile of v5, /device:TPU:1, one launch (start us, length us, event | category | flops | bytes accessed | tf_op | source)
XLA Modules:
  0.0 280.9 jit_solution(6152735771980047052)
XLA Ops:
  8.9 4.0 %collective-permute-start = (bf16[32,1152]{1,0:T(8,128)(2,1)S(1)}, bf16[32,1152]{1,0:T(8,128)(2,1)S(1)}, u32[]{:S(2)}, u32[]{:S(2)}) collective-permute-start(bf16[32,1152]{1,0:T(8,128)(2,1)S(1)} %get-tuple-element.7), channel_id=1, source_target_pairs={{0,256},{272,16},{32,288},{304,48},{64,320},{336,80},{96,352},{368... | collective-permute-start | bytes 221192 | tf_op jit(solution)/shard_map/ppermute | solution.py:105
  14.9 4.1 %collective-permute-done.1 = bf16[32,1152]{1,0:T(8,128)(2,1)S(1)} collective-permute-done((bf16[32,1152]{1,0:T(8,128)(2,1)S(1)}, bf16[32,1152]{1,0:T(8,128)(2,1)S(1)}, u32[]{:S(2)}, u32[]{:S(2)}) %collective-permute-start.1) | collective-permute-done | bytes 73760 | tf_op jit(solution)/shard_map/ppermute | solution.py:105
  20.0 8.4 %all-to-all-start = ((bf16[16,32,768]{2,1,0:T(8,128)(2,1)}), bf16[16,32,768]{2,1,0:T(8,128)(2,1)S(1)}, u32[]{:S(2)}, u32[]{:S(2)}) async-start(bf16[16,32,768]{2,1,0:T(8,128)(2,1)} %broadcast_in_dim.32), calls=%async_computation | async-start | bytes 1572864 | tf_op jit(solution)/shard_map/all_to_all | solution.py:41
  34.2 17.1 %collective-permute-done.4 = bf16[384,768]{1,0:T(8,128)(2,1)S(1)} collective-permute-done((bf16[384,768]{1,0:T(8,128)(2,1)S(1)}, bf16[384,768]{1,0:T(8,128)(2,1)S(1)}, u32[]{:S(2)}, u32[]{:S(2)}) %collective-permute-start.4) | collective-permute-done | bytes 589856 | tf_op jit(solution)/shard_map/ppermute | solution.py:117
  54.0 10.5 %collective-permute-done.3 = bf16[384,768]{1,0:T(8,128)(2,1)} collective-permute-done((bf16[384,768]{1,0:T(8,128)(2,1)S(1)}, bf16[384,768]{1,0:T(8,128)(2,1)}, u32[]{:S(2)}, u32[]{:S(2)}) %collective-permute-start.3) | collective-permute-done | bytes 589856 | tf_op jit(solution)/shard_map/ppermute | solution.py:116
  64.5 2.3 abs_reduce_fusion
  68.8 14.5 %all-to-all-start.1 = ((f16[8,72,768]{2,1,0:T(8,128)(2,1)}), f16[8,72,768]{2,1,0:T(8,128)(2,1)S(1)}, u32[]{:S(2)}, u32[]{:S(2)}) async-start(f16[8,72,768]{2,1,0:T(8,128)(2,1)} %concatenate.56), calls=%async_computation.1 | async-start | bytes 1769472 | tf_op jit(solution)/shard_map/all_to_all | solution.py:70
  84.1 2.9 %collective-permute-start.9 = (bf16[64,768]{1,0:T(8,128)(2,1)S(1)}, bf16[64,768]{1,0:T(8,128)(2,1)S(1)}, u32[]{:S(2)}, u32[]{:S(2)}) collective-permute-start(bf16[64,768]{1,0:T(8,128)(2,1)S(1)} %pad_maximum_fusion.1), channel_id=1, source_target_pairs={{272,256},{304,288},{336,320},{368,352},{400,384},{432,416},{464,4... | collective-permute-start | bytes 294920 | tf_op jit(solution)/shard_map/ppermute | solution.py:145
  87.0 29.6 %all-to-all-done.1 = f16[8,72,768]{2,1,0:T(8,128)(2,1)S(1)} async-done(((f16[8,72,768]{2,1,0:T(8,128)(2,1)}), f16[8,72,768]{2,1,0:T(8,128)(2,1)S(1)}, u32[]{:S(2)}, u32[]{:S(2)}) %all-to-all-start.1) | async-done | bytes 884768 | tf_op jit(solution)/shard_map/all_to_all | solution.py:70
  118.4 11.9 %collective-permute-start.7 = (bf16[64,768]{1,0:T(8,128)(2,1)S(1)}, bf16[64,768]{1,0:T(8,128)(2,1)S(1)}, u32[]{:S(2)}, u32[]{:S(2)}) collective-permute-start(bf16[64,768]{1,0:T(8,128)(2,1)S(1)} %fusion.20), channel_id=1, source_target_pairs={{272,0},{304,32},{336,64},{368,96},{400,128},{432,160},{464,192},{... | collective-permute-start | bytes 294920 | tf_op jit(solution)/shard_map/ppermute | solution.py:155
  134.7 2.6 collective-permute-done.10
  137.4 3.7 %collective-permute-start.11 = (bf16[64,384]{1,0:T(8,128)(2,1)S(1)}, bf16[64,384]{1,0:T(8,128)(2,1)S(1)}, u32[]{:S(2)}, u32[]{:S(2)}) collective-permute-start(bf16[64,384]{1,0:T(8,128)(2,1)S(1)} %pad_maximum_fusion.6), channel_id=1, source_target_pairs={{0,16},{16,0},{32,48},{48,32},{64,80},{80,64},{96,112},{112,96},{1... | collective-permute-start | bytes 147464 | tf_op jit(solution)/shard_map/ppermute | solution.py:166
  143.9 19.8 %all-to-all-start.2 = ((bf16[16,64,768]{2,1,0:T(8,128)(2,1)}), bf16[16,64,768]{2,1,0:T(8,128)(2,1)S(1)}, u32[]{:S(2)}, u32[]{:S(2)}) async-start(bf16[16,64,768]{2,1,0:T(8,128)(2,1)} %broadcast_in_dim.33), calls=%async_computation.2 | async-start | bytes 3145728 | tf_op jit(solution)/shard_map/all_to_all | solution.py:41
  164.3 22.0 %all-to-all-done.2 = bf16[16,64,768]{2,1,0:T(8,128)(2,1)S(1)} async-done(((bf16[16,64,768]{2,1,0:T(8,128)(2,1)}), bf16[16,64,768]{2,1,0:T(8,128)(2,1)S(1)}, u32[]{:S(2)}, u32[]{:S(2)}) %all-to-all-start.2) | async-done | bytes 1572896 | tf_op jit(solution)/shard_map/all_to_all | solution.py:41
  186.5 2.6 all-gather.2.cloned.1.call-done
  189.2 5.1 %multiply_reduce_fusion = (f32[]{:T(128)}, f32[768]{0:T(1024)S(1)}, f32[768]{0:T(1024)S(1)}, f32[768,768]{1,0:T(8,128)}) fusion(bf16[1024,768]{1,0:T(8,128)(2,1)S(1)} %bitcast.50, bf16[1024,768]{1,0:T(8,128)(2,1)} %all-gather.2.cloned.1.call-done), kind=kOutput, calls=%fused_computation.2 | convolution fusion | flops 1210317312 | bytes 5511172 | tf_op jit(solution)/shard_map/dot_general | solution.py:35
  196.3 5.3 %all-to-all-start.3 = ((f32[16,16,128]{2,1,0:T(8,128)}), f32[16,16,128]{2,1,0:T(8,128)S(1)}, u32[]{:S(2)}, u32[]{:S(2)}) async-start(f32[16,16,128]{2,1,0:T(8,128)} %broadcast_in_dim.64), calls=%async_computation.3 | async-start | bytes 262144 | tf_op jit(solution)/shard_map/all_to_all | solution.py:41
  201.6 2.5 convolution_convert_fusion.1
  206.3 7.2 %all-to-all-done.3 = f32[16,16,128]{2,1,0:T(8,128)S(1)} async-done(((f32[16,16,128]{2,1,0:T(8,128)}), f32[16,16,128]{2,1,0:T(8,128)S(1)}, u32[]{:S(2)}, u32[]{:S(2)}) %all-to-all-start.3) | async-done | bytes 131104 | tf_op jit(solution)/shard_map/all_to_all | solution.py:41
  217.1 13.8 %all-to-all-start.4 = ((bf16[16,72,768]{2,1,0:T(8,128)(2,1)}), bf16[16,72,768]{2,1,0:T(8,128)(2,1)S(1)}, u32[]{:S(2)}, u32[]{:S(2)}) async-start(bf16[16,72,768]{2,1,0:T(8,128)(2,1)} %pad_maximum_fusion), calls=%async_computation.4 | async-start | bytes 3538944 | tf_op jit(solution)/shard_map/all_to_all | solution.py:41
  232.4 3.0 %collective-permute-start.15 = (f32[384,768]{1,0:T(8,128)S(1)}, f32[384,768]{1,0:T(8,128)S(1)}, u32[]{:S(2)}, u32[]{:S(2)}) collective-permute-start(f32[384,768]{1,0:T(8,128)S(1)} %slice.165), channel_id=1, source_target_pairs={{0,16},{16,0},{32,48},{48,32},{64,80},{80,64},{96,112},{112,96},{1... | collective-permute-start | bytes 3538952 | tf_op jit(solution)/shard_map/ppermute | solution.py:166
  236.7 25.0 %collective-permute-done.15 = f32[384,768]{1,0:T(8,128)S(1)} collective-permute-done((f32[384,768]{1,0:T(8,128)S(1)}, f32[384,768]{1,0:T(8,128)S(1)}, u32[]{:S(2)}, u32[]{:S(2)}) %collective-permute-start.15) | collective-permute-done | bytes 1179680 | tf_op jit(solution)/shard_map/ppermute | solution.py:166
  265.7 2.7 collective-permute-start.13
  270.4 3.1 %maximum_multiply_fusion = f32[1,384,1536]{2,1,0:T(8,128)} fusion(f32[1,384,768]{2,1,0:T(8,128)} %get-tuple-element.16, f32[1,384,768]{2,1,0:T(8,128)S(1)} %get-tuple-element.15, f32[]{:T(128)S(6)} %add.77, f32[1536]{0:T(1024)S(1)} %add_reduce_fusion, f32[384]{0:T(512)S(1)} %multiply_add_fusion), kind=kLoop, calls=%fused_computation.1 | loop fusion | flops 2359296 | bytes 4726276 | tf_op jit(solution)/shard_map/mul | solution.py:228
  (119 shorter events, 38.6 us)
Async XLA Ops:
  7.2 21.3 %copy-start = (bf16[1,384,1536]{2,1,0:T(8,128)(2,1)S(1)}, bf16[1,384,1536]{2,1,0:T(8,128)(2,1)}, u32[]{:S(2)}) copy-start(bf16[1,384,1536]{2,1,0:T(8,128)(2,1)} %param.6) | copy-start | bytes 3538948
  8.9 6.0 %collective-permute-start = (bf16[32,1152]{1,0:T(8,128)(2,1)S(1)}, bf16[32,1152]{1,0:T(8,128)(2,1)S(1)}, u32[]{:S(2)}, u32[]{:S(2)}) collective-permute-start(bf16[32,1152]{1,0:T(8,128)(2,1)S(1)} %get-tuple-element.7), channel_id=1, source_target_pairs={{0,256},{272,16},{32,288},{304,48},{64,320},{336,80},{96,352},{368... | collective-permute-start | bytes 221192 | tf_op jit(solution)/shard_map/ppermute | solution.py:105
  12.9 6.1 %collective-permute-start.2 = (bf16[32,1152]{1,0:T(8,128)(2,1)S(1)}, bf16[32,1152]{1,0:T(8,128)(2,1)S(1)}, u32[]{:S(2)}, u32[]{:S(2)}) collective-permute-start(bf16[32,1152]{1,0:T(8,128)(2,1)S(1)} %get-tuple-element.7), channel_id=1, source_target_pairs={{16,256},{256,16},{48,288},{288,48},{80,320},{320,80},{112,352},{3... | collective-permute-start | bytes 221192 | tf_op jit(solution)/shard_map/ppermute | solution.py:104
  13.6 5.5 %collective-permute-start.1 = (bf16[32,1152]{1,0:T(8,128)(2,1)S(1)}, bf16[32,1152]{1,0:T(8,128)(2,1)S(1)}, u32[]{:S(2)}, u32[]{:S(2)}) collective-permute-start(bf16[32,1152]{1,0:T(8,128)(2,1)S(1)} %get-tuple-element.6), channel_id=1, source_target_pairs={{16,0},{256,272},{48,32},{288,304},{80,64},{320,336},{112,96},{352... | collective-permute-start | bytes 221192 | tf_op jit(solution)/shard_map/ppermute | solution.py:105
  20.0 32.1 %all-to-all-start = ((bf16[16,32,768]{2,1,0:T(8,128)(2,1)}), bf16[16,32,768]{2,1,0:T(8,128)(2,1)S(1)}, u32[]{:S(2)}, u32[]{:S(2)}) async-start(bf16[16,32,768]{2,1,0:T(8,128)(2,1)} %broadcast_in_dim.32), calls=%async_computation | async-start | bytes 1572864 | tf_op jit(solution)/shard_map/all_to_all | solution.py:41
  29.4 21.9 %collective-permute-start.4 = (bf16[384,768]{1,0:T(8,128)(2,1)S(1)}, bf16[384,768]{1,0:T(8,128)(2,1)S(1)}, u32[]{:S(2)}, u32[]{:S(2)}) collective-permute-start(bf16[384,768]{1,0:T(8,128)(2,1)S(1)} %get-tuple-element.19), channel_id=1, source_target_pairs={{256,16},{272,0},{288,48},{304,32},{320,80},{336,64},{352,112},{36... | collective-permute-start | bytes 1769480 | tf_op jit(solution)/shard_map/ppermute | solution.py:117
  30.7 21.5 %collective-permute-start.5 = (bf16[384,768]{1,0:T(8,128)(2,1)S(1)}, bf16[384,768]{1,0:T(8,128)(2,1)S(1)}, u32[]{:S(2)}, u32[]{:S(2)}) collective-permute-start(bf16[384,768]{1,0:T(8,128)(2,1)S(1)} %get-tuple-element.18), channel_id=1, source_target_pairs={{0,16},{16,0},{32,48},{48,32},{64,80},{80,64},{96,112},{112,96},{1... | collective-permute-start | bytes 1769480 | tf_op jit(solution)/shard_map/ppermute | solution.py:111
  32.9 31.6 %collective-permute-start.3 = (bf16[384,768]{1,0:T(8,128)(2,1)S(1)}, bf16[384,768]{1,0:T(8,128)(2,1)}, u32[]{:S(2)}, u32[]{:S(2)}) collective-permute-start(bf16[384,768]{1,0:T(8,128)(2,1)S(1)} %get-tuple-element.19), channel_id=1, source_target_pairs={{256,0},{272,16},{288,32},{304,48},{320,64},{336,80},{352,96},{368... | collective-permute-start | bytes 1769480 | tf_op jit(solution)/shard_map/ppermute | solution.py:116
  68.8 47.8 %all-to-all-start.1 = ((f16[8,72,768]{2,1,0:T(8,128)(2,1)}), f16[8,72,768]{2,1,0:T(8,128)(2,1)S(1)}, u32[]{:S(2)}, u32[]{:S(2)}) async-start(f16[8,72,768]{2,1,0:T(8,128)(2,1)} %concatenate.56), calls=%async_computation.1 | async-start | bytes 1769472 | tf_op jit(solution)/shard_map/all_to_all | solution.py:70
  83.3 105.9 %all-gather.2.cloned.1.call-start = ((), (), s32[]{:S(2)}) async-start(), calls=%async_computation.5 | async-start | bytes 1769472 | tf_op jit(solution)/shard_map/all_gather | solution.py:161
  83.4 46.9 %collective-permute-start.8 = (bf16[64,768]{1,0:T(8,128)(2,1)S(1)}, bf16[64,768]{1,0:T(8,128)(2,1)S(1)}, u32[]{:S(2)}, u32[]{:S(2)}) collective-permute-start(bf16[64,768]{1,0:T(8,128)(2,1)S(1)} %pad_maximum_fusion.1), channel_id=1, source_target_pairs={{16,272},{48,304},{80,336},{112,368},{144,400},{176,432},{208,464}... | collective-permute-start | bytes 294920 | tf_op jit(solution)/shard_map/ppermute | solution.py:144
  84.1 46.2 %collective-permute-start.9 = (bf16[64,768]{1,0:T(8,128)(2,1)S(1)}, bf16[64,768]{1,0:T(8,128)(2,1)S(1)}, u32[]{:S(2)}, u32[]{:S(2)}) collective-permute-start(bf16[64,768]{1,0:T(8,128)(2,1)S(1)} %pad_maximum_fusion.1), channel_id=1, source_target_pairs={{272,256},{304,288},{336,320},{368,352},{400,384},{432,416},{464,4... | collective-permute-start | bytes 294920 | tf_op jit(solution)/shard_map/ppermute | solution.py:145
  117.1 13.3 %collective-permute-start.6 = (bf16[64,768]{1,0:T(8,128)(2,1)S(1)}, bf16[64,768]{1,0:T(8,128)(2,1)S(1)}, u32[]{:S(2)}, u32[]{:S(2)}) collective-permute-start(bf16[64,768]{1,0:T(8,128)(2,1)S(1)} %fusion.20), channel_id=1, source_target_pairs={{256,0},{288,32},{320,64},{352,96},{384,128},{416,160},{448,192},{... | collective-permute-start | bytes 294920 | tf_op jit(solution)/shard_map/ppermute | solution.py:154
  118.4 13.5 %collective-permute-start.7 = (bf16[64,768]{1,0:T(8,128)(2,1)S(1)}, bf16[64,768]{1,0:T(8,128)(2,1)S(1)}, u32[]{:S(2)}, u32[]{:S(2)}) collective-permute-start(bf16[64,768]{1,0:T(8,128)(2,1)S(1)} %fusion.20), channel_id=1, source_target_pairs={{272,0},{304,32},{336,64},{368,96},{400,128},{432,160},{464,192},{... | collective-permute-start | bytes 294920 | tf_op jit(solution)/shard_map/ppermute | solution.py:155
  132.8 4.6 %collective-permute-start.10 = (bf16[32,384]{1,0:T(8,128)(2,1)S(1)}, bf16[32,384]{1,0:T(8,128)(2,1)S(1)}, u32[]{:S(2)}, u32[]{:S(2)}) collective-permute-start(bf16[32,384]{1,0:T(8,128)(2,1)S(1)} %broadcast_select_fusion.14), channel_id=1, source_target_pairs={{0,256},{256,0},{1,257},{257,1},{2,258},{258,2},{3,259},{259,3},{4... | collective-permute-start | bytes 73736 | tf_op jit(solution)/shard_map/ppermute | solution.py:170
  137.4 5.2 %collective-permute-start.11 = (bf16[64,384]{1,0:T(8,128)(2,1)S(1)}, bf16[64,384]{1,0:T(8,128)(2,1)S(1)}, u32[]{:S(2)}, u32[]{:S(2)}) collective-permute-start(bf16[64,384]{1,0:T(8,128)(2,1)S(1)} %pad_maximum_fusion.6), channel_id=1, source_target_pairs={{0,16},{16,0},{32,48},{48,32},{64,80},{80,64},{96,112},{112,96},{1... | collective-permute-start | bytes 147464 | tf_op jit(solution)/shard_map/ppermute | solution.py:166
  143.9 42.5 %all-to-all-start.2 = ((bf16[16,64,768]{2,1,0:T(8,128)(2,1)}), bf16[16,64,768]{2,1,0:T(8,128)(2,1)S(1)}, u32[]{:S(2)}, u32[]{:S(2)}) async-start(bf16[16,64,768]{2,1,0:T(8,128)(2,1)} %broadcast_in_dim.33), calls=%async_computation.2 | async-start | bytes 3145728 | tf_op jit(solution)/shard_map/all_to_all | solution.py:41
  196.3 17.3 %all-to-all-start.3 = ((f32[16,16,128]{2,1,0:T(8,128)}), f32[16,16,128]{2,1,0:T(8,128)S(1)}, u32[]{:S(2)}, u32[]{:S(2)}) async-start(f32[16,16,128]{2,1,0:T(8,128)} %broadcast_in_dim.64), calls=%async_computation.3 | async-start | bytes 262144 | tf_op jit(solution)/shard_map/all_to_all | solution.py:41
  217.1 45.8 %all-to-all-start.4 = ((bf16[16,72,768]{2,1,0:T(8,128)(2,1)}), bf16[16,72,768]{2,1,0:T(8,128)(2,1)S(1)}, u32[]{:S(2)}, u32[]{:S(2)}) async-start(bf16[16,72,768]{2,1,0:T(8,128)(2,1)} %pad_maximum_fusion), calls=%async_computation.4 | async-start | bytes 3538944 | tf_op jit(solution)/shard_map/all_to_all | solution.py:41
  230.9 30.8 %copy-start.1 = (f32[768,768]{1,0:T(8,128)S(1)}, f32[768,768]{1,0:T(8,128)}, u32[]{:S(2)}) copy-start(f32[768,768]{1,0:T(8,128)} %get-tuple-element.44) | copy-start | bytes 7077892
  232.4 29.3 %collective-permute-start.15 = (f32[384,768]{1,0:T(8,128)S(1)}, f32[384,768]{1,0:T(8,128)S(1)}, u32[]{:S(2)}, u32[]{:S(2)}) collective-permute-start(f32[384,768]{1,0:T(8,128)S(1)} %slice.165), channel_id=1, source_target_pairs={{0,16},{16,0},{32,48},{48,32},{64,80},{80,64},{96,112},{112,96},{1... | collective-permute-start | bytes 3538952 | tf_op jit(solution)/shard_map/ppermute | solution.py:166
  263.7 9.7 %collective-permute-start.12 = (f32[32,384]{1,0:T(8,128)S(1)}, f32[32,384]{1,0:T(8,128)S(1)}, u32[]{:S(2)}, u32[]{:S(2)}) collective-permute-start(f32[32,384]{1,0:T(8,128)S(1)} %get-tuple-element.28), channel_id=1, source_target_pairs={{0,256},{16,272},{32,288},{48,304},{64,320},{80,336},{96,352},{112... | collective-permute-start | bytes 147464 | tf_op jit(solution)/shard_map/ppermute | solution.py:214
  265.7 7.8 %collective-permute-start.13 = (f32[32,384]{1,0:T(8,128)S(1)}, f32[32,384]{1,0:T(8,128)S(1)}, u32[]{:S(2)}, u32[]{:S(2)}) collective-permute-start(f32[32,384]{1,0:T(8,128)S(1)} %get-tuple-element.27), channel_id=1, source_target_pairs={{0,16},{16,0},{32,48},{48,32},{64,80},{80,64},{96,112},{112,96},{1... | collective-permute-start | bytes 147464 | tf_op jit(solution)/shard_map/ppermute | solution.py:213
  268.4 5.0 %collective-permute-start.14 = (f32[32,384]{1,0:T(8,128)S(1)}, f32[32,384]{1,0:T(8,128)S(1)}, u32[]{:S(2)}, u32[]{:S(2)}) collective-permute-start(f32[32,384]{1,0:T(8,128)S(1)} %get-tuple-element.26), channel_id=1, source_target_pairs={{0,272},{16,256},{32,304},{48,288},{64,336},{80,320},{96,368},{112... | collective-permute-start | bytes 147464 | tf_op jit(solution)/shard_map/ppermute | solution.py:215
  (17 other events, 157.3 us)
Sparse Core Ops, SparseCore 0:
  132.9 56.2 all-gather.1

commit v6 on v5

--- a/solution.py
+++ b/solution.py
@@ -104,10 +104,11 @@
         far = lax.ppermute(other, pair, across)
         return same, lax.ppermute(other, pair, over), lax.ppermute(same, pair, beside), far
 
-    def pick(blocks, columns):
-        same, there, near, far = (block[:, columns] for block in blocks)
+    def pick(blocks):
+        same, there, near, far = blocks
         return jnp.where(home, same, there), jnp.where(home, near, far)
 
+    grad_blocks = token_blocks(grad_out, grad_out)
     tile_near = lax.ppermute(
         by_rows(jnp.where(first & even, own_tile[:, half:], own_tile[:, :half])),
         "hid",
@@ -117,11 +118,11 @@
     tile_far = lax.ppermute(
         own_tile[:, half:], pair, [(at(1, h), at(0, h ^ 1)) for h in range(hid)]
     )
-    blocks = token_blocks(
-        jnp.concatenate([grad_out, jnp.where(first, preact[:, half:], preact[:, :half])], axis=1),
-        jnp.concatenate([grad_out, jnp.where(first, preact[:, :half], preact[:, half:])], axis=1),
-    )
-    grad_half = spread(jnp.concatenate(pick(blocks, slice(features)), axis=1), "wid")
+    pre_blocks = token_blocks(
+        jnp.where(first, preact[:, half:], preact[:, :half]),
+        jnp.where(first, preact[:, :half], preact[:, half:]),
+    )
+    grad_half = spread(jnp.concatenate(pick(grad_blocks), axis=1), "wid")
     hidden_part = jnp.dot(
         grad_half[:, :features],
         jnp.where(first, tile_over, own_tile[:, :half]),
@@ -132,7 +133,7 @@
         preferred_element_type=jnp.float32,
     )
     hidden_share = sum_blocks(hidden_part, "hid", rings)
-    pre_own, pre_next = pick(blocks, slice(features, None))
+    pre_own, pre_next = pick(pre_blocks)
     pre_half = jnp.concatenate(
         [jnp.where(even, pre_own, pre_next), jnp.where(even, pre_next, pre_own)]
     )

time: 283 us -> 284 us (level)
  waiting for transfers between devices: 124 us -> 137 us
  starting transfers between devices: 104 us -> 93.7 us
    ppermute x1 -> x2, waiting for transfers between devices: 4.09 us -> 37.8 us  [token_blocks(): lax.ppermute(same, pair, beside)]
    all_to_all x1, waiting for transfers between devices: 29.6 us -> 0.01 us  [sum_blocks(): lax.all_to_all(jnp.concatenate([coded, power], axis=1), axis, split_axis=...]
    ppermute x1, starting transfers between devices: 11.9 us -> 6.82 us  [shards(): lax.ppermute(pre_share, pair, [(at(1, h + 1), at(0, h)) for h in evens] +...]
    all_to_all x4, starting transfers between devices: 47.2 us -> 42.4 us  [exchange(): return lax.all_to_all(blocks, axis, split_axis=0, concat_axis=0, tiled=True)]
    all_gather x1, waiting for transfers between devices: 2.65 us -> 6.65 us  [shards(): lax.all_gather(jnp.where(first, pre_share, act_share), 'hid', axis=0, axi...]
  transfers between devices with their start and end apart: 22 -> 25, of which waited for: 11 -> 12; matrix products, arithmetic and copies ran while one was open for 5% -> 6% of each run, Pallas kernels for 0% -> 0%
where the time goes in v6:
time: 284 us; the launch traced here: 282 us
  waiting for transfers between devices  137 us (48%)
  starting transfers between devices  93.7 us (33%)
  between operations  18.5 us (7%)
  matrix products  12.7 us (4%)
  other arithmetic  10.7 us (4%)
  local copies, waits for them, and re-layouts  10.2 us (4%)
    all_to_all x4, starting transfers between devices, exchange(): return lax.all_to_all(blocks, axis, split_axis=0, concat_axis=0, tiled=True)  42.4 us
    ppermute x2, waiting for transfers between devices, token_blocks(): lax.ppermute(same, pair, beside)  37.8 us
    all_to_all x4, waiting for transfers between devices, exchange(): return lax.all_to_all(blocks, axis, split_axis=0, concat_axis=0, tiled=True)  29.3 us
    ppermute x2, waiting for transfers between devices, neighbour(): return lax.ppermute(block, 'hid', [(h, h ^ 1) for h in range(hid)])  27.9 us
    ppermute x1, waiting for transfers between devices, shards(): lax.ppermute(own_tile[:, half:], pair, [(at(1, h), at(0, h ^ 1)) for h in...  17.4 us
    all_to_all x1, starting transfers between devices, sum_blocks(): lax.all_to_all(jnp.concatenate([coded, power], axis=1), axis, split_axis=...  14.2 us
    ppermute x1, waiting for transfers between devices, shards(): lax.ppermute(own_tile[:, half:], pair, [(at(1, h), at(0, h)) for h in ran...  10.5 us
    ppermute x1, starting transfers between devices, shards(): lax.ppermute(pre_share, pair, [(at(1, h + 1), at(0, h)) for h in evens] +...  6.82 us
  transfers between devices with their start and end apart: 25, of which 12 were waited for; matrix products, arithmetic and copies ran while one was open for 6% of the time, Pallas kernels for 0%

profile of v6, /device:TPU:1, one launch (start us, length us, event | category | flops | bytes accessed | tf_op | source)
XLA Modules:
  0.0 282.4 jit_solution(15008561619772211327)
XLA Ops:
  7.2 4.2 %collective-permute-start = (bf16[32,384]{1,0:T(8,128)(2,1)}, bf16[32,384]{1,0:T(8,128)(2,1)S(1)}, u32[]{:S(2)}, u32[]{:S(2)}) collective-permute-start(bf16[32,384]{1,0:T(8,128)(2,1)} %param.9), channel_id=1, source_target_pairs={{0,256},{272,16},{32,288},{304,48},{64,320},{336,80},{96,352},{368... | collective-permute-start | bytes 73736 | tf_op jit(solution)/shard_map/ppermute | solution.py:105
  14.1 2.7 collective-permute-done.1
  17.8 8.8 %all-to-all-start = ((bf16[16,32,768]{2,1,0:T(8,128)(2,1)}), bf16[16,32,768]{2,1,0:T(8,128)(2,1)S(1)}, u32[]{:S(2)}, u32[]{:S(2)}) async-start(bf16[16,32,768]{2,1,0:T(8,128)(2,1)} %broadcast_in_dim.32), calls=%async_computation | async-start | bytes 1572864 | tf_op jit(solution)/shard_map/all_to_all | solution.py:41
  32.0 17.4 %collective-permute-done.4 = bf16[384,768]{1,0:T(8,128)(2,1)S(1)} collective-permute-done((bf16[384,768]{1,0:T(8,128)(2,1)S(1)}, bf16[384,768]{1,0:T(8,128)(2,1)S(1)}, u32[]{:S(2)}, u32[]{:S(2)}) %collective-permute-start.4) | collective-permute-done | bytes 589856 | tf_op jit(solution)/shard_map/ppermute | solution.py:118
  52.2 10.5 %collective-permute-done.3 = bf16[384,768]{1,0:T(8,128)(2,1)} collective-permute-done((bf16[384,768]{1,0:T(8,128)(2,1)S(1)}, bf16[384,768]{1,0:T(8,128)(2,1)}, u32[]{:S(2)}, u32[]{:S(2)}) %collective-permute-start.3) | collective-permute-done | bytes 589856 | tf_op jit(solution)/shard_map/ppermute | solution.py:117
  62.7 2.3 abs_reduce_fusion
  66.9 14.2 %all-to-all-start.1 = ((f16[8,72,768]{2,1,0:T(8,128)(2,1)}), f16[8,72,768]{2,1,0:T(8,128)(2,1)S(1)}, u32[]{:S(2)}, u32[]{:S(2)}) async-start(f16[8,72,768]{2,1,0:T(8,128)(2,1)} %concatenate.48), calls=%async_computation.1 | async-start | bytes 1769472 | tf_op jit(solution)/shard_map/all_to_all | solution.py:70
  84.6 35.1 %collective-permute-done.7 = bf16[32,768]{1,0:T(8,128)(2,1)S(1)} collective-permute-done((bf16[32,768]{1,0:T(8,128)(2,1)S(1)}, bf16[32,768]{1,0:T(8,128)(2,1)S(1)}, u32[]{:S(2)}, u32[]{:S(2)}) %collective-permute-start.7) | collective-permute-done | bytes 49184 | tf_op jit(solution)/shard_map/ppermute | solution.py:105
  122.2 6.8 %collective-permute-start.10 = (bf16[64,768]{1,0:T(8,128)(2,1)S(1)}, bf16[64,768]{1,0:T(8,128)(2,1)S(1)}, u32[]{:S(2)}, u32[]{:S(2)}) collective-permute-start(bf16[64,768]{1,0:T(8,128)(2,1)S(1)} %fusion.20), channel_id=1, source_target_pairs={{272,0},{304,32},{336,64},{368,96},{400,128},{432,160},{464,192},{... | collective-permute-start | bytes 294920 | tf_op jit(solution)/shard_map/ppermute | solution.py:156
  132.1 2.3 collective-permute-done.9
  137.2 3.0 %collective-permute-done.13 = bf16[32,384]{1,0:T(8,128)(2,1)S(1)} collective-permute-done((bf16[32,384]{1,0:T(8,128)(2,1)S(1)}, bf16[32,384]{1,0:T(8,128)(2,1)S(1)}, u32[]{:S(2)}, u32[]{:S(2)}) %collective-permute-start.13) | collective-permute-done | bytes 24608 | tf_op jit(solution)/shard_map/ppermute | solution.py:171
  142.2 2.9 %collective-permute-done.14 = bf16[64,384]{1,0:T(8,128)(2,1)S(1)} collective-permute-done((bf16[64,384]{1,0:T(8,128)(2,1)S(1)}, bf16[64,384]{1,0:T(8,128)(2,1)S(1)}, u32[]{:S(2)}, u32[]{:S(2)}) %collective-permute-start.14) | collective-permute-done | bytes 49184 | tf_op jit(solution)/shard_map/ppermute | solution.py:167
  146.4 14.9 %all-to-all-start.2 = ((bf16[16,64,768]{2,1,0:T(8,128)(2,1)}), bf16[16,64,768]{2,1,0:T(8,128)(2,1)S(1)}, u32[]{:S(2)}, u32[]{:S(2)}) async-start(bf16[16,64,768]{2,1,0:T(8,128)(2,1)} %broadcast_in_dim.33), calls=%async_computation.2 | async-start | bytes 3145728 | tf_op jit(solution)/shard_map/all_to_all | solution.py:41
  162.0 22.0 %all-to-all-done.2 = bf16[16,64,768]{2,1,0:T(8,128)(2,1)S(1)} async-done(((bf16[16,64,768]{2,1,0:T(8,128)(2,1)}), bf16[16,64,768]{2,1,0:T(8,128)(2,1)S(1)}, u32[]{:S(2)}, u32[]{:S(2)}) %all-to-all-start.2) | async-done | bytes 1572896 | tf_op jit(solution)/shard_map/all_to_all | solution.py:41
  184.2 6.7 %all-gather.2.cloned.1.call-done = bf16[1024,768]{1,0:T(8,128)(2,1)} async-done(((bf16[128,768]{1,0:T(8,128)(2,1)}), bf16[1024,768]{1,0:T(8,128)(2,1)}) %all-gather.2.cloned.1.call-update) | async-done | bytes 1572880 | tf_op jit(solution)/shard_map/all_gather | solution.py:162
  190.9 5.1 %multiply_reduce_fusion = (f32[]{:T(128)}, f32[768]{0:T(1024)S(1)}, f32[768]{0:T(1024)S(1)}, f32[768,768]{1,0:T(8,128)}) fusion(bf16[1024,768]{1,0:T(8,128)(2,1)S(1)} %bitcast.50, bf16[1024,768]{1,0:T(8,128)(2,1)} %all-gather.2.cloned.1.call-done), kind=kOutput, calls=%fused_computation.2 | convolution fusion | flops 1210317312 | bytes 5511172 | tf_op jit(solution)/shard_map/dot_general | solution.py:35
  197.9 5.5 %all-to-all-start.3 = ((f32[16,16,128]{2,1,0:T(8,128)}), f32[16,16,128]{2,1,0:T(8,128)S(1)}, u32[]{:S(2)}, u32[]{:S(2)}) async-start(f32[16,16,128]{2,1,0:T(8,128)} %broadcast_in_dim.64), calls=%async_computation.3 | async-start | bytes 262144 | tf_op jit(solution)/shard_map/all_to_all | solution.py:41
  203.5 2.5 convolution_convert_fusion.1
  208.2 7.2 %all-to-all-done.3 = f32[16,16,128]{2,1,0:T(8,128)S(1)} async-done(((f32[16,16,128]{2,1,0:T(8,128)}), f32[16,16,128]{2,1,0:T(8,128)S(1)}, u32[]{:S(2)}, u32[]{:S(2)}) %all-to-all-start.3) | async-done | bytes 131104 | tf_op jit(solution)/shard_map/all_to_all | solution.py:41
  219.0 13.2 %all-to-all-start.4 = ((bf16[16,72,768]{2,1,0:T(8,128)(2,1)}), bf16[16,72,768]{2,1,0:T(8,128)(2,1)S(1)}, u32[]{:S(2)}, u32[]{:S(2)}) async-start(bf16[16,72,768]{2,1,0:T(8,128)(2,1)} %pad_maximum_fusion), calls=%async_computation.4 | async-start | bytes 3538944 | tf_op jit(solution)/shard_map/all_to_all | solution.py:41
  233.7 3.0 %collective-permute-start.18 = (f32[384,768]{1,0:T(8,128)S(1)}, f32[384,768]{1,0:T(8,128)S(1)}, u32[]{:S(2)}, u32[]{:S(2)}) collective-permute-start(f32[384,768]{1,0:T(8,128)S(1)} %slice.127), channel_id=1, source_target_pairs={{0,16},{16,0},{32,48},{48,32},{64,80},{80,64},{96,112},{112,96},{1... | collective-permute-start | bytes 3538952 | tf_op jit(solution)/shard_map/ppermute | solution.py:167
  238.1 24.9 %collective-permute-done.18 = f32[384,768]{1,0:T(8,128)S(1)} collective-permute-done((f32[384,768]{1,0:T(8,128)S(1)}, f32[384,768]{1,0:T(8,128)S(1)}, u32[]{:S(2)}, u32[]{:S(2)}) %collective-permute-start.18) | collective-permute-done | bytes 1179680 | tf_op jit(solution)/shard_map/ppermute | solution.py:167
  266.9 3.0 %collective-permute-start.16 = (f32[32,384]{1,0:T(8,128)S(1)}, f32[32,384]{1,0:T(8,128)S(1)}, u32[]{:S(2)}, u32[]{:S(2)}) collective-permute-start(f32[32,384]{1,0:T(8,128)S(1)} %get-tuple-element.29), channel_id=1, source_target_pairs={{0,16},{16,0},{32,48},{48,32},{64,80},{80,64},{96,112},{112,96},{1... | collective-permute-start | bytes 147464 | tf_op jit(solution)/shard_map/ppermute | solution.py:214
  271.8 3.1 %maximum_multiply_fusion = f32[1,384,1536]{2,1,0:T(8,128)} fusion(f32[1,384,768]{2,1,0:T(8,128)} %get-tuple-element.20, f32[1,384,768]{2,1,0:T(8,128)S(1)} %get-tuple-element.19, f32[]{:T(128)S(6)} %add.77, f32[1536]{0:T(1024)S(1)} %add_reduce_fusion, f32[384]{0:T(512)S(1)} %multiply_add_fusion), kind=kLoop, calls=%fused_computation.1 | loop fusion | flops 2359296 | bytes 4726276 | tf_op jit(solution)/shard_map/mul | solution.py:229
  (110 shorter events, 42.5 us)
Async XLA Ops:
  7.2 6.2 %collective-permute-start = (bf16[32,384]{1,0:T(8,128)(2,1)}, bf16[32,384]{1,0:T(8,128)(2,1)S(1)}, u32[]{:S(2)}, u32[]{:S(2)}) collective-permute-start(bf16[32,384]{1,0:T(8,128)(2,1)} %param.9), channel_id=1, source_target_pairs={{0,256},{272,16},{32,288},{304,48},{64,320},{336,80},{96,352},{368... | collective-permute-start | bytes 73736 | tf_op jit(solution)/shard_map/ppermute | solution.py:105
  11.3 5.5 %collective-permute-start.2 = (bf16[32,384]{1,0:T(8,128)(2,1)}, bf16[32,384]{1,0:T(8,128)(2,1)S(1)}, u32[]{:S(2)}, u32[]{:S(2)}) collective-permute-start(bf16[32,384]{1,0:T(8,128)(2,1)} %param.9), channel_id=1, source_target_pairs={{16,256},{256,16},{48,288},{288,48},{80,320},{320,80},{112,352},{3... | collective-permute-start | bytes 73736 | tf_op jit(solution)/shard_map/ppermute | solution.py:104
  12.0 4.8 %collective-permute-start.1 = (bf16[32,384]{1,0:T(8,128)(2,1)}, bf16[32,384]{1,0:T(8,128)(2,1)S(1)}, u32[]{:S(2)}, u32[]{:S(2)}) collective-permute-start(bf16[32,384]{1,0:T(8,128)(2,1)} %param.9), channel_id=1, source_target_pairs={{16,0},{256,272},{48,32},{288,304},{80,64},{320,336},{112,96},{352... | collective-permute-start | bytes 73736 | tf_op jit(solution)/shard_map/ppermute | solution.py:105
  17.8 32.5 %all-to-all-start = ((bf16[16,32,768]{2,1,0:T(8,128)(2,1)}), bf16[16,32,768]{2,1,0:T(8,128)(2,1)S(1)}, u32[]{:S(2)}, u32[]{:S(2)}) async-start(bf16[16,32,768]{2,1,0:T(8,128)(2,1)} %broadcast_in_dim.32), calls=%async_computation | async-start | bytes 1572864 | tf_op jit(solution)/shard_map/all_to_all | solution.py:41
  27.5 22.0 %collective-permute-start.4 = (bf16[384,768]{1,0:T(8,128)(2,1)S(1)}, bf16[384,768]{1,0:T(8,128)(2,1)S(1)}, u32[]{:S(2)}, u32[]{:S(2)}) collective-permute-start(bf16[384,768]{1,0:T(8,128)(2,1)S(1)} %get-tuple-element.23), channel_id=1, source_target_pairs={{256,16},{272,0},{288,48},{304,32},{320,80},{336,64},{352,112},{36... | collective-permute-start | bytes 1769480 | tf_op jit(solution)/shard_map/ppermute | solution.py:118
  28.8 21.5 %collective-permute-start.5 = (bf16[384,768]{1,0:T(8,128)(2,1)S(1)}, bf16[384,768]{1,0:T(8,128)(2,1)S(1)}, u32[]{:S(2)}, u32[]{:S(2)}) collective-permute-start(bf16[384,768]{1,0:T(8,128)(2,1)S(1)} %get-tuple-element.22), channel_id=1, source_target_pairs={{0,16},{16,0},{32,48},{48,32},{64,80},{80,64},{96,112},{112,96},{1... | collective-permute-start | bytes 1769480 | tf_op jit(solution)/shard_map/ppermute | solution.py:112
  30.7 32.0 %collective-permute-start.3 = (bf16[384,768]{1,0:T(8,128)(2,1)S(1)}, bf16[384,768]{1,0:T(8,128)(2,1)}, u32[]{:S(2)}, u32[]{:S(2)}) collective-permute-start(bf16[384,768]{1,0:T(8,128)(2,1)S(1)} %get-tuple-element.23), channel_id=1, source_target_pairs={{256,0},{272,16},{288,32},{304,48},{320,64},{336,80},{352,96},{368... | collective-permute-start | bytes 1769480 | tf_op jit(solution)/shard_map/ppermute | solution.py:117
  66.9 54.8 %all-to-all-start.1 = ((f16[8,72,768]{2,1,0:T(8,128)(2,1)}), f16[8,72,768]{2,1,0:T(8,128)(2,1)S(1)}, u32[]{:S(2)}, u32[]{:S(2)}) async-start(f16[8,72,768]{2,1,0:T(8,128)(2,1)} %concatenate.48), calls=%async_computation.1 | async-start | bytes 1769472 | tf_op jit(solution)/shard_map/all_to_all | solution.py:70
  81.1 109.7 %all-gather.2.cloned.1.call-start = ((), (), s32[]{:S(2)}) async-start(), calls=%async_computation.5 | async-start | bytes 1769472 | tf_op jit(solution)/shard_map/all_gather | solution.py:162
  82.6 37.1 %collective-permute-start.7 = (bf16[32,768]{1,0:T(8,128)(2,1)S(1)}, bf16[32,768]{1,0:T(8,128)(2,1)S(1)}, u32[]{:S(2)}, u32[]{:S(2)}) collective-permute-start(bf16[32,768]{1,0:T(8,128)(2,1)S(1)} %get-tuple-element.10), channel_id=1, source_target_pairs={{16,0},{256,272},{48,32},{288,304},{80,64},{320,336},{112,96},{352... | collective-permute-start | bytes 147464 | tf_op jit(solution)/shard_map/ppermute | solution.py:105
  83.9 35.8 %collective-permute-start.8 = (bf16[32,768]{1,0:T(8,128)(2,1)S(1)}, bf16[32,768]{1,0:T(8,128)(2,1)S(1)}, u32[]{:S(2)}, u32[]{:S(2)}) collective-permute-start(bf16[32,768]{1,0:T(8,128)(2,1)S(1)} %get-tuple-element.11), channel_id=1, source_target_pairs={{16,256},{256,16},{48,288},{288,48},{80,320},{320,80},{112,352},{3... | collective-permute-start | bytes 147464 | tf_op jit(solution)/shard_map/ppermute | solution.py:104
  119.7 10.6 %collective-permute-start.11 = (bf16[64,768]{1,0:T(8,128)(2,1)S(1)}, bf16[64,768]{1,0:T(8,128)(2,1)S(1)}, u32[]{:S(2)}, u32[]{:S(2)}) collective-permute-start(bf16[64,768]{1,0:T(8,128)(2,1)S(1)} %pad_maximum_fusion.1), channel_id=1, source_target_pairs={{16,272},{48,304},{80,336},{112,368},{144,400},{176,432},{208,464}... | collective-permute-start | bytes 294920 | tf_op jit(solution)/shard_map/ppermute | solution.py:145
  120.4 10.0 %collective-permute-start.12 = (bf16[64,768]{1,0:T(8,128)(2,1)S(1)}, bf16[64,768]{1,0:T(8,128)(2,1)S(1)}, u32[]{:S(2)}, u32[]{:S(2)}) collective-permute-start(bf16[64,768]{1,0:T(8,128)(2,1)S(1)} %pad_maximum_fusion.1), channel_id=1, source_target_pairs={{272,256},{304,288},{336,320},{368,352},{400,384},{432,416},{464,4... | collective-permute-start | bytes 294920 | tf_op jit(solution)/shard_map/ppermute | solution.py:146
  122.2 9.9 %collective-permute-start.10 = (bf16[64,768]{1,0:T(8,128)(2,1)S(1)}, bf16[64,768]{1,0:T(8,128)(2,1)S(1)}, u32[]{:S(2)}, u32[]{:S(2)}) collective-permute-start(bf16[64,768]{1,0:T(8,128)(2,1)S(1)} %fusion.20), channel_id=1, source_target_pairs={{272,0},{304,32},{336,64},{368,96},{400,128},{432,160},{464,192},{... | collective-permute-start | bytes 294920 | tf_op jit(solution)/shard_map/ppermute | solution.py:156
  129.0 5.4 %collective-permute-start.9 = (bf16[64,768]{1,0:T(8,128)(2,1)S(1)}, bf16[64,768]{1,0:T(8,128)(2,1)S(1)}, u32[]{:S(2)}, u32[]{:S(2)}) collective-permute-start(bf16[64,768]{1,0:T(8,128)(2,1)S(1)} %fusion.20), channel_id=1, source_target_pairs={{256,0},{288,32},{320,64},{352,96},{384,128},{416,160},{448,192},{... | collective-permute-start | bytes 294920 | tf_op jit(solution)/shard_map/ppermute | solution.py:155
  135.3 5.0 %collective-permute-start.13 = (bf16[32,384]{1,0:T(8,128)(2,1)S(1)}, bf16[32,384]{1,0:T(8,128)(2,1)S(1)}, u32[]{:S(2)}, u32[]{:S(2)}) collective-permute-start(bf16[32,384]{1,0:T(8,128)(2,1)S(1)} %broadcast_select_fusion.18), channel_id=1, source_target_pairs={{0,256},{256,0},{1,257},{257,1},{2,258},{258,2},{3,259},{259,3},{4... | collective-permute-start | bytes 73736 | tf_op jit(solution)/shard_map/ppermute | solution.py:171
  140.3 4.8 %collective-permute-start.14 = (bf16[64,384]{1,0:T(8,128)(2,1)S(1)}, bf16[64,384]{1,0:T(8,128)(2,1)S(1)}, u32[]{:S(2)}, u32[]{:S(2)}) collective-permute-start(bf16[64,384]{1,0:T(8,128)(2,1)S(1)} %pad_maximum_fusion.4), channel_id=1, source_target_pairs={{0,16},{16,0},{32,48},{48,32},{64,80},{80,64},{96,112},{112,96},{1... | collective-permute-start | bytes 147464 | tf_op jit(solution)/shard_map/ppermute | solution.py:167
  146.4 37.6 %all-to-all-start.2 = ((bf16[16,64,768]{2,1,0:T(8,128)(2,1)}), bf16[16,64,768]{2,1,0:T(8,128)(2,1)S(1)}, u32[]{:S(2)}, u32[]{:S(2)}) async-start(bf16[16,64,768]{2,1,0:T(8,128)(2,1)} %broadcast_in_dim.33), calls=%async_computation.2 | async-start | bytes 3145728 | tf_op jit(solution)/shard_map/all_to_all | solution.py:41
  197.9 17.5 %all-to-all-start.3 = ((f32[16,16,128]{2,1,0:T(8,128)}), f32[16,16,128]{2,1,0:T(8,128)S(1)}, u32[]{:S(2)}, u32[]{:S(2)}) async-start(f32[16,16,128]{2,1,0:T(8,128)} %broadcast_in_dim.64), calls=%async_computation.3 | async-start | bytes 262144 | tf_op jit(solution)/shard_map/all_to_all | solution.py:41
  219.0 45.2 %all-to-all-start.4 = ((bf16[16,72,768]{2,1,0:T(8,128)(2,1)}), bf16[16,72,768]{2,1,0:T(8,128)(2,1)S(1)}, u32[]{:S(2)}, u32[]{:S(2)}) async-start(bf16[16,72,768]{2,1,0:T(8,128)(2,1)} %pad_maximum_fusion), calls=%async_computation.4 | async-start | bytes 3538944 | tf_op jit(solution)/shard_map/all_to_all | solution.py:41
  233.7 29.3 %collective-permute-start.18 = (f32[384,768]{1,0:T(8,128)S(1)}, f32[384,768]{1,0:T(8,128)S(1)}, u32[]{:S(2)}, u32[]{:S(2)}) collective-permute-start(f32[384,768]{1,0:T(8,128)S(1)} %slice.127), channel_id=1, source_target_pairs={{0,16},{16,0},{32,48},{48,32},{64,80},{80,64},{96,112},{112,96},{1... | collective-permute-start | bytes 3538952 | tf_op jit(solution)/shard_map/ppermute | solution.py:167
  265.0 9.9 %collective-permute-start.15 = (f32[32,384]{1,0:T(8,128)S(1)}, f32[32,384]{1,0:T(8,128)S(1)}, u32[]{:S(2)}, u32[]{:S(2)}) collective-permute-start(f32[32,384]{1,0:T(8,128)S(1)} %get-tuple-element.30), channel_id=1, source_target_pairs={{0,256},{16,272},{32,288},{48,304},{64,320},{80,336},{96,352},{112... | collective-permute-start | bytes 147464 | tf_op jit(solution)/shard_map/ppermute | solution.py:215
  266.9 8.0 %collective-permute-start.16 = (f32[32,384]{1,0:T(8,128)S(1)}, f32[32,384]{1,0:T(8,128)S(1)}, u32[]{:S(2)}, u32[]{:S(2)}) collective-permute-start(f32[32,384]{1,0:T(8,128)S(1)} %get-tuple-element.29), channel_id=1, source_target_pairs={{0,16},{16,0},{32,48},{48,32},{64,80},{80,64},{96,112},{112,96},{1... | collective-permute-start | bytes 147464 | tf_op jit(solution)/shard_map/ppermute | solution.py:214
  269.9 5.0 %collective-permute-start.17 = (f32[32,384]{1,0:T(8,128)S(1)}, f32[32,384]{1,0:T(8,128)S(1)}, u32[]{:S(2)}, u32[]{:S(2)}) collective-permute-start(f32[32,384]{1,0:T(8,128)S(1)} %get-tuple-element.28), channel_id=1, source_target_pairs={{0,272},{16,256},{32,304},{48,288},{64,336},{80,320},{96,368},{112... | collective-permute-start | bytes 147464 | tf_op jit(solution)/shard_map/ppermute | solution.py:216
  (13 other events, 135.6 us)
Sparse Core Ops, SparseCore 0:
  135.4 55.4 all-gather.1

commit v7 on v6

--- a/solution.py
+++ b/solution.py
@@ -60,11 +60,15 @@
     return out.astype(jnp.bfloat16)
 
 
+def scale_power(top):
+    return jnp.clip(jnp.ceil(jnp.log2(jnp.maximum(top, 1e-30))), -96.0, 96.0)
+
+
 def sum_blocks(partial, axis, groups):
     members = len(groups[0])
     columns = partial.shape[1]
     rows = partial.shape[0] // members
-    power = jnp.clip(jnp.ceil(jnp.log2(jnp.maximum(jnp.max(jnp.abs(partial)), 1e-30))), -96.0, 96.0)
+    power = scale_power(jnp.max(jnp.abs(partial)))
     coded = (partial * jnp.exp2(14.0 - power)).astype(jnp.float16).reshape(members, rows, columns)
     power = jnp.broadcast_to(power, (members, 8, columns)).astype(jnp.float16)
     taken = lax.all_to_all(
@@ -178,12 +182,13 @@
     squares = both * both
     row_both = jnp.sum(squares, axis=1)
     col_local = jnp.sum(squares, axis=0)
-    swapped = neighbour(both[features:])
+    power = scale_power(jnp.sqrt(jnp.sum(row_both[features:])))
+    swapped = neighbour((both[features:] * jnp.exp2(14.0 - power)).astype(jnp.float16))
     row_prev = row_state[0]
     col_prev = col_state[0]
-    scalars = jnp.stack([jnp.sum(row_both), jnp.sum(row_prev)])
+    scalars = jnp.stack([jnp.sum(row_both), jnp.sum(row_prev), power])
     packed = jnp.concatenate(
-        [col_local, row_both[features:], scalars, jnp.zeros((-(half + features + 2) % (8 * LANES),), jnp.float32)]
+        [col_local, row_both[features:], scalars, jnp.zeros((-(half + features + 3) % (8 * LANES),), jnp.float32)]
     ).reshape(-1, LANES)
     taken = spread(packed, "hid").reshape((hid,) + packed.shape)
     over_hid = jnp.sum(taken.reshape((hid // 2, 2) + packed.shape), axis=0).reshape(2, -1)
@@ -191,10 +196,11 @@
     square_sum = over_hid[0, half + features] + over_hid[1, half + features]
     prev_sum = over_hid[0, half + features + 1] + over_hid[1, half + features + 1]
     is_near = lax.broadcasted_iota(jnp.int32, (hid, 1, 1), 0) == lax.axis_index("hid") ^ 1
-    row_near = jnp.sum(
-        jnp.where(is_near, taken[:, half // LANES : (half + features) // LANES], 0.0), axis=0
+    from_near = jnp.sum(
+        jnp.where(is_near, taken[:, half // LANES : (half + features) // LANES + 1], 0.0), axis=0
     ).reshape(-1)
-    row_local = row_both[:features] + row_near
+    row_local = row_both[:features] + from_near[:features]
+    power_near = from_near[features + 2]
 
     my_columns = jnp.where(even, own_tile[:, :half], own_tile[:, half:])
     my_columns, tile_next = lax.optimization_barrier((by_rows(my_columns), by_rows(tile_near)))
@@ -209,7 +215,8 @@
     blocks = jnp.concatenate([input_blocks(my_columns), input_blocks(tile_next)], axis=2)
     extra = thirds(row_local, square_sum)
     blocks = jnp.concatenate([blocks, jnp.broadcast_to(extra[None], (wid,) + extra.shape)], axis=1)
-    over_wid = jnp.sum(exchange(blocks, "wid").astype(jnp.float32), axis=0)
+    blocks = exchange(blocks, "wid")
+    over_wid = jnp.sum(blocks.astype(jnp.float32), axis=0)
     mine, others = over_wid[: 2 * rows, :features], over_wid[: 2 * rows, features:]
     near_sum = lax.ppermute(others[:rows], pair, [(at(0, h), at(0, h ^ 1)) for h in range(hid)])
     over_sum = lax.ppermute(mine[rows:], pair, [(at(0, h), at(1, h)) for h in range(hid)])
@@ -220,6 +227,7 @@
     row_total, square_total = totals[:features], totals[features]
 
     own_half = both[:features]
+    swapped = swapped.astype(jnp.float32) * jnp.exp2(power_near - 14.0)
     gradient = jnp.concatenate(
         [jnp.where(even, own_half, swapped), jnp.where(even, swapped, own_half)], axis=1
     )

time: 284 us -> 278 us (0.979)
  waiting for transfers between devices: 137 us -> 127 us
  other arithmetic: 10.7 us -> 14 us
    ppermute x2, waiting for transfers between devices: 27.9 us -> 13.9 us  [neighbour(): return lax.ppermute(block, 'hid', [(h, h ^ 1) for h in range(hid)])]
    all_to_all x4, waiting for transfers between devices: 29.3 us -> 33.4 us  [exchange(): return lax.all_to_all(blocks, axis, split_axis=0, concat_axis=0, tiled=True)]
  transfers between devices with their start and end apart: 25 -> 25, of which waited for: 12 -> 13; matrix products, arithmetic and copies ran while one was open for 6% -> 6% of each run, Pallas kernels for 0% -> 0%
where the time goes in v7:
time: 278 us; the launch traced here: 277 us
  waiting for transfers between devices  127 us (46%)
  starting transfers between devices  93.6 us (34%)
  between operations  19.9 us (7%)
  other arithmetic  14 us (5%)
  matrix products  12.7 us (5%)
  local copies, waits for them, and re-layouts  9.43 us (3%)
    all_to_all x4, starting transfers between devices, exchange(): return lax.all_to_all(blocks, axis, split_axis=0, concat_axis=0, tiled=True)  42.1 us
    ppermute x2, waiting for transfers between devices, token_blocks(): lax.ppermute(same, pair, beside)  37.8 us
    all_to_all x4, waiting for transfers between devices, exchange(): return lax.all_to_all(blocks, axis, split_axis=0, concat_axis=0, tiled=True)  33.4 us
    ppermute x1, waiting for transfers between devices, shards(): lax.ppermute(own_tile[:, half:], pair, [(at(1, h), at(0, h ^ 1)) for h in...  17.4 us
    all_to_all x1, starting transfers between devices, sum_blocks(): lax.all_to_all(jnp.concatenate([coded, power], axis=1), axis, split_axis=...  14.2 us
    ppermute x2, waiting for transfers between devices, neighbour(): return lax.ppermute(block, 'hid', [(h, h ^ 1) for h in range(hid)])  13.9 us
    ppermute x1, waiting for transfers between devices, shards(): lax.ppermute(own_tile[:, half:], pair, [(at(1, h), at(0, h)) for h in ran...  10.5 us
    ppermute x1, starting transfers between devices, shards(): lax.ppermute(pre_share, pair, [(at(1, h + 1), at(0, h)) for h in evens] +...  6.96 us
  transfers between devices with their start and end apart: 25, of which 13 were waited for; matrix products, arithmetic and copies ran while one was open for 6% of the time, Pallas kernels for 0%

profile of v7, /device:TPU:1, one launch (start us, length us, event | category | flops | bytes accessed | tf_op | source)
XLA Modules:
  0.0 276.6 jit_solution(373162318383319988)
XLA Ops:
  7.2 4.2 %collective-permute-start = (bf16[32,384]{1,0:T(8,128)(2,1)}, bf16[32,384]{1,0:T(8,128)(2,1)S(1)}, u32[]{:S(2)}, u32[]{:S(2)}) collective-permute-start(bf16[32,384]{1,0:T(8,128)(2,1)} %param.9), channel_id=1, source_target_pairs={{0,256},{272,16},{32,288},{304,48},{64,320},{336,80},{96,352},{368... | collective-permute-start | bytes 73736 | tf_op jit(solution)/shard_map/ppermute | solution.py:109
  14.1 2.7 collective-permute-done.1
  17.8 8.8 %all-to-all-start = ((bf16[16,32,768]{2,1,0:T(8,128)(2,1)}), bf16[16,32,768]{2,1,0:T(8,128)(2,1)S(1)}, u32[]{:S(2)}, u32[]{:S(2)}) async-start(bf16[16,32,768]{2,1,0:T(8,128)(2,1)} %broadcast_in_dim.32), calls=%async_computation | async-start | bytes 1572864 | tf_op jit(solution)/shard_map/all_to_all | solution.py:41
  32.0 17.4 %collective-permute-done.4 = bf16[384,768]{1,0:T(8,128)(2,1)S(1)} collective-permute-done((bf16[384,768]{1,0:T(8,128)(2,1)S(1)}, bf16[384,768]{1,0:T(8,128)(2,1)S(1)}, u32[]{:S(2)}, u32[]{:S(2)}) %collective-permute-start.4) | collective-permute-done | bytes 589856 | tf_op jit(solution)/shard_map/ppermute | solution.py:122
  52.2 10.5 %collective-permute-done.3 = bf16[384,768]{1,0:T(8,128)(2,1)} collective-permute-done((bf16[384,768]{1,0:T(8,128)(2,1)S(1)}, bf16[384,768]{1,0:T(8,128)(2,1)}, u32[]{:S(2)}, u32[]{:S(2)}) %collective-permute-start.3) | collective-permute-done | bytes 589856 | tf_op jit(solution)/shard_map/ppermute | solution.py:121
  66.9 14.2 %all-to-all-start.1 = ((f16[8,72,768]{2,1,0:T(8,128)(2,1)}), f16[8,72,768]{2,1,0:T(8,128)(2,1)S(1)}, u32[]{:S(2)}, u32[]{:S(2)}) async-start(f16[8,72,768]{2,1,0:T(8,128)(2,1)} %concatenate.48), calls=%async_computation.1 | async-start | bytes 1769472 | tf_op jit(solution)/shard_map/all_to_all | solution.py:74
  84.6 35.1 %collective-permute-done.7 = bf16[32,768]{1,0:T(8,128)(2,1)S(1)} collective-permute-done((bf16[32,768]{1,0:T(8,128)(2,1)S(1)}, bf16[32,768]{1,0:T(8,128)(2,1)S(1)}, u32[]{:S(2)}, u32[]{:S(2)}) %collective-permute-start.7) | collective-permute-done | bytes 49184 | tf_op jit(solution)/shard_map/ppermute | solution.py:109
  122.2 7.0 %collective-permute-start.10 = (bf16[64,768]{1,0:T(8,128)(2,1)S(1)}, bf16[64,768]{1,0:T(8,128)(2,1)S(1)}, u32[]{:S(2)}, u32[]{:S(2)}) collective-permute-start(bf16[64,768]{1,0:T(8,128)(2,1)S(1)} %fusion.21), channel_id=1, source_target_pairs={{272,0},{304,32},{336,64},{368,96},{400,128},{432,160},{464,192},{... | collective-permute-start | bytes 294920 | tf_op jit(solution)/shard_map/ppermute | solution.py:160
  137.4 3.2 %collective-permute-done.13 = bf16[32,384]{1,0:T(8,128)(2,1)S(1)} collective-permute-done((bf16[32,384]{1,0:T(8,128)(2,1)S(1)}, bf16[32,384]{1,0:T(8,128)(2,1)S(1)}, u32[]{:S(2)}, u32[]{:S(2)}) %collective-permute-start.13) | collective-permute-done | bytes 24608 | tf_op jit(solution)/shard_map/ppermute | solution.py:175
  142.5 2.9 %collective-permute-done.14 = bf16[64,384]{1,0:T(8,128)(2,1)S(1)} collective-permute-done((bf16[64,384]{1,0:T(8,128)(2,1)S(1)}, bf16[64,384]{1,0:T(8,128)(2,1)S(1)}, u32[]{:S(2)}, u32[]{:S(2)}) %collective-permute-start.14) | collective-permute-done | bytes 49184 | tf_op jit(solution)/shard_map/ppermute | solution.py:171
  146.8 14.6 %all-to-all-start.2 = ((bf16[16,64,768]{2,1,0:T(8,128)(2,1)}), bf16[16,64,768]{2,1,0:T(8,128)(2,1)S(1)}, u32[]{:S(2)}, u32[]{:S(2)}) async-start(bf16[16,64,768]{2,1,0:T(8,128)(2,1)} %broadcast_in_dim.33), calls=%async_computation.2 | async-start | bytes 3145728 | tf_op jit(solution)/shard_map/all_to_all | solution.py:41
  162.1 22.0 %all-to-all-done.2 = bf16[16,64,768]{2,1,0:T(8,128)(2,1)S(1)} async-done(((bf16[16,64,768]{2,1,0:T(8,128)(2,1)}), bf16[16,64,768]{2,1,0:T(8,128)(2,1)S(1)}, u32[]{:S(2)}, u32[]{:S(2)}) %all-to-all-start.2) | async-done | bytes 1572896 | tf_op jit(solution)/shard_map/all_to_all | solution.py:41
  184.2 6.6 %all-gather.2.cloned.1.call-done = bf16[1024,768]{1,0:T(8,128)(2,1)} async-done(((bf16[128,768]{1,0:T(8,128)(2,1)}), bf16[1024,768]{1,0:T(8,128)(2,1)}) %all-gather.2.cloned.1.call-update) | async-done | bytes 1572880 | tf_op jit(solution)/shard_map/all_gather | solution.py:166
  190.9 5.1 %multiply_reduce_fusion = (f32[]{:T(128)}, f32[768]{0:T(1024)S(1)}, f32[768]{0:T(1024)S(1)}, f32[768,768]{1,0:T(8,128)}) fusion(bf16[1024,768]{1,0:T(8,128)(2,1)S(1)} %bitcast.53, bf16[1024,768]{1,0:T(8,128)(2,1)} %all-gather.2.cloned.1.call-done), kind=kOutput, calls=%fused_computation.2 | convolution fusion | flops 1210317312 | bytes 5511172 | tf_op jit(solution)/shard_map/dot_general | solution.py:35
  199.4 5.5 %all-to-all-start.3 = ((f32[16,16,128]{2,1,0:T(8,128)}), f32[16,16,128]{2,1,0:T(8,128)S(1)}, u32[]{:S(2)}, u32[]{:S(2)}) async-start(f32[16,16,128]{2,1,0:T(8,128)} %broadcast_in_dim.64), calls=%async_computation.3 | async-start | bytes 262144 | tf_op jit(solution)/shard_map/all_to_all | solution.py:41
  204.9 2.5 convolution_convert_fusion.1
  209.6 7.2 %all-to-all-done.3 = f32[16,16,128]{2,1,0:T(8,128)S(1)} async-done(((f32[16,16,128]{2,1,0:T(8,128)}), f32[16,16,128]{2,1,0:T(8,128)S(1)}, u32[]{:S(2)}, u32[]{:S(2)}) %all-to-all-start.3) | async-done | bytes 131104 | tf_op jit(solution)/shard_map/all_to_all | solution.py:41
  220.4 13.2 %all-to-all-start.4 = ((bf16[16,72,768]{2,1,0:T(8,128)(2,1)}), bf16[16,72,768]{2,1,0:T(8,128)(2,1)S(1)}, u32[]{:S(2)}, u32[]{:S(2)}) async-start(bf16[16,72,768]{2,1,0:T(8,128)(2,1)} %pad_maximum_fusion), calls=%async_computation.4 | async-start | bytes 3538944 | tf_op jit(solution)/shard_map/all_to_all | solution.py:41
  235.0 3.0 %collective-permute-start.18 = (f16[384,768]{1,0:T(8,128)(2,1)S(1)}, f16[384,768]{1,0:T(8,128)(2,1)S(1)}, u32[]{:S(2)}, u32[]{:S(2)}) collective-permute-start(f16[384,768]{1,0:T(8,128)(2,1)S(1)} %fusion), channel_id=1, source_target_pairs={{0,16},{16,0},{32,48},{48,32},{64,80},{80,64},{96,112},{112,96},{1... | collective-permute-start | bytes 1769480 | tf_op jit(solution)/shard_map/ppermute | solution.py:171
  240.7 11.0 %collective-permute-done.18 = f16[384,768]{1,0:T(8,128)(2,1)S(1)} collective-permute-done((f16[384,768]{1,0:T(8,128)(2,1)S(1)}, f16[384,768]{1,0:T(8,128)(2,1)S(1)}, u32[]{:S(2)}, u32[]{:S(2)}) %collective-permute-start.18) | collective-permute-done | bytes 589856 | tf_op jit(solution)/shard_map/ppermute | solution.py:171
  251.7 2.5 select_bitcast_fusion.1
  254.2 4.2 %all-to-all-done.4 = bf16[16,72,768]{2,1,0:T(8,128)(2,1)S(1)} async-done(((bf16[16,72,768]{2,1,0:T(8,128)(2,1)}), bf16[16,72,768]{2,1,0:T(8,128)(2,1)S(1)}, u32[]{:S(2)}, u32[]{:S(2)}) %all-to-all-start.4) | async-done | bytes 1769504 | tf_op jit(solution)/shard_map/all_to_all | solution.py:41
  261.1 3.0 %collective-permute-start.16 = (f32[32,384]{1,0:T(8,128)S(1)}, f32[32,384]{1,0:T(8,128)S(1)}, u32[]{:S(2)}, u32[]{:S(2)}) collective-permute-start(f32[32,384]{1,0:T(8,128)S(1)} %get-tuple-element.29), channel_id=1, source_target_pairs={{0,16},{16,0},{32,48},{48,32},{64,80},{80,64},{96,112},{112,96},{1... | collective-permute-start | bytes 147464 | tf_op jit(solution)/shard_map/ppermute | solution.py:221
  266.0 3.1 %maximum_multiply_fusion = f32[1,384,1536]{2,1,0:T(8,128)} fusion(f32[1,384,768]{2,1,0:T(8,128)} %get-tuple-element.20, f32[1,384,768]{2,1,0:T(8,128)S(1)} %get-tuple-element.19, f32[]{:T(128)S(6)} %add.79, f32[1536]{0:T(1024)S(1)} %add_reduce_fusion, f32[384]{0:T(512)S(1)} %multiply_add_fusion), kind=kLoop, calls=%fused_computation.1 | loop fusion | flops 2359296 | bytes 4726276 | tf_op jit(solution)/shard_map/mul | solution.py:237
  (109 shorter events, 47.2 us)
Async XLA Ops:
  7.2 6.2 %collective-permute-start = (bf16[32,384]{1,0:T(8,128)(2,1)}, bf16[32,384]{1,0:T(8,128)(2,1)S(1)}, u32[]{:S(2)}, u32[]{:S(2)}) collective-permute-start(bf16[32,384]{1,0:T(8,128)(2,1)} %param.9), channel_id=1, source_target_pairs={{0,256},{272,16},{32,288},{304,48},{64,320},{336,80},{96,352},{368... | collective-permute-start | bytes 73736 | tf_op jit(solution)/shard_map/ppermute | solution.py:109
  11.3 5.5 %collective-permute-start.2 = (bf16[32,384]{1,0:T(8,128)(2,1)}, bf16[32,384]{1,0:T(8,128)(2,1)S(1)}, u32[]{:S(2)}, u32[]{:S(2)}) collective-permute-start(bf16[32,384]{1,0:T(8,128)(2,1)} %param.9), channel_id=1, source_target_pairs={{16,256},{256,16},{48,288},{288,48},{80,320},{320,80},{112,352},{3... | collective-permute-start | bytes 73736 | tf_op jit(solution)/shard_map/ppermute | solution.py:108
  12.0 4.8 %collective-permute-start.1 = (bf16[32,384]{1,0:T(8,128)(2,1)}, bf16[32,384]{1,0:T(8,128)(2,1)S(1)}, u32[]{:S(2)}, u32[]{:S(2)}) collective-permute-start(bf16[32,384]{1,0:T(8,128)(2,1)} %param.9), channel_id=1, source_target_pairs={{16,0},{256,272},{48,32},{288,304},{80,64},{320,336},{112,96},{352... | collective-permute-start | bytes 73736 | tf_op jit(solution)/shard_map/ppermute | solution.py:109
  17.8 32.5 %all-to-all-start = ((bf16[16,32,768]{2,1,0:T(8,128)(2,1)}), bf16[16,32,768]{2,1,0:T(8,128)(2,1)S(1)}, u32[]{:S(2)}, u32[]{:S(2)}) async-start(bf16[16,32,768]{2,1,0:T(8,128)(2,1)} %broadcast_in_dim.32), calls=%async_computation | async-start | bytes 1572864 | tf_op jit(solution)/shard_map/all_to_all | solution.py:41
  27.5 21.9 %collective-permute-start.4 = (bf16[384,768]{1,0:T(8,128)(2,1)S(1)}, bf16[384,768]{1,0:T(8,128)(2,1)S(1)}, u32[]{:S(2)}, u32[]{:S(2)}) collective-permute-start(bf16[384,768]{1,0:T(8,128)(2,1)S(1)} %get-tuple-element.23), channel_id=1, source_target_pairs={{256,16},{272,0},{288,48},{304,32},{320,80},{336,64},{352,112},{36... | collective-permute-start | bytes 1769480 | tf_op jit(solution)/shard_map/ppermute | solution.py:122
  28.8 21.5 %collective-permute-start.5 = (bf16[384,768]{1,0:T(8,128)(2,1)S(1)}, bf16[384,768]{1,0:T(8,128)(2,1)S(1)}, u32[]{:S(2)}, u32[]{:S(2)}) collective-permute-start(bf16[384,768]{1,0:T(8,128)(2,1)S(1)} %get-tuple-element.22), channel_id=1, source_target_pairs={{0,16},{16,0},{32,48},{48,32},{64,80},{80,64},{96,112},{112,96},{1... | collective-permute-start | bytes 1769480 | tf_op jit(solution)/shard_map/ppermute | solution.py:116
  30.7 31.9 %collective-permute-start.3 = (bf16[384,768]{1,0:T(8,128)(2,1)S(1)}, bf16[384,768]{1,0:T(8,128)(2,1)}, u32[]{:S(2)}, u32[]{:S(2)}) collective-permute-start(bf16[384,768]{1,0:T(8,128)(2,1)S(1)} %get-tuple-element.23), channel_id=1, source_target_pairs={{256,0},{272,16},{288,32},{304,48},{320,64},{336,80},{352,96},{368... | collective-permute-start | bytes 1769480 | tf_op jit(solution)/shard_map/ppermute | solution.py:121
  66.9 54.8 %all-to-all-start.1 = ((f16[8,72,768]{2,1,0:T(8,128)(2,1)}), f16[8,72,768]{2,1,0:T(8,128)(2,1)S(1)}, u32[]{:S(2)}, u32[]{:S(2)}) async-start(f16[8,72,768]{2,1,0:T(8,128)(2,1)} %concatenate.48), calls=%async_computation.1 | async-start | bytes 1769472 | tf_op jit(solution)/shard_map/all_to_all | solution.py:74
  81.1 109.7 %all-gather.2.cloned.1.call-start = ((), (), s32[]{:S(2)}) async-start(), calls=%async_computation.5 | async-start | bytes 1769472 | tf_op jit(solution)/shard_map/all_gather | solution.py:166
  82.6 37.1 %collective-permute-start.7 = (bf16[32,768]{1,0:T(8,128)(2,1)S(1)}, bf16[32,768]{1,0:T(8,128)(2,1)S(1)}, u32[]{:S(2)}, u32[]{:S(2)}) collective-permute-start(bf16[32,768]{1,0:T(8,128)(2,1)S(1)} %get-tuple-element.10), channel_id=1, source_target_pairs={{16,0},{256,272},{48,32},{288,304},{80,64},{320,336},{112,96},{352... | collective-permute-start | bytes 147464 | tf_op jit(solution)/shard_map/ppermute | solution.py:109
  83.9 35.8 %collective-permute-start.8 = (bf16[32,768]{1,0:T(8,128)(2,1)S(1)}, bf16[32,768]{1,0:T(8,128)(2,1)S(1)}, u32[]{:S(2)}, u32[]{:S(2)}) collective-permute-start(bf16[32,768]{1,0:T(8,128)(2,1)S(1)} %get-tuple-element.11), channel_id=1, source_target_pairs={{16,256},{256,16},{48,288},{288,48},{80,320},{320,80},{112,352},{3... | collective-permute-start | bytes 147464 | tf_op jit(solution)/shard_map/ppermute | solution.py:108
  119.7 10.8 %collective-permute-start.11 = (bf16[64,768]{1,0:T(8,128)(2,1)S(1)}, bf16[64,768]{1,0:T(8,128)(2,1)S(1)}, u32[]{:S(2)}, u32[]{:S(2)}) collective-permute-start(bf16[64,768]{1,0:T(8,128)(2,1)S(1)} %pad_maximum_fusion.1), channel_id=1, source_target_pairs={{16,272},{48,304},{80,336},{112,368},{144,400},{176,432},{208,464}... | collective-permute-start | bytes 294920 | tf_op jit(solution)/shard_map/ppermute | solution.py:149
  120.4 10.1 %collective-permute-start.12 = (bf16[64,768]{1,0:T(8,128)(2,1)S(1)}, bf16[64,768]{1,0:T(8,128)(2,1)S(1)}, u32[]{:S(2)}, u32[]{:S(2)}) collective-permute-start(bf16[64,768]{1,0:T(8,128)(2,1)S(1)} %pad_maximum_fusion.1), channel_id=1, source_target_pairs={{272,256},{304,288},{336,320},{368,352},{400,384},{432,416},{464,4... | collective-permute-start | bytes 294920 | tf_op jit(solution)/shard_map/ppermute | solution.py:150
  122.2 9.9 %collective-permute-start.10 = (bf16[64,768]{1,0:T(8,128)(2,1)S(1)}, bf16[64,768]{1,0:T(8,128)(2,1)S(1)}, u32[]{:S(2)}, u32[]{:S(2)}) collective-permute-start(bf16[64,768]{1,0:T(8,128)(2,1)S(1)} %fusion.21), channel_id=1, source_target_pairs={{272,0},{304,32},{336,64},{368,96},{400,128},{432,160},{464,192},{... | collective-permute-start | bytes 294920 | tf_op jit(solution)/shard_map/ppermute | solution.py:160
  129.2 5.4 %collective-permute-start.9 = (bf16[64,768]{1,0:T(8,128)(2,1)S(1)}, bf16[64,768]{1,0:T(8,128)(2,1)S(1)}, u32[]{:S(2)}, u32[]{:S(2)}) collective-permute-start(bf16[64,768]{1,0:T(8,128)(2,1)S(1)} %fusion.21), channel_id=1, source_target_pairs={{256,0},{288,32},{320,64},{352,96},{384,128},{416,160},{448,192},{... | collective-permute-start | bytes 294920 | tf_op jit(solution)/shard_map/ppermute | solution.py:159
  135.4 5.1 %collective-permute-start.13 = (bf16[32,384]{1,0:T(8,128)(2,1)S(1)}, bf16[32,384]{1,0:T(8,128)(2,1)S(1)}, u32[]{:S(2)}, u32[]{:S(2)}) collective-permute-start(bf16[32,384]{1,0:T(8,128)(2,1)S(1)} %broadcast_select_fusion.18), channel_id=1, source_target_pairs={{0,256},{256,0},{1,257},{257,1},{2,258},{258,2},{3,259},{259,3},{4... | collective-permute-start | bytes 73736 | tf_op jit(solution)/shard_map/ppermute | solution.py:175
  140.6 4.8 %collective-permute-start.14 = (bf16[64,384]{1,0:T(8,128)(2,1)S(1)}, bf16[64,384]{1,0:T(8,128)(2,1)S(1)}, u32[]{:S(2)}, u32[]{:S(2)}) collective-permute-start(bf16[64,384]{1,0:T(8,128)(2,1)S(1)} %pad_maximum_fusion.4), channel_id=1, source_target_pairs={{0,16},{16,0},{32,48},{48,32},{64,80},{80,64},{96,112},{112,96},{1... | collective-permute-start | bytes 147464 | tf_op jit(solution)/shard_map/ppermute | solution.py:171
  146.8 37.3 %all-to-all-start.2 = ((bf16[16,64,768]{2,1,0:T(8,128)(2,1)}), bf16[16,64,768]{2,1,0:T(8,128)(2,1)S(1)}, u32[]{:S(2)}, u32[]{:S(2)}) async-start(bf16[16,64,768]{2,1,0:T(8,128)(2,1)} %broadcast_in_dim.33), calls=%async_computation.2 | async-start | bytes 3145728 | tf_op jit(solution)/shard_map/all_to_all | solution.py:41
  199.4 17.5 %all-to-all-start.3 = ((f32[16,16,128]{2,1,0:T(8,128)}), f32[16,16,128]{2,1,0:T(8,128)S(1)}, u32[]{:S(2)}, u32[]{:S(2)}) async-start(f32[16,16,128]{2,1,0:T(8,128)} %broadcast_in_dim.64), calls=%async_computation.3 | async-start | bytes 262144 | tf_op jit(solution)/shard_map/all_to_all | solution.py:41
  220.4 38.0 %all-to-all-start.4 = ((bf16[16,72,768]{2,1,0:T(8,128)(2,1)}), bf16[16,72,768]{2,1,0:T(8,128)(2,1)S(1)}, u32[]{:S(2)}, u32[]{:S(2)}) async-start(bf16[16,72,768]{2,1,0:T(8,128)(2,1)} %pad_maximum_fusion), calls=%async_computation.4 | async-start | bytes 3538944 | tf_op jit(solution)/shard_map/all_to_all | solution.py:41
  235.0 16.7 %collective-permute-start.18 = (f16[384,768]{1,0:T(8,128)(2,1)S(1)}, f16[384,768]{1,0:T(8,128)(2,1)S(1)}, u32[]{:S(2)}, u32[]{:S(2)}) collective-permute-start(f16[384,768]{1,0:T(8,128)(2,1)S(1)} %fusion), channel_id=1, source_target_pairs={{0,16},{16,0},{32,48},{48,32},{64,80},{80,64},{96,112},{112,96},{1... | collective-permute-start | bytes 1769480 | tf_op jit(solution)/shard_map/ppermute | solution.py:171
  259.2 9.9 %collective-permute-start.15 = (f32[32,384]{1,0:T(8,128)S(1)}, f32[32,384]{1,0:T(8,128)S(1)}, u32[]{:S(2)}, u32[]{:S(2)}) collective-permute-start(f32[32,384]{1,0:T(8,128)S(1)} %get-tuple-element.30), channel_id=1, source_target_pairs={{0,256},{16,272},{32,288},{48,304},{64,320},{80,336},{96,352},{112... | collective-permute-start | bytes 147464 | tf_op jit(solution)/shard_map/ppermute | solution.py:222
  261.1 8.0 %collective-permute-start.16 = (f32[32,384]{1,0:T(8,128)S(1)}, f32[32,384]{1,0:T(8,128)S(1)}, u32[]{:S(2)}, u32[]{:S(2)}) collective-permute-start(f32[32,384]{1,0:T(8,128)S(1)} %get-tuple-element.29), channel_id=1, source_target_pairs={{0,16},{16,0},{32,48},{48,32},{64,80},{80,64},{96,112},{112,96},{1... | collective-permute-start | bytes 147464 | tf_op jit(solution)/shard_map/ppermute | solution.py:221
  264.1 5.0 %collective-permute-start.17 = (f32[32,384]{1,0:T(8,128)S(1)}, f32[32,384]{1,0:T(8,128)S(1)}, u32[]{:S(2)}, u32[]{:S(2)}) collective-permute-start(f32[32,384]{1,0:T(8,128)S(1)} %get-tuple-element.28), channel_id=1, source_target_pairs={{0,272},{16,256},{32,304},{48,288},{64,336},{80,320},{96,368},{112... | collective-permute-start | bytes 147464 | tf_op jit(solution)/shard_map/ppermute | solution.py:223
  (12 other events, 107.4 us)
Sparse Core Ops, SparseCore 0:
  135.5 55.2 all-gather.1

commit v8 on v4

--- a/solution.py
+++ b/solution.py
@@ -1,7 +1,9 @@
 import jax
 import jax.numpy as jnp
 from jax import lax
+from jax.experimental.layout import Layout, with_layout_constraint
 from jax.sharding import PartitionSpec as P
+
 
 D = 6144
 FF = 24576
@@ -23,6 +25,10 @@
 
 def gelu_slope(pre):
     return normal_cdf(pre) + pre * jnp.exp(-0.5 * pre * pre) * inv_root_tau
+
+
+def by_rows(block):
+    return with_layout_constraint(block, Layout(major_to_minor=(0, 1)))
 
 
 def contract(left, right):
@@ -53,11 +59,15 @@
     return out.astype(jnp.bfloat16)
 
 
+def scale_power(top):
+    return jnp.clip(jnp.ceil(jnp.log2(jnp.maximum(top, 1e-30))), -96.0, 96.0)
+
+
 def sum_blocks(partial, axis, groups):
     members = len(groups[0])
     columns = partial.shape[1]
     rows = partial.shape[0] // members
-    power = jnp.clip(jnp.ceil(jnp.log2(jnp.maximum(jnp.max(jnp.abs(partial)), 1e-30))), -96.0, 96.0)
+    power = scale_power(jnp.max(jnp.abs(partial)))
     coded = (partial * jnp.exp2(14.0 - power)).astype(jnp.float16).reshape(members, rows, columns)
     power = jnp.broadcast_to(power, (members, 8, columns)).astype(jnp.float16)
     taken = lax.all_to_all(
@@ -93,21 +103,33 @@
     rings = [list(range(p, hid, 2)) for p in range(2)]
 
     def token_blocks(same, other):
-        own = jnp.where(home, same, lax.ppermute(other, pair, over))
-        near = lax.ppermute(same, pair, beside)
+        same, other = lax.optimization_barrier((same, other))
         far = lax.ppermute(other, pair, across)
-        return own, jnp.where(home, near, far)
-
-    grad_pair = jnp.concatenate(token_blocks(grad_out, grad_out), axis=1)
-    tile_near = lax.ppermute(own_tile[:, :half], pair, [(at(1, h), at(1, h ^ 1)) for h in range(hid)])
+        return same, lax.ppermute(other, pair, over), lax.ppermute(same, pair, beside), far
+
+    def pick(blocks, columns):
+        same, there, near, far = (block[:, columns] for block in blocks)
+        return jnp.where(home, same, there), jnp.where(home, near, far)
+
+    tile_near = lax.ppermute(
+        own_tile[:, :half], pair, [(at(1, h), at(1, h ^ 1)) for h in range(hid)]
+    )
     tile_over = lax.ppermute(own_tile[:, half:], pair, [(at(1, h), at(0, h)) for h in range(hid)])
-    tile_far = lax.ppermute(own_tile[:, half:], pair, [(at(1, h), at(0, h ^ 1)) for h in range(hid)])
-    grad_half = spread(grad_pair, "wid")
-    pre_own, pre_next = token_blocks(
-        jnp.where(first, preact[:, half:], preact[:, :half]),
-        jnp.where(first, preact[:, :half], preact[:, half:]),
-    )
-    grad_half, pre_own, pre_next = lax.optimization_barrier((grad_half, pre_own, pre_next))
+    tile_far = lax.ppermute(
+        own_tile[:, half:], pair, [(at(1, h), at(0, h ^ 1)) for h in range(hid)]
+    )
+    blocks = token_blocks(
+        jnp.concatenate([grad_out, jnp.where(first, preact[:, half:], preact[:, :half])], axis=1),
+        jnp.concatenate([grad_out, jnp.where(first, preact[:, :half], preact[:, half:])], axis=1),
+    )
+    grad_half = spread(jnp.concatenate(pick(blocks, slice(features)), axis=1), "wid")
+    pre_own, pre_next = pick(blocks, slice(features, None))
+    pre_half = jnp.concatenate(
+        [jnp.where(even, pre_own, pre_next), jnp.where(even, pre_next, pre_own)]
+    )
+    pre_float = pre_half.astype(jnp.float32)
+    act_half = gelu_value(pre_float).astype(jnp.bfloat16)
+    acts = lax.all_gather(act_half, "hid", axis=0, tiled=True)
     hidden_part = jnp.dot(
         grad_half[:, :features],
         jnp.where(first, tile_over, own_tile[:, :half]),
@@ -118,31 +140,44 @@
         preferred_element_type=jnp.float32,
     )
     hidden_share = sum_blocks(hidden_part, "hid", rings)
-    pre_half = jnp.concatenate(
-        [jnp.where(even, pre_own, pre_next), jnp.where(even, pre_next, pre_own)]
-    )
-    pre_taken = lax.ppermute(pre_half, "section", [(0, 1)])
-    act_share = gelu_value(
-        jnp.concatenate([pre_half, pre_taken], axis=1).astype(jnp.float32)
-    ).astype(jnp.bfloat16)
-    pre_share = (hidden_share * gelu_slope(pre_half.astype(jnp.float32))).astype(jnp.bfloat16)
-    pre_share = jnp.concatenate(
-        [lax.ppermute(pre_share, "section", [(1, 0)]), pre_share], axis=1
-    )
-    right = lax.all_gather(jnp.where(first, pre_share, act_share), "hid", axis=0, tiled=True)
-
-    kept = jnp.where(first, inputs, grad_out)
-    given = jnp.where(first, grad_out, inputs)
-    taken = lax.ppermute(given, "section", [(0, 1), (1, 0)])
-    left_own = jnp.concatenate([jnp.where(first, kept, taken), jnp.where(first, taken, kept)])
+    hidden_share, acts = lax.optimization_barrier((hidden_share, acts))
+    pre_share = (hidden_share * gelu_slope(pre_float)).astype(jnp.bfloat16)
+    pre_share, up_left, down_left = lax.optimization_barrier((pre_share, inputs, grad_out))
+    pres = lax.all_gather(pre_share, "hid", axis=0, tiled=True)
+
+    def other_section(block):
+        return lax.ppermute(block, "section", [(0, 1), (1, 0)])
+
+    mine = jnp.concatenate([up_left, down_left], axis=1)
+    taken = other_section(mine)
+    tile_up = lax.ppermute(own_tile[:, :half], "section", [(0, 1)])
+    left_own = jnp.concatenate([jnp.where(first, mine, taken), jnp.where(first, taken, mine)])
     left = jnp.swapaxes(
-        spread(left_own, "wid").reshape(wid // 2, 2, 2, rows, features), 1, 2
-    ).reshape(2 * wid * rows, features)
-
-    gradient = contract(left, right)
-    squares = gradient * gradient
-    row_local = jnp.sum(squares, axis=1)
-    col_local = jnp.sum(squares, axis=0)
+        spread(left_own, "wid").reshape(wid // 2, 2, 2, rows, 2 * features), 1, 2
+    ).reshape(2 * wid * rows, 2 * features)
+
+    def half_gradient(left_side, right_side):
+        grad = by_rows(contract(left_side, right_side))
+        squares = grad * grad
+        row_sums, col_sums = jnp.sum(squares, axis=1), jnp.sum(squares, axis=0)
+        return grad, row_sums, col_sums, scale_power(jnp.sqrt(jnp.sum(row_sums)))
+
+    def coded(grad, power):
+        return (grad * jnp.exp2(14.0 - power)).astype(jnp.float16)
+
+    down = half_gradient(left[:, features:], acts)
+    down_taken = lax.ppermute(coded(down[0], down[3]), "section", [(0, 1)])
+    up = half_gradient(left[:, :features], pres)
+    kept = [jnp.where(first, x, y) for x, y in zip(up, down)]
+    given = [jnp.where(first, y, x) for x, y in zip(up[1:], down[1:])]
+    sums = jnp.concatenate([given[1], given[0], jnp.broadcast_to(given[2], (LANES,))])
+    sums = other_section(sums.reshape(-1, LANES)).reshape(-1)
+    up_taken = lax.ppermute(coded(up[0], up[3]), "section", [(1, 0)])
+    row_local = kept[1] + sums[half : half + features]
+    col_local = jnp.concatenate(
+        [jnp.where(first, sums[:half], kept[2]), jnp.where(first, kept[2], sums[:half])]
+    )
+    power = sums[half + features]
     row_prev = row_state[0]
     col_prev = col_state[0]
     scalars = jnp.stack([jnp.sum(row_local), jnp.sum(row_prev)])
@@ -155,7 +190,10 @@
     square_sum, prev_sum = over_hid[hidden], over_hid[hidden + 1]
 
     partial = lax.dot_general(
-        right, own_tile, (((1,), (1,)), ((), ())), preferred_element_type=jnp.float32
+        pres,
+        by_rows(jnp.where(first, own_tile[:, half:], tile_up)),
+        (((1,), (1,)), ((), ())),
+        preferred_element_type=jnp.float32,
     ).astype(jnp.bfloat16)
     blocks = jnp.swapaxes(partial.reshape(wid // 2, 2, 2, rows, features), 1, 2)
     extra = thirds(row_local, square_sum)
@@ -163,14 +201,18 @@
         [blocks.reshape(wid, 2 * rows, features), jnp.broadcast_to(extra[None], (wid,) + extra.shape)],
         axis=1,
     )
-    over_wid = jnp.sum(exchange(blocks, "wid").astype(jnp.float32), axis=0)
-    input_sum = jnp.where(
-        first, over_wid[:rows], lax.ppermute(over_wid[rows : 2 * rows], "section", [(0, 1)])
-    )
+    blocks = exchange(blocks, "wid")
+    over_wid = jnp.sum(blocks.astype(jnp.float32), axis=0)
+    low, high = over_wid[:rows], over_wid[rows : 2 * rows]
+    input_sum = jnp.where(first, low, high) + other_section(jnp.where(first, high, low))
     input_grad = input_sum + grad_out.astype(jnp.float32)
     row_total = jnp.sum(over_wid[2 * rows : 2 * rows + 8], axis=0)
     square_total = jnp.sum(over_wid[2 * rows + 8 :, 0])
 
+    swapped = jnp.where(first, up_taken, down_taken).astype(jnp.float32) * jnp.exp2(power - 14.0)
+    gradient = jnp.concatenate(
+        [jnp.where(first, swapped, kept[0]), jnp.where(first, kept[0], swapped)], axis=1
+    )
     row_moment = decay_rate * row_prev + (1.0 - decay_rate) / FF * row_total
     col_moment = decay_rate * col_prev + (1.0 - decay_rate) / D * col_total
     row_mean = decay_rate / D * prev_sum + (1.0 - decay_rate) / FF / D * square_total
@@ -187,6 +229,7 @@
         P("section", "hid"),
         P("section", "wid"),
     )
+
     return jax.shard_map(
         shards,
         mesh=mesh,

time: 274 us -> 318 us (1.16)
  waiting for transfers between devices: 139 us -> 168 us
  other arithmetic: 9.81 us -> 19.3 us
  local copies, waits for them, and re-layouts: 7.24 us -> 11.4 us
    ppermute x1, waiting for transfers between devices: 0.01 us -> 17.9 us  [shards(): lax.ppermute(own_tile[:, half:], pair, [(at(1, h), at(0, h ^ 1)) for h in...]
    ppermute x8, waiting for transfers between devices: 14.4 us -> 7.41 us  [the longest x1 4.08 us: token_blocks(): lax.ppermute(same, pair, beside)]
    ppermute x1, waiting for transfers between devices: 5.95 us -> 12.6 us  [shards(): lax.ppermute(own_tile[:, half:], pair, [(at(1, h), at(0, h)) for h in ran...]
    all_to_all x4, starting transfers between devices: 43.1 us -> 49.4 us  [exchange(): return lax.all_to_all(blocks, axis, split_axis=0, concat_axis=0, tiled=True)]
    ppermute x8, starting transfers between devices: 24.9 us -> 19.2 us  [the longest x3 8.03 us: other_section(): return lax.ppermute(block, 'section', [(0, 1), (1, 0)])]
    all_gather x1 -> x2, waiting for transfers between devices: 53 us -> 57.4 us  [the longest x1 43.5 us: shards(): acts = lax.all_gather(act_half, 'hid', axis=0, tiled=True)]
    all_to_all x1, waiting for transfers between devices: 29.3 us -> 33.6 us  [sum_blocks(): lax.all_to_all(jnp.concatenate([coded, power], axis=1), axis, split_axis=...]
  transfers between devices with their start and end apart: 19 -> 19, of which waited for: 9 -> 11; matrix products, arithmetic and copies ran while one was open for 5% -> 10% of each run, Pallas kernels for 0% -> 0%
where the time goes in v8:
time: 318 us; the launch traced here: 316 us
  waiting for transfers between devices  168 us (53%)
  starting transfers between devices  88 us (28%)
  other arithmetic  19.3 us (6%)
  between operations  18.9 us (6%)
  local copies, waits for them, and re-layouts  11.4 us (4%)
  matrix products  10.9 us (3%)
    all_to_all x4, starting transfers between devices, exchange(): return lax.all_to_all(blocks, axis, split_axis=0, concat_axis=0, tiled=True)  49.4 us
    all_gather x1, waiting for transfers between devices, shards(): acts = lax.all_gather(act_half, 'hid', axis=0, tiled=True)  43.5 us
    all_to_all x4, waiting for transfers between devices, exchange(): return lax.all_to_all(blocks, axis, split_axis=0, concat_axis=0, tiled=True)  38.9 us
    all_to_all x1, waiting for transfers between devices, sum_blocks(): lax.all_to_all(jnp.concatenate([coded, power], axis=1), axis, split_axis=...  33.6 us
    ppermute x1, waiting for transfers between devices, shards(): lax.ppermute(own_tile[:, half:], pair, [(at(1, h), at(0, h ^ 1)) for h in...  17.9 us
    all_to_all x1, starting transfers between devices, sum_blocks(): lax.all_to_all(jnp.concatenate([coded, power], axis=1), axis, split_axis=...  14.6 us
    all_gather x1, waiting for transfers between devices, shards(): pres = lax.all_gather(pre_share, 'hid', axis=0, tiled=True)  13.9 us
    ppermute x1, waiting for transfers between devices, shards(): lax.ppermute(own_tile[:, half:], pair, [(at(1, h), at(0, h)) for h in ran...  12.6 us
  transfers between devices with their start and end apart: 19, of which 11 were waited for; matrix products, arithmetic and copies ran while one was open for 10% of the time, Pallas kernels for 0%

profile of v8, /device:TPU:1, one launch (start us, length us, event | category | flops | bytes accessed | tf_op | source)
XLA Modules:
  0.0 316.3 jit_solution(5558618408768053598)
XLA Ops:
  8.9 4.0 %collective-permute-start = (bf16[32,1152]{1,0:T(8,128)(2,1)S(1)}, bf16[32,1152]{1,0:T(8,128)(2,1)S(1)}, u32[]{:S(2)}, u32[]{:S(2)}) collective-permute-start(bf16[32,1152]{1,0:T(8,128)(2,1)S(1)} %get-tuple-element.10), channel_id=1, source_target_pairs={{0,256},{272,16},{32,288},{304,48},{64,320},{336,80},{96,352},{368... | collective-permute-start | bytes 221192 | tf_op jit(solution)/shard_map/ppermute | solution.py:108
  15.0 4.1 %collective-permute-done.1 = bf16[32,1152]{1,0:T(8,128)(2,1)S(1)} collective-permute-done((bf16[32,1152]{1,0:T(8,128)(2,1)S(1)}, bf16[32,1152]{1,0:T(8,128)(2,1)S(1)}, u32[]{:S(2)}, u32[]{:S(2)}) %collective-permute-start.1) | collective-permute-done | bytes 73760 | tf_op jit(solution)/shard_map/ppermute | solution.py:108
  20.0 8.4 %all-to-all-start = ((bf16[16,32,768]{2,1,0:T(8,128)(2,1)}), bf16[16,32,768]{2,1,0:T(8,128)(2,1)S(1)}, u32[]{:S(2)}, u32[]{:S(2)}) async-start(bf16[16,32,768]{2,1,0:T(8,128)(2,1)} %broadcast_in_dim.22), calls=%async_computation | async-start | bytes 1572864 | tf_op jit(solution)/shard_map/all_to_all | solution.py:41
  33.4 17.9 %collective-permute-done.4 = bf16[384,768]{1,0:T(8,128)(2,1)S(1)} collective-permute-done((bf16[384,768]{1,0:T(8,128)(2,1)S(1)}, bf16[384,768]{1,0:T(8,128)(2,1)S(1)}, u32[]{:S(2)}, u32[]{:S(2)}) %collective-permute-start.4) | collective-permute-done | bytes 589856 | tf_op jit(solution)/shard_map/ppermute | solution.py:118
  51.9 12.6 %collective-permute-done.3 = bf16[384,768]{1,0:T(8,128)(2,1)} collective-permute-done((bf16[384,768]{1,0:T(8,128)(2,1)S(1)}, bf16[384,768]{1,0:T(8,128)(2,1)}, u32[]{:S(2)}, u32[]{:S(2)}) %collective-permute-start.3) | collective-permute-done | bytes 589856 | tf_op jit(solution)/shard_map/ppermute | solution.py:117
  64.5 2.3 abs_reduce_fusion
  68.8 14.6 %all-to-all-start.1 = ((f16[8,72,768]{2,1,0:T(8,128)(2,1)}), f16[8,72,768]{2,1,0:T(8,128)(2,1)S(1)}, u32[]{:S(2)}, u32[]{:S(2)}) async-start(f16[8,72,768]{2,1,0:T(8,128)(2,1)} %concatenate.47), calls=%async_computation.1 | async-start | bytes 1769472 | tf_op jit(solution)/shard_map/all_to_all | solution.py:73
  84.3 33.6 %all-to-all-done.1 = f16[8,72,768]{2,1,0:T(8,128)(2,1)S(1)} async-done(((f16[8,72,768]{2,1,0:T(8,128)(2,1)}), f16[8,72,768]{2,1,0:T(8,128)(2,1)S(1)}, u32[]{:S(2)}, u32[]{:S(2)}) %all-to-all-start.1) | async-done | bytes 884768 | tf_op jit(solution)/shard_map/all_to_all | solution.py:73
  118.3 43.5 %all-gather.3.cloned.1.call-done = bf16[1024,768]{1,0:T(8,128)(2,1)} async-done(((bf16[64,768]{1,0:T(8,128)(2,1)}), bf16[1024,768]{1,0:T(8,128)(2,1)}) %all-gather.3.cloned.1.call-update) | async-done | bytes 1572880 | tf_op jit(solution)/shard_map/all_gather | solution.py:132
  162.6 2.3 collective-permute-start.7
  164.9 2.9 collective-permute-done.7
  169.1 15.3 %all-to-all-start.2 = ((bf16[16,64,768]{2,1,0:T(8,128)(2,1)}), bf16[16,64,768]{2,1,0:T(8,128)(2,1)S(1)}, u32[]{:S(2)}, u32[]{:S(2)}) async-start(bf16[16,64,768]{2,1,0:T(8,128)(2,1)} %broadcast_in_dim.23), calls=%async_computation.2 | async-start | bytes 3145728 | tf_op jit(solution)/shard_map/all_to_all | solution.py:41
  184.5 2.3 collective-permute-start.6
  188.5 18.7 %all-to-all-done.2 = bf16[16,64,768]{2,1,0:T(8,128)(2,1)S(1)} async-done(((bf16[16,64,768]{2,1,0:T(8,128)(2,1)}), bf16[16,64,768]{2,1,0:T(8,128)(2,1)S(1)}, u32[]{:S(2)}, u32[]{:S(2)}) %all-to-all-start.2) | async-done | bytes 1572896 | tf_op jit(solution)/shard_map/all_to_all | solution.py:41
  212.4 2.3 collective-permute-start.11
  214.7 13.9 %all-gather.5.cloned.1.call-done = bf16[1024,768]{1,0:T(8,128)(2,1)} async-done(((bf16[64,768]{1,0:T(8,128)(2,1)}), bf16[1024,768]{1,0:T(8,128)(2,1)}) %all-gather.5.cloned.1.call-update) | async-done | bytes 1572880 | tf_op jit(solution)/shard_map/all_gather | solution.py:146
  228.6 3.2 %multiply_reduce_fusion.5 = (f32[768]{0:T(1024)S(1)}, f32[]{:T(128)}, f32[384]{0:T(512)S(1)}, f32[384,768]{1,0:T(8,128)S(1)}) fusion(bf16[1024,768]{1,0:T(8,128)(2,1)} %all-gather.5.cloned.1.call-done, bf16[1024,768]{1,0:T(8,128)(2,1)} %bitcast.56), kind=kOutput, calls=%fused_computation.16 | convolution fusion | flops 605158272 | bytes 3543556 | tf_op jit(solution)/shard_map/dot_general | solution.py:35
  233.2 3.7 %collective-permute-start.8 = (f32[10,128]{1,0:T(8,128)}, f32[10,128]{1,0:T(8,128)}, u32[]{:S(2)}, u32[]{:S(2)}) collective-permute-start(f32[10,128]{1,0:T(8,128)} %maximum_bitcast_fusion), channel_id=1, source_target_pairs={{0,256},{256,0},{1,257},{257,1},{2,258},{258,2},{3,259},{259,3},{4... | collective-permute-start | bytes 15368 | tf_op jit(solution)/shard_map/ppermute | solution.py:149
  237.0 3.3 %convolution_convert_fusion = bf16[1024,384]{1,0:T(8,128)(2,1)} fusion(bf16[1024,768]{1,0:T(8,128)(2,1)} %all-gather.5.cloned.1.call-done, bf16[384,768]{1,0:T(8,128)(2,1)} %collective-permute-done.6, pred[]{:T(512)S(6)} %eq.44, bf16[384,1536]{1,0:T(8,128)(2,1)S(1)} %bitcast.54), kind=kOutput, calls=%fused_computation.6 | convolution fusion | flops 604667904 | bytes 3538945 | tf_op jit(solution)/shard_map/dot_general | solution.py:192
  245.6 6.6 %all-to-all-start.3 = ((f32[16,16,128]{2,1,0:T(8,128)}), f32[16,16,128]{2,1,0:T(8,128)S(1)}, u32[]{:S(2)}, u32[]{:S(2)}) async-start(f32[16,16,128]{2,1,0:T(8,128)} %broadcast_in_dim.28), calls=%async_computation.3 | async-start | bytes 262144 | tf_op jit(solution)/shard_map/all_to_all | solution.py:41
  255.1 9.0 %all-to-all-done.3 = f32[16,16,128]{2,1,0:T(8,128)S(1)} async-done(((f32[16,16,128]{2,1,0:T(8,128)}), f32[16,16,128]{2,1,0:T(8,128)S(1)}, u32[]{:S(2)}, u32[]{:S(2)}) %all-to-all-start.3) | async-done | bytes 131104 | tf_op jit(solution)/shard_map/all_to_all | solution.py:41
  266.7 19.1 %all-to-all-start.4 = ((bf16[16,80,384]{2,1,0:T(8,128)(2,1)}), bf16[16,80,384]{2,1,0:T(8,128)(2,1)}, u32[]{:S(2)}, u32[]{:S(2)}) async-start(bf16[16,80,384]{2,1,0:T(8,128)(2,1)} %pad_maximum_fusion), calls=%async_computation.4 | async-start | bytes 1966080 | tf_op jit(solution)/shard_map/all_to_all | solution.py:41
  288.5 2.4 select_bitcast_fusion.1
  290.9 11.2 %all-to-all-done.4 = bf16[16,80,384]{2,1,0:T(8,128)(2,1)} async-done(((bf16[16,80,384]{2,1,0:T(8,128)(2,1)}), bf16[16,80,384]{2,1,0:T(8,128)(2,1)}, u32[]{:S(2)}, u32[]{:S(2)}) %all-to-all-start.4) | async-done | bytes 983072 | tf_op jit(solution)/shard_map/all_to_all | solution.py:41
  (118 shorter events, 40.3 us)
Async XLA Ops:
  8.9 6.0 %collective-permute-start = (bf16[32,1152]{1,0:T(8,128)(2,1)S(1)}, bf16[32,1152]{1,0:T(8,128)(2,1)S(1)}, u32[]{:S(2)}, u32[]{:S(2)}) collective-permute-start(bf16[32,1152]{1,0:T(8,128)(2,1)S(1)} %get-tuple-element.10), channel_id=1, source_target_pairs={{0,256},{272,16},{32,288},{304,48},{64,320},{336,80},{96,352},{368... | collective-permute-start | bytes 221192 | tf_op jit(solution)/shard_map/ppermute | solution.py:108
  12.9 2.0 collective-permute-start.2
  13.6 5.5 %collective-permute-start.1 = (bf16[32,1152]{1,0:T(8,128)(2,1)S(1)}, bf16[32,1152]{1,0:T(8,128)(2,1)S(1)}, u32[]{:S(2)}, u32[]{:S(2)}) collective-permute-start(bf16[32,1152]{1,0:T(8,128)(2,1)S(1)} %get-tuple-element.9), channel_id=1, source_target_pairs={{16,0},{256,272},{48,32},{288,304},{80,64},{320,336},{112,96},{352... | collective-permute-start | bytes 221192 | tf_op jit(solution)/shard_map/ppermute | solution.py:108
  20.0 31.3 %all-to-all-start = ((bf16[16,32,768]{2,1,0:T(8,128)(2,1)}), bf16[16,32,768]{2,1,0:T(8,128)(2,1)S(1)}, u32[]{:S(2)}, u32[]{:S(2)}) async-start(bf16[16,32,768]{2,1,0:T(8,128)(2,1)} %broadcast_in_dim.22), calls=%async_computation | async-start | bytes 1572864 | tf_op jit(solution)/shard_map/all_to_all | solution.py:41
  29.3 21.9 %collective-permute-start.4 = (bf16[384,768]{1,0:T(8,128)(2,1)S(1)}, bf16[384,768]{1,0:T(8,128)(2,1)S(1)}, u32[]{:S(2)}, u32[]{:S(2)}) collective-permute-start(bf16[384,768]{1,0:T(8,128)(2,1)S(1)} %get-tuple-element.27), channel_id=1, source_target_pairs={{256,16},{272,0},{288,48},{304,32},{320,80},{336,64},{352,112},{36... | collective-permute-start | bytes 1769480 | tf_op jit(solution)/shard_map/ppermute | solution.py:118
  30.6 20.7 %collective-permute-start.5 = (bf16[384,768]{1,0:T(8,128)(2,1)}, bf16[384,768]{1,0:T(8,128)(2,1)}, u32[]{:S(2)}, u32[]{:S(2)}) collective-permute-start(bf16[384,768]{1,0:T(8,128)(2,1)} %get-tuple-element.26), channel_id=1, source_target_pairs={{256,272},{272,256},{288,304},{304,288},{320,336},{336,320},{352,3... | collective-permute-start | bytes 1769480 | tf_op jit(solution)/shard_map/ppermute | solution.py:114
  32.1 32.4 %collective-permute-start.3 = (bf16[384,768]{1,0:T(8,128)(2,1)S(1)}, bf16[384,768]{1,0:T(8,128)(2,1)}, u32[]{:S(2)}, u32[]{:S(2)}) collective-permute-start(bf16[384,768]{1,0:T(8,128)(2,1)S(1)} %get-tuple-element.27), channel_id=1, source_target_pairs={{256,0},{272,16},{288,32},{304,48},{320,64},{336,80},{352,96},{368... | collective-permute-start | bytes 1769480 | tf_op jit(solution)/shard_map/ppermute | solution.py:117
  68.8 93.7 %copy-start.13 = (bf16[32,384]{1,0:T(8,128)(2,1)S(1)}, bf16[32,384]{1,0:T(8,128)(2,1)}, u32[]{:S(2)}) copy-start(bf16[32,384]{1,0:T(8,128)(2,1)} %param.8) | copy-start | bytes 73732
  68.8 93.8 %copy-start.5 = (bf16[32,384]{1,0:T(8,128)(2,1)S(1)}, bf16[32,384]{1,0:T(8,128)(2,1)}, u32[]{:S(2)}) copy-start(bf16[32,384]{1,0:T(8,128)(2,1)} %param.9) | copy-start | bytes 73732
  68.8 49.1 %all-to-all-start.1 = ((f16[8,72,768]{2,1,0:T(8,128)(2,1)}), f16[8,72,768]{2,1,0:T(8,128)(2,1)S(1)}, u32[]{:S(2)}, u32[]{:S(2)}) async-start(f16[8,72,768]{2,1,0:T(8,128)(2,1)} %concatenate.47), calls=%async_computation.1 | async-start | bytes 1769472 | tf_op jit(solution)/shard_map/all_to_all | solution.py:73
  83.4 78.4 %all-gather.3.cloned.1.call-start = ((), (), s32[]{:S(2)}) async-start(), calls=%async_computation.5 | async-start | bytes 1671168 | tf_op jit(solution)/shard_map/all_gather | solution.py:132
  84.2 144.4 %all-gather.5.cloned.1.call-start = ((), (), s32[]{:S(2)}) async-start(), calls=%async_computation.6 | async-start | bytes 1671168 | tf_op jit(solution)/shard_map/all_gather | solution.py:146
  162.6 5.2 %collective-permute-start.7 = (bf16[32,768]{1,0:T(8,128)(2,1)S(1)}, bf16[32,768]{1,0:T(8,128)(2,1)S(1)}, u32[]{:S(2)}, u32[]{:S(2)}) collective-permute-start(bf16[32,768]{1,0:T(8,128)(2,1)S(1)} %constant_dynamic-update-slice_fusion), channel_id=1, source_target_pairs={{0,256},{256,0},{1,257},{257,1},{2,258},{258,2},{3,259},{259,3},{4... | collective-permute-start | bytes 147464 | tf_op jit(solution)/shard_map/ppermute | solution.py:149
  169.1 38.0 %all-to-all-start.2 = ((bf16[16,64,768]{2,1,0:T(8,128)(2,1)}), bf16[16,64,768]{2,1,0:T(8,128)(2,1)S(1)}, u32[]{:S(2)}, u32[]{:S(2)}) async-start(bf16[16,64,768]{2,1,0:T(8,128)(2,1)} %broadcast_in_dim.23), calls=%async_computation.2 | async-start | bytes 3145728 | tf_op jit(solution)/shard_map/all_to_all | solution.py:41
  184.5 52.5 %collective-permute-start.6 = (bf16[384,768]{1,0:T(8,128)(2,1)}, bf16[384,768]{1,0:T(8,128)(2,1)}, u32[]{:S(2)}, u32[]{:S(2)}) collective-permute-start(bf16[384,768]{1,0:T(8,128)(2,1)} %get-tuple-element.26), channel_id=1, source_target_pairs={{0,256},{1,257},{2,258},{3,259},{4,260},{5,261},{6,262},{7,263},{8... | collective-permute-start | bytes 1769480 | tf_op jit(solution)/shard_map/ppermute | solution.py:153
  212.4 76.1 %collective-permute-start.11 = (f16[384,768]{1,0:T(8,128)(2,1)}, f16[384,768]{1,0:T(8,128)(2,1)}, u32[]{:S(2)}, u32[]{:S(2)}) collective-permute-start(f16[384,768]{1,0:T(8,128)(2,1)} %multiply_convert_fusion.1), channel_id=1, source_target_pairs={{0,256},{1,257},{2,258},{3,259},{4,260},{5,261},{6,262},{7,263},{8... | collective-permute-start | bytes 1769480 | tf_op jit(solution)/shard_map/ppermute | solution.py:169
  233.2 8.4 %collective-permute-start.8 = (f32[10,128]{1,0:T(8,128)}, f32[10,128]{1,0:T(8,128)}, u32[]{:S(2)}, u32[]{:S(2)}) collective-permute-start(f32[10,128]{1,0:T(8,128)} %maximum_bitcast_fusion), channel_id=1, source_target_pairs={{0,256},{256,0},{1,257},{257,1},{2,258},{258,2},{3,259},{259,3},{4... | collective-permute-start | bytes 15368 | tf_op jit(solution)/shard_map/ppermute | solution.py:149
  241.5 23.3 %copy-start.17 = (s32[16]{0:T(128)S(1)}, s32[16]{0:T(128)}, u32[]{:S(2)}) copy-start(s32[16]{0:T(128)} %get-tuple-element.46) | copy-start | bytes 196
  241.5 23.3 %copy-start.18 = (s32[16]{0:T(128)S(1)}, s32[16]{0:T(128)}, u32[]{:S(2)}) copy-start(s32[16]{0:T(128)} %get-tuple-element.47) | copy-start | bytes 196
  241.5 23.2 %copy-start.19 = (pred[16]{0:T(512)(128)(4,1)S(1)}, pred[16]{0:T(512)(128)(4,1)}, u32[]{:S(2)}) copy-start(pred[16]{0:T(512)(128)(4,1)} %get-tuple-element.44) | copy-start | bytes 52
  245.6 18.5 %all-to-all-start.3 = ((f32[16,16,128]{2,1,0:T(8,128)}), f32[16,16,128]{2,1,0:T(8,128)S(1)}, u32[]{:S(2)}, u32[]{:S(2)}) async-start(f32[16,16,128]{2,1,0:T(8,128)} %broadcast_in_dim.28), calls=%async_computation.3 | async-start | bytes 262144 | tf_op jit(solution)/shard_map/all_to_all | solution.py:41
  253.1 35.4 %collective-permute-start.10 = (f16[384,768]{1,0:T(8,128)(2,1)}, f16[384,768]{1,0:T(8,128)(2,1)}, u32[]{:S(2)}, u32[]{:S(2)}) collective-permute-start(f16[384,768]{1,0:T(8,128)(2,1)} %multiply_convert_fusion.2), channel_id=1, source_target_pairs={{256,0},{257,1},{258,2},{259,3},{260,4},{261,5},{262,6},{263,7},{2... | collective-permute-start | bytes 1769480 | tf_op jit(solution)/shard_map/ppermute | solution.py:175
  266.7 35.3 %all-to-all-start.4 = ((bf16[16,80,384]{2,1,0:T(8,128)(2,1)}), bf16[16,80,384]{2,1,0:T(8,128)(2,1)}, u32[]{:S(2)}, u32[]{:S(2)}) async-start(bf16[16,80,384]{2,1,0:T(8,128)(2,1)} %pad_maximum_fusion), calls=%async_computation.4 | async-start | bytes 1966080 | tf_op jit(solution)/shard_map/all_to_all | solution.py:41
  304.0 4.8 %collective-permute-start.9 = (f32[32,384]{1,0:T(8,128)S(1)}, f32[32,384]{1,0:T(8,128)S(1)}, u32[]{:S(2)}, u32[]{:S(2)}) collective-permute-start(f32[32,384]{1,0:T(8,128)S(1)} %slice_select_fusion.2), channel_id=1, source_target_pairs={{0,256},{256,0},{1,257},{257,1},{2,258},{258,2},{3,259},{259,3},{4... | collective-permute-start | bytes 147464 | tf_op jit(solution)/shard_map/ppermute | solution.py:149
  (17 other events, 212.9 us)
Sparse Core Ops, SparseCore 0:
  86.3 75.4 all-gather.2
  163.8 64.7 all-gather.4

commit v9 on v4

--- a/solution.py
+++ b/solution.py
@@ -2,6 +2,7 @@
 import jax.numpy as jnp
 from jax import lax
 from jax.sharding import PartitionSpec as P
+
 
 D = 6144
 FF = 24576
@@ -93,21 +94,26 @@
     rings = [list(range(p, hid, 2)) for p in range(2)]
 
     def token_blocks(same, other):
-        own = jnp.where(home, same, lax.ppermute(other, pair, over))
-        near = lax.ppermute(same, pair, beside)
+        same, other = lax.optimization_barrier((same, other))
         far = lax.ppermute(other, pair, across)
-        return own, jnp.where(home, near, far)
-
-    grad_pair = jnp.concatenate(token_blocks(grad_out, grad_out), axis=1)
-    tile_near = lax.ppermute(own_tile[:, :half], pair, [(at(1, h), at(1, h ^ 1)) for h in range(hid)])
+        return same, lax.ppermute(other, pair, over), lax.ppermute(same, pair, beside), far
+
+    def pick(blocks, columns):
+        same, there, near, far = (block[:, columns] for block in blocks)
+        return jnp.where(home, same, there), jnp.where(home, near, far)
+
+    tile_near = lax.ppermute(
+        own_tile[:, :half], pair, [(at(1, h), at(1, h ^ 1)) for h in range(hid)]
+    )
     tile_over = lax.ppermute(own_tile[:, half:], pair, [(at(1, h), at(0, h)) for h in range(hid)])
-    tile_far = lax.ppermute(own_tile[:, half:], pair, [(at(1, h), at(0, h ^ 1)) for h in range(hid)])
-    grad_half = spread(grad_pair, "wid")
-    pre_own, pre_next = token_blocks(
-        jnp.where(first, preact[:, half:], preact[:, :half]),
-        jnp.where(first, preact[:, :half], preact[:, half:]),
-    )
-    grad_half, pre_own, pre_next = lax.optimization_barrier((grad_half, pre_own, pre_next))
+    tile_far = lax.ppermute(
+        own_tile[:, half:], pair, [(at(1, h), at(0, h ^ 1)) for h in range(hid)]
+    )
+    blocks = token_blocks(
+        jnp.concatenate([grad_out, jnp.where(first, preact[:, half:], preact[:, :half])], axis=1),
+        jnp.concatenate([grad_out, jnp.where(first, preact[:, :half], preact[:, half:])], axis=1),
+    )
+    grad_half = spread(jnp.concatenate(pick(blocks, slice(features)), axis=1), "wid")
     hidden_part = jnp.dot(
         grad_half[:, :features],
         jnp.where(first, tile_over, own_tile[:, :half]),
@@ -118,6 +124,7 @@
         preferred_element_type=jnp.float32,
     )
     hidden_share = sum_blocks(hidden_part, "hid", rings)
+    pre_own, pre_next = pick(blocks, slice(features, None))
     pre_half = jnp.concatenate(
         [jnp.where(even, pre_own, pre_next), jnp.where(even, pre_next, pre_own)]
     )
@@ -187,6 +194,7 @@
         P("section", "hid"),
         P("section", "wid"),
     )
+
     return jax.shard_map(
         shards,
         mesh=mesh,

time: 274 us -> 274 us (level)
  waiting for transfers between devices: 139 us -> 150 us
  starting transfers between devices: 87.3 us -> 80.5 us
    ppermute x1, waiting for transfers between devices: 0.01 us -> 18.5 us  [shards(): lax.ppermute(own_tile[:, half:], pair, [(at(1, h), at(0, h ^ 1)) for h in...]
    all_gather x1, waiting for transfers between devices: 53 us -> 35.8 us  [shards(): lax.all_gather(jnp.where(first, pre_share, act_share), 'hid', axis=0, til...]
    ppermute x4 -> x2, starting transfers between devices: 13.7 us -> 5.31 us  [the longest x1 4.02 us: token_blocks(): lax.ppermute(other, pair, over)]
    ppermute x1, waiting for transfers between devices: 5.95 us -> 12.6 us  [shards(): lax.ppermute(own_tile[:, half:], pair, [(at(1, h), at(0, h)) for h in ran...]
    ppermute x4 -> x2, waiting for transfers between devices: 10.4 us -> 4.1 us  [the longest x1 4.1 us: token_blocks(): lax.ppermute(same, pair, beside)]
    all_to_all x1, waiting for transfers between devices: 29.3 us -> 35.4 us  [sum_blocks(): lax.all_to_all(jnp.concatenate([coded, power], axis=1), axis, split_axis=...]
    all_to_all x4, starting transfers between devices: 43.1 us -> 47.6 us  [exchange(): return lax.all_to_all(blocks, axis, split_axis=0, concat_axis=0, tiled=True)]
    ppermute x1, starting transfers between devices: 6.41 us -> 1.92 us  [shards(): taken = lax.ppermute(given, 'section', [(0, 1), (1, 0)])]
  transfers between devices with their start and end apart: 19 -> 16, of which waited for: 9 -> 10; matrix products, arithmetic and copies ran while one was open for 5% -> 3% of each run, Pallas kernels for 0% -> 0%
where the time goes in v9:
time: 274 us; the launch traced here: 273 us
  waiting for transfers between devices  150 us (55%)
  starting transfers between devices  80.5 us (29%)
  between operations  16.5 us (6%)
  matrix products  11.9 us (4%)
  other arithmetic  8.82 us (3%)
  local copies, waits for them, and re-layouts  5.99 us (2%)
    all_to_all x4, starting transfers between devices, exchange(): return lax.all_to_all(blocks, axis, split_axis=0, concat_axis=0, tiled=True)  47.6 us
    all_to_all x4, waiting for transfers between devices, exchange(): return lax.all_to_all(blocks, axis, split_axis=0, concat_axis=0, tiled=True)  36.5 us
    all_gather x1, waiting for transfers between devices, shards(): lax.all_gather(jnp.where(first, pre_share, act_share), 'hid', axis=0, til...  35.8 us
    all_to_all x1, waiting for transfers between devices, sum_blocks(): lax.all_to_all(jnp.concatenate([coded, power], axis=1), axis, split_axis=...  35.4 us
    ppermute x1, waiting for transfers between devices, shards(): lax.ppermute(own_tile[:, half:], pair, [(at(1, h), at(0, h ^ 1)) for h in...  18.5 us
    all_to_all x1, starting transfers between devices, sum_blocks(): lax.all_to_all(jnp.concatenate([coded, power], axis=1), axis, split_axis=...  14.7 us
    ppermute x1, waiting for transfers between devices, shards(): lax.ppermute(own_tile[:, half:], pair, [(at(1, h), at(0, h)) for h in ran...  12.6 us
  transfers between devices with their start and end apart: 16, of which 10 were waited for; matrix products, arithmetic and copies ran while one was open for 3% of the time, Pallas kernels for 0%

profile of v9, /device:TPU:1, one launch (start us, length us, event | category | flops | bytes accessed | tf_op | source)
XLA Modules:
  0.0 273.5 jit_solution(7979857386908178813)
XLA Ops:
  8.9 4.0 %collective-permute-start = (bf16[32,1152]{1,0:T(8,128)(2,1)S(1)}, bf16[32,1152]{1,0:T(8,128)(2,1)S(1)}, u32[]{:S(2)}, u32[]{:S(2)}) collective-permute-start(bf16[32,1152]{1,0:T(8,128)(2,1)S(1)} %get-tuple-element.5), channel_id=1, source_target_pairs={{0,256},{272,16},{32,288},{304,48},{64,320},{336,80},{96,352},{368... | collective-permute-start | bytes 221192 | tf_op jit(solution)/shard_map/ppermute | solution.py:99
  14.9 4.1 %collective-permute-done.1 = bf16[32,1152]{1,0:T(8,128)(2,1)S(1)} collective-permute-done((bf16[32,1152]{1,0:T(8,128)(2,1)S(1)}, bf16[32,1152]{1,0:T(8,128)(2,1)S(1)}, u32[]{:S(2)}, u32[]{:S(2)}) %collective-permute-start.1) | collective-permute-done | bytes 73760 | tf_op jit(solution)/shard_map/ppermute | solution.py:99
  20.0 8.4 %all-to-all-start = ((bf16[16,32,768]{2,1,0:T(8,128)(2,1)}), bf16[16,32,768]{2,1,0:T(8,128)(2,1)S(1)}, u32[]{:S(2)}, u32[]{:S(2)}) async-start(bf16[16,32,768]{2,1,0:T(8,128)(2,1)} %broadcast_in_dim.22), calls=%async_computation | async-start | bytes 1572864 | tf_op jit(solution)/shard_map/all_to_all | solution.py:36
  29.9 1.5 collective-permute-start.5
  32.6 18.5 %collective-permute-done.4 = bf16[384,768]{1,0:T(8,128)(2,1)S(1)} collective-permute-done((bf16[384,768]{1,0:T(8,128)(2,1)S(1)}, bf16[384,768]{1,0:T(8,128)(2,1)S(1)}, u32[]{:S(2)}, u32[]{:S(2)}) %collective-permute-start.4) | collective-permute-done | bytes 589856 | tf_op jit(solution)/shard_map/ppermute | solution.py:109
  51.7 12.6 %collective-permute-done.3 = bf16[384,768]{1,0:T(8,128)(2,1)} collective-permute-done((bf16[384,768]{1,0:T(8,128)(2,1)S(1)}, bf16[384,768]{1,0:T(8,128)(2,1)}, u32[]{:S(2)}, u32[]{:S(2)}) %collective-permute-start.3) | collective-permute-done | bytes 589856 | tf_op jit(solution)/shard_map/ppermute | solution.py:108
  64.4 2.3 abs_reduce_fusion
  68.6 14.7 %all-to-all-start.1 = ((f16[8,72,768]{2,1,0:T(8,128)(2,1)}), f16[8,72,768]{2,1,0:T(8,128)(2,1)S(1)}, u32[]{:S(2)}, u32[]{:S(2)}) async-start(f16[8,72,768]{2,1,0:T(8,128)(2,1)} %concatenate.33), calls=%async_computation.1 | async-start | bytes 1769472 | tf_op jit(solution)/shard_map/all_to_all | solution.py:64
  83.5 2.4 collective-permute-start.7
  85.8 35.4 %all-to-all-done.1 = f16[8,72,768]{2,1,0:T(8,128)(2,1)S(1)} async-done(((f16[8,72,768]{2,1,0:T(8,128)(2,1)}), f16[8,72,768]{2,1,0:T(8,128)(2,1)S(1)}, u32[]{:S(2)}, u32[]{:S(2)}) %all-to-all-start.1) | async-done | bytes 884768 | tf_op jit(solution)/shard_map/all_to_all | solution.py:64
  123.1 4.1 %collective-permute-done.6 = bf16[64,768]{1,0:T(8,128)(2,1)S(1)} collective-permute-done((bf16[64,768]{1,0:T(8,128)(2,1)S(1)}, bf16[64,768]{1,0:T(8,128)(2,1)S(1)}, u32[]{:S(2)}, u32[]{:S(2)}) %collective-permute-start.6) | collective-permute-done | bytes 98336 | tf_op jit(solution)/shard_map/ppermute | solution.py:137
  128.0 1.9 collective-permute-start.8
  129.9 2.6 collective-permute-done.8
  133.6 14.0 %all-to-all-start.2 = ((bf16[16,64,384]{2,1,0:T(8,128)(2,1)}), bf16[16,64,384]{2,1,0:T(8,128)(2,1)S(1)}, u32[]{:S(2)}, u32[]{:S(2)}) async-start(bf16[16,64,384]{2,1,0:T(8,128)(2,1)} %broadcast_in_dim.23), calls=%async_computation.2 | async-start | bytes 1572864 | tf_op jit(solution)/shard_map/all_to_all | solution.py:36
  148.2 12.9 %all-to-all-done.2 = bf16[16,64,384]{2,1,0:T(8,128)(2,1)S(1)} async-done(((bf16[16,64,384]{2,1,0:T(8,128)(2,1)}), bf16[16,64,384]{2,1,0:T(8,128)(2,1)S(1)}, u32[]{:S(2)}, u32[]{:S(2)}) %all-to-all-start.2) | async-done | bytes 786464 | tf_op jit(solution)/shard_map/all_to_all | solution.py:36
  161.3 35.8 %all-gather.2.cloned.1.call-done = bf16[1024,1536]{1,0:T(8,128)(2,1)} async-done(((bf16[64,1536]{1,0:T(8,128)(2,1)}), bf16[1024,1536]{1,0:T(8,128)(2,1)}) %all-gather.2.cloned.1.call-update) | async-done | bytes 3145744 | tf_op jit(solution)/shard_map/all_gather | solution.py:139
  197.1 5.4 %multiply_reduce_fusion.2 = (f32[384]{0:T(512)S(1)}, f32[1536]{0:T(1024)S(1)}, f32[]{:T(128)}, f32[384,1536]{1,0:T(8,128)}) fusion(bf16[1024,384]{1,0:T(8,128)(2,1)S(1)} %bitcast.38, bf16[1024,1536]{1,0:T(8,128)(2,1)} %all-gather.2.cloned.1.call-done), kind=kOutput, calls=%fused_computation.3 | convolution fusion | flops 1210316928 | bytes 6299140 | tf_op jit(solution)/shard_map/dot_general | solution.py:30
  204.5 6.9 %all-to-all-start.3 = ((f32[16,16,128]{2,1,0:T(8,128)}), f32[16,16,128]{2,1,0:T(8,128)S(1)}, u32[]{:S(2)}, u32[]{:S(2)}) async-start(f32[16,16,128]{2,1,0:T(8,128)} %broadcast_in_dim.27), calls=%async_computation.3 | async-start | bytes 262144 | tf_op jit(solution)/shard_map/all_to_all | solution.py:36
  211.4 3.7 %convolution_convert_fusion = bf16[1024,384]{1,0:T(8,128)(2,1)S(1)} fusion(bf16[1024,1536]{1,0:T(8,128)(2,1)} %all-gather.2.cloned.1.call-done, bf16[1,384,1536]{2,1,0:T(8,128)(2,1)S(1)} %copy-done), kind=kOutput, calls=%fused_computation.9 | convolution fusion | flops 1208352768 | bytes 5111808 | tf_op jit(solution)/shard_map/dot_general | solution.py:164
  215.2 8.1 %all-to-all-done.3 = f32[16,16,128]{2,1,0:T(8,128)S(1)} async-done(((f32[16,16,128]{2,1,0:T(8,128)}), f32[16,16,128]{2,1,0:T(8,128)S(1)}, u32[]{:S(2)}, u32[]{:S(2)}) %all-to-all-start.3) | async-done | bytes 131104 | tf_op jit(solution)/shard_map/all_to_all | solution.py:36
  225.7 18.4 %all-to-all-start.4 = ((bf16[16,80,384]{2,1,0:T(8,128)(2,1)}), bf16[16,80,384]{2,1,0:T(8,128)(2,1)S(1)}, u32[]{:S(2)}, u32[]{:S(2)}) async-start(bf16[16,80,384]{2,1,0:T(8,128)(2,1)} %pad_maximum_fusion), calls=%async_computation.4 | async-start | bytes 1966080 | tf_op jit(solution)/shard_map/all_to_all | solution.py:36
  244.8 15.4 %all-to-all-done.4 = bf16[16,80,384]{2,1,0:T(8,128)(2,1)S(1)} async-done(((bf16[16,80,384]{2,1,0:T(8,128)(2,1)}), bf16[16,80,384]{2,1,0:T(8,128)(2,1)S(1)}, u32[]{:S(2)}, u32[]{:S(2)}) %all-to-all-start.4) | async-done | bytes 983072 | tf_op jit(solution)/shard_map/all_to_all | solution.py:36
  261.0 2.5 collective-permute-start.9
  264.2 1.8 multiply_bitcast_fusion
  (85 shorter events, 19.5 us)
Async XLA Ops:
  7.2 21.3 %copy-start = (bf16[1,384,1536]{2,1,0:T(8,128)(2,1)S(1)}, bf16[1,384,1536]{2,1,0:T(8,128)(2,1)}, u32[]{:S(2)}) copy-start(bf16[1,384,1536]{2,1,0:T(8,128)(2,1)} %param.6) | copy-start | bytes 3538948
  8.9 19.6 %copy-start.4 = (bf16[32,1152]{1,0:T(8,128)(2,1)}, bf16[32,1152]{1,0:T(8,128)(2,1)S(1)}, u32[]{:S(2)}) copy-start(bf16[32,1152]{1,0:T(8,128)(2,1)S(1)} %get-tuple-element.4) | copy-start | bytes 221188
  8.9 6.0 %collective-permute-start = (bf16[32,1152]{1,0:T(8,128)(2,1)S(1)}, bf16[32,1152]{1,0:T(8,128)(2,1)S(1)}, u32[]{:S(2)}, u32[]{:S(2)}) collective-permute-start(bf16[32,1152]{1,0:T(8,128)(2,1)S(1)} %get-tuple-element.5), channel_id=1, source_target_pairs={{0,256},{272,16},{32,288},{304,48},{64,320},{336,80},{96,352},{368... | collective-permute-start | bytes 221192 | tf_op jit(solution)/shard_map/ppermute | solution.py:99
  12.9 6.1 %collective-permute-start.2 = (bf16[32,1152]{1,0:T(8,128)(2,1)S(1)}, bf16[32,1152]{1,0:T(8,128)(2,1)S(1)}, u32[]{:S(2)}, u32[]{:S(2)}) collective-permute-start(bf16[32,1152]{1,0:T(8,128)(2,1)S(1)} %get-tuple-element.5), channel_id=1, source_target_pairs={{16,256},{256,16},{48,288},{288,48},{80,320},{320,80},{112,352},{3... | collective-permute-start | bytes 221192 | tf_op jit(solution)/shard_map/ppermute | solution.py:98
  13.6 5.5 %collective-permute-start.1 = (bf16[32,1152]{1,0:T(8,128)(2,1)S(1)}, bf16[32,1152]{1,0:T(8,128)(2,1)S(1)}, u32[]{:S(2)}, u32[]{:S(2)}) collective-permute-start(bf16[32,1152]{1,0:T(8,128)(2,1)S(1)} %get-tuple-element.4), channel_id=1, source_target_pairs={{16,0},{256,272},{48,32},{288,304},{80,64},{320,336},{112,96},{352... | collective-permute-start | bytes 221192 | tf_op jit(solution)/shard_map/ppermute | solution.py:99
  20.0 31.1 %all-to-all-start = ((bf16[16,32,768]{2,1,0:T(8,128)(2,1)}), bf16[16,32,768]{2,1,0:T(8,128)(2,1)S(1)}, u32[]{:S(2)}, u32[]{:S(2)}) async-start(bf16[16,32,768]{2,1,0:T(8,128)(2,1)} %broadcast_in_dim.22), calls=%async_computation | async-start | bytes 1572864 | tf_op jit(solution)/shard_map/all_to_all | solution.py:36
  28.6 22.6 %collective-permute-start.4 = (bf16[384,768]{1,0:T(8,128)(2,1)S(1)}, bf16[384,768]{1,0:T(8,128)(2,1)S(1)}, u32[]{:S(2)}, u32[]{:S(2)}) collective-permute-start(bf16[384,768]{1,0:T(8,128)(2,1)S(1)} %get-tuple-element.12), channel_id=1, source_target_pairs={{256,16},{272,0},{288,48},{304,32},{320,80},{336,64},{352,112},{36... | collective-permute-start | bytes 1769480 | tf_op jit(solution)/shard_map/ppermute | solution.py:109
  29.9 21.3 %collective-permute-start.5 = (bf16[384,768]{1,0:T(8,128)(2,1)S(1)}, bf16[384,768]{1,0:T(8,128)(2,1)}, u32[]{:S(2)}, u32[]{:S(2)}) collective-permute-start(bf16[384,768]{1,0:T(8,128)(2,1)S(1)} %get-tuple-element.11), channel_id=1, source_target_pairs={{256,272},{272,256},{288,304},{304,288},{320,336},{336,320},{352,3... | collective-permute-start | bytes 1769480 | tf_op jit(solution)/shard_map/ppermute | solution.py:105
  31.4 33.0 %collective-permute-start.3 = (bf16[384,768]{1,0:T(8,128)(2,1)S(1)}, bf16[384,768]{1,0:T(8,128)(2,1)}, u32[]{:S(2)}, u32[]{:S(2)}) collective-permute-start(bf16[384,768]{1,0:T(8,128)(2,1)S(1)} %get-tuple-element.12), channel_id=1, source_target_pairs={{256,0},{272,16},{288,32},{304,48},{320,64},{336,80},{352,96},{368... | collective-permute-start | bytes 1769480 | tf_op jit(solution)/shard_map/ppermute | solution.py:108
  67.5 15.9 %copy-start.5 = (bf16[32,1152]{1,0:T(8,128)(2,1)S(1)}, bf16[32,1152]{1,0:T(8,128)(2,1)}, u32[]{:S(2)}) copy-start(bf16[32,1152]{1,0:T(8,128)(2,1)} %copy-done.4) | copy-start | bytes 221188
  68.6 59.3 %copy-start.2 = (bf16[32,384]{1,0:T(8,128)(2,1)S(1)}, bf16[32,384]{1,0:T(8,128)(2,1)}, u32[]{:S(2)}) copy-start(bf16[32,384]{1,0:T(8,128)(2,1)} %param.9) | copy-start | bytes 73732
  68.6 59.3 %copy-start.6 = (bf16[32,384]{1,0:T(8,128)(2,1)S(1)}, bf16[32,384]{1,0:T(8,128)(2,1)}, u32[]{:S(2)}) copy-start(bf16[32,384]{1,0:T(8,128)(2,1)} %param.8) | copy-start | bytes 73732
  68.6 52.6 %all-to-all-start.1 = ((f16[8,72,768]{2,1,0:T(8,128)(2,1)}), f16[8,72,768]{2,1,0:T(8,128)(2,1)S(1)}, u32[]{:S(2)}, u32[]{:S(2)}) async-start(f16[8,72,768]{2,1,0:T(8,128)(2,1)} %concatenate.33), calls=%async_computation.1 | async-start | bytes 1769472 | tf_op jit(solution)/shard_map/all_to_all | solution.py:64
  83.3 113.8 %all-gather.2.cloned.1.call-start = ((), (), s32[]{:S(2)}) async-start(), calls=%async_computation.5 | async-start | bytes 3342336 | tf_op jit(solution)/shard_map/all_gather | solution.py:139
  83.5 39.6 %collective-permute-start.7 = (bf16[64,768]{1,0:T(8,128)(2,1)S(1)}, bf16[64,768]{1,0:T(8,128)(2,1)S(1)}, u32[]{:S(2)}, u32[]{:S(2)}) collective-permute-start(bf16[64,768]{1,0:T(8,128)(2,1)S(1)} %pad_maximum_fusion.1), channel_id=1, source_target_pairs={{0,256},{1,257},{2,258},{3,259},{4,260},{5,261},{6,262},{7,263},{8... | collective-permute-start | bytes 294920 | tf_op jit(solution)/shard_map/ppermute | solution.py:131
  121.6 26.0 %copy-start.14 = (f32[1,384]{1,0:T(1,128)S(1)}, f32[1,384]{1,0:T(1,128)}, u32[]{:S(2)}) copy-start(f32[1,384]{1,0:T(1,128)} %param.10) | copy-start | bytes 4612
  121.8 5.4 %collective-permute-start.6 = (bf16[64,768]{1,0:T(8,128)(2,1)S(1)}, bf16[64,768]{1,0:T(8,128)(2,1)S(1)}, u32[]{:S(2)}, u32[]{:S(2)}) collective-permute-start(bf16[64,768]{1,0:T(8,128)(2,1)S(1)} %fusion.19), channel_id=1, source_target_pairs={{256,0},{257,1},{258,2},{259,3},{260,4},{261,5},{262,6},{263,7},{2... | collective-permute-start | bytes 294920 | tf_op jit(solution)/shard_map/ppermute | solution.py:137
  128.0 4.6 %collective-permute-start.8 = (bf16[32,384]{1,0:T(8,128)(2,1)S(1)}, bf16[32,384]{1,0:T(8,128)(2,1)S(1)}, u32[]{:S(2)}, u32[]{:S(2)}) collective-permute-start(bf16[32,384]{1,0:T(8,128)(2,1)S(1)} %broadcast_select_fusion.6), channel_id=1, source_target_pairs={{0,256},{256,0},{1,257},{257,1},{2,258},{258,2},{3,259},{259,3},{4... | collective-permute-start | bytes 73736 | tf_op jit(solution)/shard_map/ppermute | solution.py:143
  133.6 27.6 %all-to-all-start.2 = ((bf16[16,64,384]{2,1,0:T(8,128)(2,1)}), bf16[16,64,384]{2,1,0:T(8,128)(2,1)S(1)}, u32[]{:S(2)}, u32[]{:S(2)}) async-start(bf16[16,64,384]{2,1,0:T(8,128)(2,1)} %broadcast_in_dim.23), calls=%async_computation.2 | async-start | bytes 1572864 | tf_op jit(solution)/shard_map/all_to_all | solution.py:36
  204.5 18.8 %all-to-all-start.3 = ((f32[16,16,128]{2,1,0:T(8,128)}), f32[16,16,128]{2,1,0:T(8,128)S(1)}, u32[]{:S(2)}, u32[]{:S(2)}) async-start(f32[16,16,128]{2,1,0:T(8,128)} %broadcast_in_dim.27), calls=%async_computation.3 | async-start | bytes 262144 | tf_op jit(solution)/shard_map/all_to_all | solution.py:36
  224.7 20.1 %copy-start.13 = (f32[1,1536]{1,0:T(1,128)S(1)}, f32[1,1536]{1,0:T(1,128)}, u32[]{:S(2)}) copy-start(f32[1,1536]{1,0:T(1,128)} %param.11) | copy-start | bytes 18436
  225.7 38.5 %copy-start.1 = (f32[384,1536]{1,0:T(8,128)S(1)}, f32[384,1536]{1,0:T(8,128)}, u32[]{:S(2)}) copy-start(f32[384,1536]{1,0:T(8,128)} %get-tuple-element.25) | copy-start | bytes 7077892
  225.7 34.5 %all-to-all-start.4 = ((bf16[16,80,384]{2,1,0:T(8,128)(2,1)}), bf16[16,80,384]{2,1,0:T(8,128)(2,1)S(1)}, u32[]{:S(2)}, u32[]{:S(2)}) async-start(bf16[16,80,384]{2,1,0:T(8,128)(2,1)} %pad_maximum_fusion), calls=%async_computation.4 | async-start | bytes 1966080 | tf_op jit(solution)/shard_map/all_to_all | solution.py:36
  261.0 5.0 %collective-permute-start.9 = (f32[32,384]{1,0:T(8,128)S(1)}, f32[32,384]{1,0:T(8,128)S(1)}, u32[]{:S(2)}, u32[]{:S(2)}) collective-permute-start(f32[32,384]{1,0:T(8,128)S(1)} %slice.111), channel_id=1, source_target_pairs={{0,256},{1,257},{2,258},{3,259},{4,260},{5,261},{6,262},{7,263},{8... | collective-permute-start | bytes 147464 | tf_op jit(solution)/shard_map/ppermute | solution.py:175
  (7 other events, 72.4 us)
Sparse Core Ops, SparseCore 0:
  128.1 68.9 all-gather.1
